TPU v7x, 512 devices: a whole 4x4x16 slice. The times are simulated.
512 devices in a mesh: tm: 16 (over z_lo, y), series: 32 (over z_hi, x, core).
Axes of the slice: x: 4, y: 4, z: 16 (z_hi: 4, z_lo: 4; z = z_hi * 4 + z_lo), core: 2. Of those that a mesh axis runs over, the one named last changes fastest.
Arguments:
- inputs: bfloat16 [64, 8192, 512], P('series', 'tm'), may hold values from -6 to 6
- cotangent: bfloat16 [64, 8192, 512], P('series', 'tm'), may hold values from -6 to 6
- taps: int32 [3], replicated, may hold values from 0 to 128, as said below
- weight: float32 [1536, 512], P('series'), may hold values from -0.15625 to 0.15625
- moment_one: float32 [1536, 512], P('series'), may hold values from -10 to 10
- second_moment_state: float32 [1536, 512], P('series'), may hold values from 1 to 100
Outputs:
- grad_input: bfloat16 [64, 8192, 512], P('series', 'tm')
- new_weight: float32 [1536, 512], P('series')
- new_moment_one: float32 [1536, 512], P('series')
- new_moment_two: float32 [1536, 512], P('series')
Inputs may be any that keep to these rules, and one draw needn't show every extreme that they name: taps[0] is 0, taps[2] is 128, and taps[1] lies strictly between them.
All inputs are finite; a program needn't handle non-finite values.
Results may differ from a plain program's by a relative error of at most 0.0045.
Values may be sent and summed in bfloat16 or wider, within the bound.
No kernel may reach another device: no remote copies, remote signals or barrier semaphores. Data moves between devices by JAX's collectives and lax.ppermute only.
A program may use at most 64 MiB of HBM per device.

v0:
```python
import jax
import jax.numpy as jnp
from jax import lax
from jax.sharding import PartitionSpec as P

DILATION_GAP = 64


def passed_along(array, axis, by):
    size = lax.axis_size(axis)
    pairs = [(i, i + by) for i in range(size) if 0 <= i + by < size]
    return lax.ppermute(array, axis, pairs)


def adamw(weight, grad, moment_one, second_moment_state):
    first = 0.9 * moment_one + 0.1 * grad
    second = 0.999 * second_moment_state + 0.001 * grad * grad
    unbiased_one = first / (1.0 - 0.9**10)
    unbiased_two = second / (1.0 - 0.999**10)
    updated = weight - 0.01 * (unbiased_one / (jnp.sqrt(unbiased_two) + 1e-08) + 0.1 * weight)
    return (updated, first, second)


def body(inputs, cotangent, taps, weight, moment_one, second_moment_state):
    series_n, time_n, width = inputs.shape
    tap_count = taps.shape[0]
    receptive_span = (tap_count - 1) * DILATION_GAP
    rows = series_n * time_n
    wide = lax.all_gather(weight.astype(jnp.bfloat16), "series", axis=0, tiled=True)
    earlier = passed_along(inputs[:, time_n - receptive_span :, :], "tm", 1)
    extended = jnp.concatenate([earlier, inputs], 1)
    shifted = [
        lax.dynamic_slice_in_dim(extended, receptive_span - taps[k], time_n, 1)
        for k in range(tap_count)
    ]
    stacked = jnp.concatenate(shifted, 2).reshape(rows, tap_count * width)
    pre = jnp.dot(stacked, wide, preferred_element_type=jnp.float32)
    sig = jax.nn.sigmoid(pre)
    upstream = cotangent.reshape(rows, width)
    dpre_flat = (upstream.astype(jnp.float32) * (sig * (1.0 + pre * (1.0 - sig)))).astype(
        jnp.bfloat16
    )
    dpre = dpre_flat.reshape(series_n, time_n, width)
    ahead = passed_along(dpre[:, :receptive_span, :], "tm", -1)
    later = jnp.concatenate([dpre, ahead], 1)
    result = upstream.astype(jnp.float32)
    for k in range(tap_count):
        moved = lax.dynamic_slice_in_dim(later, taps[k], time_n, 1).reshape(rows, width)
        result = result + lax.dot_general(
            moved,
            wide[k * width : (k + 1) * width],
            (((1,), (1,)), ((), ())),
            preferred_element_type=jnp.float32,
        )
    grad_input = result.astype(jnp.bfloat16).reshape(series_n, time_n, width)
    grad_shard = lax.psum_scatter(
        lax.dot_general(
            stacked, dpre_flat, (((0,), (0,)), ((), ())), preferred_element_type=jnp.float32
        ),
        "series",
        scatter_dimension=0,
        tiled=True,
    )
    grad_shard = lax.psum(grad_shard, "tm")
    new_weight, new_moment_one, new_moment_two = adamw(
        weight, grad_shard, moment_one, second_moment_state
    )
    return (grad_input, new_weight, new_moment_one, new_moment_two)


def solution(mesh):
    in_specs = (
        P("series", "tm", None),
        P("series", "tm", None),
        P(),
        P("series", None),
        P("series", None),
        P("series", None),
    )
    out_specs = (P("series", "tm", None), P("series", None), P("series", None), P("series", None))
    return jax.shard_map(body, mesh=mesh, in_specs=in_specs, out_specs=out_specs, check_vma=False)
```

profile of v0, /device:TPU:6, one launch (start us, length us, event | category | flops | bytes accessed | tf_op | source)
XLA Modules:
  0.0 394.0 jit_solution(17457735593663713182)
XLA Ops:
  7.2 0.0 all-gather.2.cloned.1.call-start
  7.2 1.5 convert_element_type.18
  8.7 0.0 all-gather.2.cloned.1.call-update
  8.8 0.0 reduce-scatter.2.cloned.1.call-start
  8.8 1.0 slice.27
  9.8 3.5 collective-permute-start
  13.3 1.4 fusion.14
  18.4 0.5 collective-permute-done
  18.8 1.3 constant_dynamic-update-slice_fusion
  20.1 0.8 constant_dynamic-slice_fusion.2
  21.0 0.3 pad_maximum_fusion
  21.2 68.9 %all-gather.2.cloned.1.call-done = bf16[1536,512]{1,0:T(8,128)(2,1)} async-done(((bf16[48,512]{1,0:T(8,128)(2,1)}), bf16[1536,512]{1,0:T(8,128)(2,1)}) %all-gather.2.cloned.1.call-update) | async-done | bytes 1572880 | tf_op jit(solution)/shard_map/all_gather | solution.py:29
  90.1 4.0 %fusion = bf16[1024,512]{1,0:T(8,128)(2,1)S(1)} fusion(bf16[2,512,512]{2,1,0:T(8,128)(2,1)} %param.7, bf16[1024,1536]{1,0:T(8,128)(2,1)S(1)} %bitcast.22, bf16[1536,512]{1,0:T(8,128)(2,1)} %all-gather.2.cloned.1.call-done), kind=kOutput, calls=%fused_computation.3 | convolution fusion | flops 1615855616 | bytes 6815744 | tf_op jit(solution)/shard_map/dot_general | solution.py:37
  94.2 0.0 copy-start
  94.2 1.0 copy-done
  95.1 3.5 fusion.15
  98.6 0.0 copy-start.1
  98.6 0.0 reduce-scatter.2.cloned.1.call-update
  98.6 0.0 all-reduce.2.cloned.1.call-start
  98.7 1.1 copy-done.1
  99.8 1.3 collective-permute-start.1
  106.7 0.0 copy-start.2
  106.7 5.1 %collective-permute-done.1 = bf16[2,128,512]{2,1,0:T(8,128)(2,1)S(1)} collective-permute-done((bf16[2,128,512]{2,1,0:T(8,128)(2,1)S(1)}, bf16[2,128,512]{2,1,0:T(8,128)(2,1)S(1)}, u32[]{:S(2)}, u32[]{:S(2)}) %collective-permute-start.1) | collective-permute-done | bytes 262176 | tf_op jit(solution)/shard_map/ppermute | solution.py:12
  111.9 3.0 fusion.4
  114.9 0.0 copy-done.2
  114.9 0.7 fusion.10
  115.7 2.1 fusion.8
  117.8 106.9 %reduce-scatter.2.cloned.1.call-done = f32[48,512]{1,0:T(8,128)} async-done(((f32[1536,512]{1,0:T(8,128)}), f32[48,512]{1,0:T(8,128)}) %reduce-scatter.2.cloned.1.call-update) | async-done | bytes 98320 | tf_op jit(solution)/shard_map/reduce_scatter | solution.py:56
  224.7 0.0 all-reduce.2.cloned.1.call-update
  224.7 0.0 copy-start.3
  224.7 0.0 copy-start.4
  224.7 0.0 copy-start.5
  224.7 3.8 fusion.3
  228.5 157.3 %all-reduce.2.cloned.1.call-done = f32[48,512]{1,0:T(8,128)} async-done(((f32[48,512]{1,0:T(8,128)}), f32[48,512]{1,0:T(8,128)}) %all-reduce.2.cloned.1.call-update) | async-done | bytes 98320 | tf_op jit(solution)/shard_map/psum | solution.py:64
  385.8 0.0 copy-done.3
  385.8 0.0 copy-done.4
  385.8 0.0 copy-done.5
  385.8 1.6 multiply_subtract_fusion
  (2 shorter events, 0.0 us)
Async XLA Ops:
  7.2 82.9 %all-gather.2.cloned.1.call-start = ((), (), s32[]{:S(2)}) async-start(), calls=%async_computation.1 | async-start | bytes 1622016 | tf_op jit(solution)/shard_map/all_gather | solution.py:29
  8.8 215.9 %reduce-scatter.2.cloned.1.call-start = ((), (), s32[]{:S(2)}) async-start(), calls=%async_computation.2 | async-start | bytes 3244032 | tf_op jit(solution)/shard_map/reduce_scatter | solution.py:56
  9.8 9.0 %collective-permute-start = (bf16[2,128,512]{2,1,0:T(8,128)(2,1)S(1)}, bf16[2,128,512]{2,1,0:T(8,128)(2,1)S(1)}, u32[]{:S(2)}, u32[]{:S(2)}) collective-permute-start(bf16[2,128,512]{2,1,0:T(8,128)(2,1)S(1)} %slice.27), channel_id=1, source_target_pairs={{0,32},{32,64},{64,96},{96,128},{128,160},{160,192},{192,224},{224... | collective-permute-start | bytes 786440 | tf_op jit(solution)/shard_map/ppermute | solution.py:12
  94.2 1.0 copy-start
  98.6 1.2 copy-start.1
  98.6 287.2 %all-reduce.2.cloned.1.call-start = ((), (), s32[]{:S(2)}) async-start(), calls=%async_computation.3 | async-start | bytes 196608 | tf_op jit(solution)/shard_map/psum | solution.py:64
  99.8 12.0 %collective-permute-start.1 = (bf16[2,128,512]{2,1,0:T(8,128)(2,1)S(1)}, bf16[2,128,512]{2,1,0:T(8,128)(2,1)S(1)}, u32[]{:S(2)}, u32[]{:S(2)}) collective-permute-start(bf16[2,128,512]{2,1,0:T(8,128)(2,1)S(1)} %slice.35), channel_id=1, source_target_pairs={{32,0},{64,32},{96,64},{128,96},{160,128},{192,160},{224,192},{256... | collective-permute-start | bytes 786440 | tf_op jit(solution)/shard_map/ppermute | solution.py:12
  106.7 8.2 %copy-start.2 = (bf16[1536,512]{1,0:T(8,128)(2,1)S(1)}, bf16[1536,512]{1,0:T(8,128)(2,1)}, u32[]{:S(2)}) copy-start(bf16[1536,512]{1,0:T(8,128)(2,1)} %all-gather.2.cloned.1.call-done) | copy-start | bytes 4718596
  224.7 161.2 %copy-start.3 = (f32[48,512]{1,0:T(8,128)S(1)}, f32[48,512]{1,0:T(8,128)}, u32[]{:S(2)}) copy-start(f32[48,512]{1,0:T(8,128)} %param.9) | copy-start | bytes 294916
  224.7 161.1 %copy-start.4 = (f32[48,512]{1,0:T(8,128)S(1)}, f32[48,512]{1,0:T(8,128)}, u32[]{:S(2)}) copy-start(f32[48,512]{1,0:T(8,128)} %param.10) | copy-start | bytes 294916
  224.7 161.1 %copy-start.5 = (f32[48,512]{1,0:T(8,128)S(1)}, f32[48,512]{1,0:T(8,128)}, u32[]{:S(2)}) copy-start(f32[48,512]{1,0:T(8,128)} %param.11) | copy-start | bytes 294916
Sparse Core Ops, SparseCore 0:
  11.7 78.3 all-gather.1
  98.8 125.8 reduce-scatter.1
  227.8 157.9 all-reduce.1
where the time goes:
time: 395 us; the launch traced here: 394 us
  waiting for transfers between devices  339 us (86%)
  between operations  23.1 us (6%)
  matrix products  14.2 us (4%)
  local copies, waits for them, and re-layouts  6.6 us (2%)
  other arithmetic  6.45 us (2%)
  starting transfers between devices  4.91 us (1%)
    psum x1, waiting for transfers between devices, body(): grad_shard = lax.psum(grad_shard, 'tm')  157 us
    reduce_scatter x1, waiting for transfers between devices, body(): lax.psum_scatter(lax.dot_general(stacked, dpre_flat, (((0,), (0,)), ((),...  107 us
    all_gather x1, waiting for transfers between devices, body(): lax.all_gather(weight.astype(jnp.bfloat16), 'series', axis=0, tiled=True)  68.9 us
  transfers between devices with their start and end apart: 5, of which 5 were waited for; matrix products, arithmetic and copies ran while one was open for 4% of the time, Pallas kernels for 0%

commit v1 on v0

v1 whole, which is shorter than its diff:
```python
import jax
import jax.numpy as jnp
from jax import lax
from jax.sharding import Mesh
from jax.sharding import PartitionSpec as P

DILATION_GAP = 64
TM = ("z_lo", "y")
SERIES = ("z_hi", "x", "core")
PLANE = ("x", "y")
LINE = ("z_hi", "z_lo")
LANES = 128


def passed_along(array, by):
    size = lax.axis_size(TM)
    pairs = [(i, i + by) for i in range(size) if 0 <= i + by < size]
    return lax.ppermute(array, TM, pairs)


def gathered(piece, axes):
    size = lax.axis_size(axes)
    return lax.all_to_all(jnp.broadcast_to(piece[None], (size,) + piece.shape), axes, 0, 0)


def swapped(array):
    return lax.ppermute(array, "core", [(0, 1), (1, 0)])


def gather_weight(shard):
    rows, width = shard.shape
    z_hi, z_lo = lax.axis_size("z_hi"), lax.axis_size("z_lo")
    x, y = lax.axis_size("x"), lax.axis_size("y")
    part, lanes = rows // z_lo, width // y
    piece = lax.dynamic_slice(
        shard, (lax.axis_index("z_lo") * part, lax.axis_index("y") * lanes), (part, lanes)
    )
    line = gathered(piece, LINE).reshape(z_hi * rows, lanes)
    mine = gathered(line, PLANE)
    other = swapped(mine)
    first = lax.axis_index("core") == 0
    both = jnp.stack([jnp.where(first, mine, other), jnp.where(first, other, mine)])
    both = both.reshape(2, x, y, z_hi, rows, lanes).transpose(3, 1, 0, 4, 2, 5)
    return both.reshape(z_hi * x * 2 * rows, width)


def reduce_grad(grad):
    z_hi, z_lo = lax.axis_size("z_hi"), lax.axis_size("z_lo")
    x, y = lax.axis_size("x"), lax.axis_size("y")
    total, width = grad.shape
    rows, lanes = total // (z_hi * x * 2), width // y
    halves = grad.reshape(z_hi, x, 2, rows, width)
    core = lax.axis_index("core")
    keep = lax.dynamic_index_in_dim(halves, core, 2, keepdims=False)
    give = lax.dynamic_index_in_dim(halves, 1 - core, 2, keepdims=False)
    chip = keep + swapped(give)
    chunks = chip.reshape(z_hi, x, rows, y, lanes).transpose(1, 3, 0, 2, 4)
    chunks = chunks.reshape(x * y, z_hi * rows, lanes).astype(jnp.bfloat16)
    plane = jnp.sum(lax.all_to_all(chunks, PLANE, 0, 0).astype(jnp.float32), 0)
    line = plane.reshape(z_hi * z_lo, rows // z_lo, lanes)
    piece = jnp.sum(lax.all_to_all(line, LINE, 0, 0), 0)
    pieces = gathered(piece, TM).reshape(z_lo, y, rows // z_lo, lanes)
    return pieces.transpose(0, 2, 1, 3).reshape(rows, width)


def adamw(weight, grad, moment_one, second_moment_state):
    first = 0.9 * moment_one + 0.1 * grad
    second = 0.999 * second_moment_state + 0.001 * grad * grad
    unbiased_one = first / (1.0 - 0.9**10)
    unbiased_two = second / (1.0 - 0.999**10)
    updated = weight - 0.01 * (unbiased_one / (jnp.sqrt(unbiased_two) + 1e-08) + 0.1 * weight)
    return (updated, first, second)


def body(inputs, cotangent, taps, weight, moment_one, second_moment_state):
    series_n, time_n, width = inputs.shape
    tap_count = taps.shape[0]
    receptive_span = (tap_count - 1) * DILATION_GAP
    rows = series_n * time_n
    wide = gather_weight(weight.astype(jnp.bfloat16))
    earlier = passed_along(inputs[:, time_n - receptive_span :, :], 1)
    extended = jnp.concatenate([earlier, inputs], 1)
    shifted = [
        lax.dynamic_slice_in_dim(extended, receptive_span - taps[k], time_n, 1)
        for k in range(tap_count)
    ]
    stacked = jnp.concatenate(shifted, 2).reshape(rows, tap_count * width)
    pre = jnp.dot(stacked, wide, preferred_element_type=jnp.float32)
    sig = jax.nn.sigmoid(pre)
    upstream = cotangent.reshape(rows, width)
    dpre_flat = (upstream.astype(jnp.float32) * (sig * (1.0 + pre * (1.0 - sig)))).astype(
        jnp.bfloat16
    )
    dpre = dpre_flat.reshape(series_n, time_n, width)
    grad = lax.dot_general(
        stacked, dpre_flat, (((0,), (0,)), ((), ())), preferred_element_type=jnp.float32
    )
    grad_shard = reduce_grad(grad)
    ahead = passed_along(dpre[:, :receptive_span, :], -1)
    later = jnp.concatenate([dpre, ahead], 1)
    result = upstream.astype(jnp.float32)
    for k in range(tap_count):
        moved = lax.dynamic_slice_in_dim(later, taps[k], time_n, 1).reshape(rows, width)
        result = result + lax.dot_general(
            moved,
            wide[k * width : (k + 1) * width],
            (((1,), (1,)), ((), ())),
            preferred_element_type=jnp.float32,
        )
    grad_input = result.astype(jnp.bfloat16).reshape(series_n, time_n, width)
    new_weight, new_moment_one, new_moment_two = adamw(
        weight, grad_shard, moment_one, second_moment_state
    )
    return (grad_input, new_weight, new_moment_one, new_moment_two)


def solution(mesh):
    torus = Mesh(mesh.devices.reshape(4, 4, 4, 4, 2), TM + SERIES)
    tokens = P(SERIES, TM, None)
    rows = P(SERIES, None)
    return jax.shard_map(
        body,
        mesh=torus,
        in_specs=(tokens, tokens, P(), rows, rows, rows),
        out_specs=(tokens, rows, rows, rows),
        check_vma=False,
    )
```

time: 395 us -> 146 us (0.37)
  waiting for transfers between devices: 339 us -> 32.3 us
  starting transfers between devices: 4.91 us -> 35.7 us
  blocking collectives: 0 us -> 27.7 us
  between operations: 23.1 us -> 10.7 us
  local copies, waits for them, and re-layouts: 6.6 us -> 15.4 us
    psum x1 -> x0, waiting for transfers between devices: 157 us -> none  [body(): grad_shard = lax.psum(grad_shard, 'tm')]
    reduce_scatter x1 -> x0, waiting for transfers between devices: 107 us -> none  [body(): lax.psum_scatter(lax.dot_general(stacked, dpre_flat, (((0,), (0,)), ((),...]
    all_gather x1 -> x0, waiting for transfers between devices: 68.9 us -> none  [body(): lax.all_gather(weight.astype(jnp.bfloat16), 'series', axis=0, tiled=True)]
    all_to_all x0 -> x1, blocking collectives: none -> 27.7 us  [gathered(): lax.all_to_all(jnp.broadcast_to(piece[None], (size,) + piece.shape), axes...]
    all_to_all x0 -> x4, starting transfers between devices: none -> 26.7 us  [the longest x2 13.4 us: gathered(): lax.all_to_all(jnp.broadcast_to(piece[None], (size,) + piece.shape), axes...]
    all_to_all x0 -> x4, waiting for transfers between devices: none -> 21.6 us  [the longest x2 12.7 us: gathered(): lax.all_to_all(jnp.broadcast_to(piece[None], (size,) + piece.shape), axes...]
    ppermute x2 -> x4, waiting for transfers between devices: 5.61 us -> 10.7 us  [the longest x2 7.5 us: passed_along(): return lax.ppermute(array, TM, pairs)]
    ppermute x2 -> x4, starting transfers between devices: 4.79 us -> 8.97 us  [the longest x2 4.66 us: passed_along(): return lax.ppermute(array, TM, pairs)]
  transfers between devices with their start and end apart: 5 -> 8, of which waited for: 5 -> 5; matrix products, arithmetic and copies ran while one was open for 4% -> 14% of each run, Pallas kernels for 0% -> 0%
where the time goes in v1:
time: 146 us; the launch traced here: 145 us
  starting transfers between devices  35.7 us (24%)
  waiting for transfers between devices  32.3 us (22%)
  blocking collectives  27.7 us (19%)
  local copies, waits for them, and re-layouts  15.4 us (11%)
  matrix products  13.5 us (9%)
  between operations  10.7 us (7%)
  other arithmetic  10.1 us (7%)
    all_to_all x1, blocking collectives, gathered(): lax.all_to_all(jnp.broadcast_to(piece[None], (size,) + piece.shape), axes...  27.7 us
    all_to_all x2, starting transfers between devices, gathered(): lax.all_to_all(jnp.broadcast_to(piece[None], (size,) + piece.shape), axes...  13.4 us
    all_to_all x2, waiting for transfers between devices, gathered(): lax.all_to_all(jnp.broadcast_to(piece[None], (size,) + piece.shape), axes...  12.7 us
    dot_general x3, matrix products, body(): lax.dot_general(moved, wide[k * width:(k + 1) * width], (((1,), (1,)), ((...  9.3 us
    all_to_all x1, waiting for transfers between devices, reduce_grad(): piece = jnp.sum(lax.all_to_all(line, LINE, 0, 0), 0)  8.89 us
    all_to_all x1, starting transfers between devices, reduce_grad(): piece = jnp.sum(lax.all_to_all(line, LINE, 0, 0), 0)  7.65 us
    ppermute x2, waiting for transfers between devices, passed_along(): return lax.ppermute(array, TM, pairs)  7.5 us
    all_to_all x1, starting transfers between devices, reduce_grad(): plane = jnp.sum(lax.all_to_all(chunks, PLANE, 0, 0).astype(jnp.float32), 0)  5.7 us
  transfers between devices with their start and end apart: 8, of which 5 were waited for; matrix products, arithmetic and copies ran while one was open for 14% of the time, Pallas kernels for 0%

profile of v1, /device:TPU:6, one launch (start us, length us, event | category | flops | bytes accessed | tf_op | source)
XLA Modules:
  0.0 145.3 jit_solution(1880252851923373987)
XLA Ops:
  0.6 0.0 copy-start.4
  0.6 0.0 copy-start.10
  0.7 0.9 dynamic_slice.68
  1.5 27.7 %all_to_all.25 = bf16[16,12,128]{2,1,0:T(8,128)(2,1)S(1)} all-to-all(bf16[16,12,128]{2,1,0:T(8,128)(2,1)S(1)} %broadcast_in_dim.8), channel_id=1, replica_groups=mesh['z_lo'=4,'y'=4,'z_hi'=4,'x'=4,'core'=2] {'z_hi','z_lo'}, dimensions={0} | all-to-all | bytes 98304 | tf_op jit(solution)/shard_map/all_to_all | solution.py:23
  29.3 1.0 broadcast_in_dim.10
  30.3 7.4 %all-to-all-start.1 = ((bf16[16,192,128]{2,1,0:T(8,128)(2,1)}), bf16[16,192,128]{2,1,0:T(8,128)(2,1)}, u32[]{:S(2)}, u32[]{:S(2)}) async-start(bf16[16,192,128]{2,1,0:T(8,128)(2,1)} %broadcast_in_dim.10), calls=%async_computation.1 | async-start | bytes 1572864 | tf_op jit(solution)/shard_map/all_to_all | solution.py:23
  37.7 0.0 copy-done.4
  37.8 3.4 %collective-permute-start = (bf16[2,128,512]{2,1,0:T(8,128)(2,1)S(1)}, bf16[2,128,512]{2,1,0:T(8,128)(2,1)S(1)}, u32[]{:S(2)}, u32[]{:S(2)}) collective-permute-start(bf16[2,128,512]{2,1,0:T(8,128)(2,1)S(1)} %slice.27), channel_id=1, source_target_pairs={{0,32},{32,64},{64,96},{96,128},{128,160},{160,192},{192,224},{224... | collective-permute-start | bytes 786440 | tf_op jit(solution)/shard_map/ppermute | solution.py:18
  41.2 7.5 %all-to-all-done.1 = bf16[16,192,128]{2,1,0:T(8,128)(2,1)} async-done(((bf16[16,192,128]{2,1,0:T(8,128)(2,1)}), bf16[16,192,128]{2,1,0:T(8,128)(2,1)}, u32[]{:S(2)}, u32[]{:S(2)}) %all-to-all-start.1) | async-done | bytes 786464 | tf_op jit(solution)/shard_map/all_to_all | solution.py:23
  48.7 1.9 %collective-permute-start.1 = (bf16[16,192,128]{2,1,0:T(8,128)(2,1)}, bf16[16,192,128]{2,1,0:T(8,128)(2,1)}, u32[]{:S(2)}, u32[]{:S(2)}) collective-permute-start(bf16[16,192,128]{2,1,0:T(8,128)(2,1)} %all-to-all-done.1), channel_id=1, source_target_pairs={{0,1},{1,0},{2,3},{3,2},{4,5},{5,4},{6,7},{7,6},{8,9},{9,8},{10,11... | collective-permute-start | bytes 2359304 | tf_op jit(solution)/shard_map/ppermute | solution.py:27
  50.6 0.0 copy-done.10
  50.6 0.6 fusion.20
  55.1 0.0 collective-permute-done
  55.2 0.1 constant_dynamic-update-slice_fusion
  55.2 0.8 constant_dynamic-slice_fusion.2
  56.0 0.3 pad_maximum_fusion
  56.3 2.9 %copy.17 = bf16[1024,1536]{0,1:T(8,128)(2,1)} copy(bf16[1024,1536]{1,0:T(8,128)(2,1)S(1)} %bitcast.59) | data formatting | bytes 6291456 | tf_op jit(solution)/shard_map/reshape | solution.py:87
  59.2 0.0 collective-permute-done.1
  59.2 1.5 %broadcast_select_fusion.1 = (bf16[16,192,128]{2,1,0:T(8,128)(2,1)S(1)}, bf16[16,192,128]{2,1,0:T(8,128)(2,1)S(1)}) fusion(bf16[16,192,128]{2,1,0:T(8,128)(2,1)} %all-to-all-done.1, bf16[16,192,128]{2,1,0:T(8,128)(2,1)} %collective-permute-done.1, pred[]{:T(512)S(6)} %eq.3), kind=kLoop, calls=%fused_computation.25 | loop fusion | flops 786432 | bytes 3145729 | tf_op jit(solution)/shard_map/jit(_where)/select_n | solution.py:42
  60.7 0.1 maximum_bitcast_fusion
  60.8 0.0 copy-start.7
  60.9 1.2 copy.16
  62.1 0.0 copy-start
  62.1 0.0 copy-done.7
  62.1 0.0 copy-start.2
  62.1 2.4 %fusion = bf16[1024,512]{1,0:T(8,128)(2,1)S(1)} fusion(bf16[2,512,512]{2,1,0:T(8,128)(2,1)S(1)} %copy-done.7, bf16[1024,1536]{1,0:T(8,128)(2,1)S(1)} %bitcast.60, bf16[192,8,4,128]{3,2,1,0:T(4,128)(2,1)S(1)} %bitcast.61), kind=kOutput, calls=%fused_computation.3 | convolution fusion | flops 1615855616 | bytes 6815744 | tf_op jit(solution)/shard_map/dot_general | solution.py:88
  64.5 0.0 copy-done
  64.5 0.0 copy-start.5
  64.5 0.0 copy-done.2
  64.6 1.8 %fusion.8 = f32[4,4,2,48,512]{4,3,2,1,0:T(8,128)S(1)} fusion(bf16[4,4,2,48,1024]{4,3,2,1,0:T(8,128)(2,1)S(1)} %bitcast.69, bf16[1024,512]{1,0:T(8,128)(2,1)S(1)} %fusion), kind=kOutput, calls=%fused_computation.22 | convolution fusion | flops 1610612736 | bytes 7340032 | tf_op jit(solution)/shard_map/dot_general | solution.py:95
  66.4 0.0 copy-done.5
  66.4 0.0 copy-start.3
  66.4 1.6 %copy-done.3 = f32[4,4,2,48,512]{4,3,2,1,0:T(8,128)} copy-done((f32[4,4,2,48,512]{4,3,2,1,0:T(8,128)}, f32[4,4,2,48,512]{4,3,2,1,0:T(8,128)S(1)}, u32[]{:S(2)}) %copy-start.3) | copy-done | bytes 3145752
  68.1 1.4 dynamic-slice_bitcast_fusion
  69.4 2.4 %collective-permute-start.3 = (f32[4,4,48,512]{3,2,1,0:T(8,128)}, f32[4,4,48,512]{3,2,1,0:T(8,128)S(1)}, u32[]{:S(2)}, u32[]{:S(2)}) collective-permute-start(f32[4,4,48,512]{3,2,1,0:T(8,128)} %dynamic-slice_bitcast_fusion), channel_id=1, source_target_pairs={{0,1},{1,0},{2,3},{3,2},{4,5},{5,4},{6,7},{7,6},{8,9},{9,8},{10,11... | collective-permute-start | bytes 4718600 | tf_op jit(solution)/shard_map/ppermute | solution.py:27
  71.8 3.2 %collective-permute-done.3 = f32[4,4,48,512]{3,2,1,0:T(8,128)S(1)} collective-permute-done((f32[4,4,48,512]{3,2,1,0:T(8,128)}, f32[4,4,48,512]{3,2,1,0:T(8,128)S(1)}, u32[]{:S(2)}, u32[]{:S(2)}) %collective-permute-start.3) | collective-permute-done | bytes 1572896 | tf_op jit(solution)/shard_map/ppermute | solution.py:27
  75.0 1.7 %fusion.4 = bf16[4,4,48,512]{3,2,1,0:T(8,128)(2,1)S(1)} fusion(f32[4,4,48,512]{3,2,1,0:T(8,128)S(1)} %collective-permute-done.3, f32[4,4,2,48,512]{4,3,2,1,0:T(8,128)} %copy-done.3, s32[]{:T(128)S(6)} %select_n.54), kind=kLoop, calls=%fused_computation.13 | loop fusion | flops 786432 | bytes 3932164 | tf_op jit(solution)/shard_map/convert_element_type | solution.py:58
  76.7 0.0 copy-start.6
  76.7 0.2 convert_element_type.37
  76.9 0.0 copy-start.1
  76.9 1.0 copy.18
  78.0 5.7 %all-to-all-start.2 = ((bf16[16,192,128]{2,1,0:T(8,128)(2,1)}), bf16[16,192,128]{2,1,0:T(8,128)(2,1)S(1)}, u32[]{:S(2)}, u32[]{:S(2)}) async-start(bf16[16,192,128]{2,1,0:T(8,128)(2,1)} %bitcast.21), calls=%async_computation.2 | async-start | bytes 1572864 | tf_op jit(solution)/shard_map/all_to_all | solution.py:59
  83.7 0.0 copy-done.6
  83.7 0.7 slice.35
  84.4 1.3 collective-permute-start.2
  91.5 0.0 copy-done.1
  91.5 1.4 copy.32
  92.9 7.5 %collective-permute-done.2 = bf16[2,128,512]{2,1,0:T(8,128)(2,1)} collective-permute-done((bf16[2,128,512]{2,1,0:T(8,128)(2,1)}, bf16[2,128,512]{2,1,0:T(8,128)(2,1)}, u32[]{:S(2)}, u32[]{:S(2)}) %collective-permute-start.2) | collective-permute-done | bytes 262176 | tf_op jit(solution)/shard_map/ppermute | solution.py:18
  100.4 4.7 %fusion.5 = (bf16[2,512,512]{2,1,0:T(8,128)(2,1)S(1)}, bf16[2,512,512]{2,1,0:T(8,128)(2,1)}, bf16[2,512,512]{2,1,0:T(8,128)(2,1)}) fusion(s32[]{:T(128)S(6)} %select_n.53, bf16[2,512,512]{2,1,0:T(8,128)(2,1)S(1)} %bitcast.74, bf16[2,128,512]{2,1,0:T(8,128)(2,1)} %collective-permute-done.2, s32[]{:T(128)S(6)} %select_n.51, s32[]{:T(128)S(6)} %select_n.52), kind=kLoop, calls=%fused_computation.19 | loop fusion | flops 6291456 | bytes 4456460 | tf_op jit(solution)/shard_map/concatenate | solution.py:100
  105.2 0.0 all-to-all-done.2
  105.2 0.1 convert_reduce_fusion
  105.3 0.7 reshape.62
  105.9 7.7 %all-to-all-start.3 = ((f32[16,12,128]{2,1,0:T(8,128)}), f32[16,12,128]{2,1,0:T(8,128)S(1)}, u32[]{:S(2)}, u32[]{:S(2)}) async-start(f32[16,12,128]{2,1,0:T(8,128)} %reshape.62), calls=%async_computation.3 | async-start | bytes 262144 | tf_op jit(solution)/shard_map/all_to_all | solution.py:61
  113.6 2.1 %fusion.13 = f32[1024,512]{1,0:T(8,128)S(1)} fusion(bf16[1024,512]{1,0:T(8,128)(2,1)} %bitcast.68, bf16[1536,512]{1,0:T(8,128)(2,1)} %bitcast.63), kind=kOutput, calls=%fused_computation.29 | convolution fusion | flops 536870912 | bytes 3670016 | tf_op jit(solution)/shard_map/dot_general | solution.py:104
  115.7 3.4 %fusion.11 = f32[1024,512]{1,0:T(8,128)} fusion(bf16[1024,512]{1,0:T(8,128)(2,1)} %bitcast.67, bf16[1536,512]{1,0:T(8,128)(2,1)} %bitcast.64), kind=kOutput, calls=%fused_computation.27 | convolution fusion | flops 536870912 | bytes 3670016 | tf_op jit(solution)/shard_map/dot_general | solution.py:104
  119.1 8.9 %all-to-all-done.3 = f32[16,12,128]{2,1,0:T(8,128)S(1)} async-done(((f32[16,12,128]{2,1,0:T(8,128)}), f32[16,12,128]{2,1,0:T(8,128)S(1)}, u32[]{:S(2)}, u32[]{:S(2)}) %all-to-all-start.3) | async-done | bytes 98336 | tf_op jit(solution)/shard_map/all_to_all | solution.py:61
  128.0 0.7 broadcast_in_dim.22
  128.7 6.0 %all-to-all-start.4 = ((f32[16,12,128]{2,1,0:T(8,128)}), f32[16,12,128]{2,1,0:T(8,128)S(1)}, u32[]{:S(2)}, u32[]{:S(2)}) async-start(f32[16,12,128]{2,1,0:T(8,128)} %broadcast_in_dim.22), calls=%async_computation.4 | async-start | bytes 262144 | tf_op jit(solution)/shard_map/all_to_all | solution.py:23
  134.7 0.0 copy-start.8
  134.7 0.0 copy-start.9
  134.7 3.8 %fusion.3 = bf16[1024,512]{1,0:T(8,128)(2,1)} fusion(f32[1024,512]{1,0:T(8,128)} %fusion.11, f32[1024,512]{1,0:T(8,128)S(1)} %fusion.13, bf16[1024,512]{1,0:T(8,128)(2,1)} %bitcast.75, bf16[1024,512]{1,0:T(8,128)(2,1)S(1)} %bitcast.66, bf16[1536,512]{1,0:T(8,128)(2,1)} %bitcast.65), kind=kOutput, calls=%fused_computation.6 | convolution fusion | flops 539492352 | bytes 7864320 | tf_op jit(solution)/shard_map/dot_general | solution.py:104
  138.5 5.1 %all-to-all-done.4 = f32[16,12,128]{2,1,0:T(8,128)S(1)} async-done(((f32[16,12,128]{2,1,0:T(8,128)}), f32[16,12,128]{2,1,0:T(8,128)S(1)}, u32[]{:S(2)}, u32[]{:S(2)}) %all-to-all-start.4) | async-done | bytes 98336 | tf_op jit(solution)/shard_map/all_to_all | solution.py:23
  143.7 0.0 copy-done.8
  143.7 1.6 %multiply_subtract_fusion = (f32[48,512]{1,0:T(8,128)}, f32[48,512]{1,0:T(8,128)}, f32[48,512]{1,0:T(8,128)}) fusion(f32[48,512]{1,0:T(8,128)S(1)} %copy-done.8, f32[6,8,4,128]{3,2,1,0:T(4,128)S(1)} %bitcast.78, f32[48,512]{1,0:T(8,128)S(1)} %copy-done.9, f32[48,512]{1,0:T(8,128)} %param.11), kind=kLoop, calls=%fused_computation.35 | loop fusion | flops 368640 | bytes 688128 | tf_op jit(solution)/shard_map/sub | solution.py:71
  (8 shorter events, 0.1 us)
Async XLA Ops:
  0.6 37.1 %copy-start.4 = (bf16[2,512,512]{2,1,0:T(8,128)(2,1)S(1)}, bf16[2,512,512]{2,1,0:T(8,128)(2,1)}, u32[]{:S(2)}) copy-start(bf16[2,512,512]{2,1,0:T(8,128)(2,1)} %param.6) | copy-start | bytes 3145732
  0.6 50.0 %copy-start.10 = (s32[3]{0:T(128)S(1)}, s32[3]{0:T(128)}, u32[]{:S(2)}) copy-start(s32[3]{0:T(128)} %param.8) | copy-start | bytes 40
  30.3 18.4 %all-to-all-start.1 = ((bf16[16,192,128]{2,1,0:T(8,128)(2,1)}), bf16[16,192,128]{2,1,0:T(8,128)(2,1)}, u32[]{:S(2)}, u32[]{:S(2)}) async-start(bf16[16,192,128]{2,1,0:T(8,128)(2,1)} %broadcast_in_dim.10), calls=%async_computation.1 | async-start | bytes 1572864 | tf_op jit(solution)/shard_map/all_to_all | solution.py:23
  37.8 17.3 %collective-permute-start = (bf16[2,128,512]{2,1,0:T(8,128)(2,1)S(1)}, bf16[2,128,512]{2,1,0:T(8,128)(2,1)S(1)}, u32[]{:S(2)}, u32[]{:S(2)}) collective-permute-start(bf16[2,128,512]{2,1,0:T(8,128)(2,1)S(1)} %slice.27), channel_id=1, source_target_pairs={{0,32},{32,64},{64,96},{96,128},{128,160},{160,192},{192,224},{224... | collective-permute-start | bytes 786440 | tf_op jit(solution)/shard_map/ppermute | solution.py:18
  48.7 10.5 %collective-permute-start.1 = (bf16[16,192,128]{2,1,0:T(8,128)(2,1)}, bf16[16,192,128]{2,1,0:T(8,128)(2,1)}, u32[]{:S(2)}, u32[]{:S(2)}) collective-permute-start(bf16[16,192,128]{2,1,0:T(8,128)(2,1)} %all-to-all-done.1), channel_id=1, source_target_pairs={{0,1},{1,0},{2,3},{3,2},{4,5},{5,4},{6,7},{7,6},{8,9},{9,8},{10,11... | collective-permute-start | bytes 2359304 | tf_op jit(solution)/shard_map/ppermute | solution.py:27
  60.8 1.2 copy-start.7
  62.1 2.4 %copy-start = (bf16[4,4,2,48,4,128]{5,4,3,2,1,0:T(4,128)(2,1)}, bf16[4,4,2,48,4,128]{5,4,3,2,1,0:T(4,128)(2,1)S(1)}, u32[]{:S(2)}) copy-start(bf16[4,4,2,48,4,128]{5,4,3,2,1,0:T(4,128)(2,1)S(1)} %copy.16) | copy-start | bytes 4718596
  62.1 2.5 %copy-start.2 = (bf16[1024,1536]{0,1:T(8,128)(2,1)S(1)}, bf16[1024,1536]{0,1:T(8,128)(2,1)}, u32[]{:S(2)}) copy-start(bf16[1024,1536]{0,1:T(8,128)(2,1)} %copy.17) | copy-start | bytes 9437188
  64.5 1.9 %copy-start.5 = (bf16[1024,512]{1,0:T(8,128)(2,1)}, bf16[1024,512]{1,0:T(8,128)(2,1)S(1)}, u32[]{:S(2)}) copy-start(bf16[1024,512]{1,0:T(8,128)(2,1)S(1)} %fusion) | copy-start | bytes 3145732
  66.4 1.6 %copy-start.3 = (f32[4,4,2,48,512]{4,3,2,1,0:T(8,128)}, f32[4,4,2,48,512]{4,3,2,1,0:T(8,128)S(1)}, u32[]{:S(2)}) copy-start(f32[4,4,2,48,512]{4,3,2,1,0:T(8,128)S(1)} %fusion.8) | copy-start | bytes 9437188
  69.4 5.6 %collective-permute-start.3 = (f32[4,4,48,512]{3,2,1,0:T(8,128)}, f32[4,4,48,512]{3,2,1,0:T(8,128)S(1)}, u32[]{:S(2)}, u32[]{:S(2)}) collective-permute-start(f32[4,4,48,512]{3,2,1,0:T(8,128)} %dynamic-slice_bitcast_fusion), channel_id=1, source_target_pairs={{0,1},{1,0},{2,3},{3,2},{4,5},{5,4},{6,7},{7,6},{8,9},{9,8},{10,11... | collective-permute-start | bytes 4718600 | tf_op jit(solution)/shard_map/ppermute | solution.py:27
  76.7 6.9 %copy-start.6 = (bf16[1024,512]{1,0:T(8,128)(2,1)S(1)}, bf16[1024,512]{1,0:T(8,128)(2,1)}, u32[]{:S(2)}) copy-start(bf16[1024,512]{1,0:T(8,128)(2,1)} %copy-done.5) | copy-start | bytes 3145732
  76.9 14.6 %copy-start.1 = (bf16[4,4,2,48,4,128]{5,4,3,2,1,0:T(4,128)(2,1)S(1)}, bf16[4,4,2,48,4,128]{5,4,3,2,1,0:T(4,128)(2,1)}, u32[]{:S(2)}) copy-start(bf16[4,4,2,48,4,128]{5,4,3,2,1,0:T(4,128)(2,1)} %copy-done) | copy-start | bytes 4718596
  78.0 27.2 %all-to-all-start.2 = ((bf16[16,192,128]{2,1,0:T(8,128)(2,1)}), bf16[16,192,128]{2,1,0:T(8,128)(2,1)S(1)}, u32[]{:S(2)}, u32[]{:S(2)}) async-start(bf16[16,192,128]{2,1,0:T(8,128)(2,1)} %bitcast.21), calls=%async_computation.2 | async-start | bytes 1572864 | tf_op jit(solution)/shard_map/all_to_all | solution.py:59
  84.4 16.0 %collective-permute-start.2 = (bf16[2,128,512]{2,1,0:T(8,128)(2,1)}, bf16[2,128,512]{2,1,0:T(8,128)(2,1)}, u32[]{:S(2)}, u32[]{:S(2)}) collective-permute-start(bf16[2,128,512]{2,1,0:T(8,128)(2,1)} %slice.35), channel_id=1, source_target_pairs={{32,0},{64,32},{96,64},{128,96},{160,128},{192,160},{224,192},{256... | collective-permute-start | bytes 786440 | tf_op jit(solution)/shard_map/ppermute | solution.py:18
  105.9 22.1 %all-to-all-start.3 = ((f32[16,12,128]{2,1,0:T(8,128)}), f32[16,12,128]{2,1,0:T(8,128)S(1)}, u32[]{:S(2)}, u32[]{:S(2)}) async-start(f32[16,12,128]{2,1,0:T(8,128)} %reshape.62), calls=%async_computation.3 | async-start | bytes 262144 | tf_op jit(solution)/shard_map/all_to_all | solution.py:61
  128.7 14.9 %all-to-all-start.4 = ((f32[16,12,128]{2,1,0:T(8,128)}), f32[16,12,128]{2,1,0:T(8,128)S(1)}, u32[]{:S(2)}, u32[]{:S(2)}) async-start(f32[16,12,128]{2,1,0:T(8,128)} %broadcast_in_dim.22), calls=%async_computation.4 | async-start | bytes 262144 | tf_op jit(solution)/shard_map/all_to_all | solution.py:23
  134.7 9.0 %copy-start.8 = (f32[48,512]{1,0:T(8,128)S(1)}, f32[48,512]{1,0:T(8,128)}, u32[]{:S(2)}) copy-start(f32[48,512]{1,0:T(8,128)} %param.9) | copy-start | bytes 294916
  134.7 9.0 %copy-start.9 = (f32[48,512]{1,0:T(8,128)S(1)}, f32[48,512]{1,0:T(8,128)}, u32[]{:S(2)}) copy-start(f32[48,512]{1,0:T(8,128)} %param.10) | copy-start | bytes 294916

commit v2 on v1

v2 whole, which is shorter than its diff:
```python
import jax
import jax.numpy as jnp
from jax import lax
from jax.experimental import pallas as pl
from jax.experimental.pallas import tpu as pltpu
from jax.sharding import Mesh
from jax.sharding import PartitionSpec as P

DILATION_GAP = 64
TM = ("z_lo", "y")
SERIES = ("z_hi", "x", "core")
PLANE = ("x", "y")
LINE = ("z_hi", "z_lo")
BLOCK_ROWS = 48


def passed_along(array, by):
    size = lax.axis_size(TM)
    pairs = [(i, i + by) for i in range(size) if 0 <= i + by < size]
    return lax.ppermute(array, TM, pairs)


def gathered(piece, axes):
    size = lax.axis_size(axes)
    return lax.all_to_all(jnp.broadcast_to(piece[None], (size,) + piece.shape), axes, 0, 0)


def swapped(array):
    return lax.ppermute(array, "core", [(0, 1), (1, 0)])


def gather_weight(shard):
    rows, width = shard.shape
    z_hi, z_lo = lax.axis_size("z_hi"), lax.axis_size("z_lo")
    part, lanes = rows // z_lo, width // lax.axis_size("y")
    piece = lax.dynamic_slice(
        shard, (lax.axis_index("z_lo") * part, lax.axis_index("y") * lanes), (part, lanes)
    )
    line = gathered(piece, LINE).reshape(z_hi * rows, lanes)
    mine = gathered(line, PLANE)
    return mine, swapped(mine)


def layer_kernel(
    core_ref, mine_ref, other_ref, near_ref, mid_ref, up_ref, dpre_ref, wide_ref, keep_ref, give_ref, acc_ref
):
    series_n, time_n, width = up_ref.shape
    span = near_ref.shape[1] - time_n
    own_n = time_n - span
    planes, line_rows, lanes = mine_ref.shape
    y = width // lanes
    x = planes // y
    rows = BLOCK_ROWS
    z_hi = line_rows // rows
    core = core_ref[0]

    def blocks():
        for h in range(z_hi):
            for i in range(x):
                for j in range(y):
                    yield h, (h * x + i) * 2 * rows, i * y + j, j * lanes

    own, far = core * rows, (1 - core) * rows
    for h, base, p, lane in blocks():
        here = pl.ds(pl.multiple_of(base + own, 16), rows)
        there = pl.ds(pl.multiple_of(base + far, 16), rows)
        wide_ref[here, lane : lane + lanes] = mine_ref[p, h * rows : (h + 1) * rows, :]
        wide_ref[there, lane : lane + lanes] = other_ref[p, h * rows : (h + 1) * rows, :]
    chunk = 128
    for s in range(series_n):
        for m in range(0, time_n, chunk):
            taken = (
                near_ref[s, span + m : span + m + chunk, :],
                mid_ref[s, m : m + chunk, :],
                near_ref[s, m : m + chunk, :],
            )
            pre = sum(
                jnp.dot(
                    t,
                    wide_ref[k * width : (k + 1) * width, :],
                    preferred_element_type=jnp.float32,
                )
                for k, t in enumerate(taken)
            )
            sig = jax.nn.sigmoid(pre)
            up = up_ref[s, m : m + chunk, :].astype(jnp.float32)
            dpre_ref[s, m : m + chunk, :] = (up * (sig * (1.0 + pre * (1.0 - sig)))).astype(
                jnp.bfloat16
            )
    for k in range(3):
        for s in range(series_n):
            taken = (
                near_ref[s, span : span + own_n, :],
                mid_ref[s, :own_n, :],
                near_ref[s, :own_n, :],
            )[k]
            part = lax.dot_general(
                taken,
                dpre_ref[s, :own_n, :],
                (((0,), (0,)), ((), ())),
                preferred_element_type=jnp.float32,
            )
            if s == 0:
                acc_ref[k * width : (k + 1) * width, :] = part
            else:
                acc_ref[k * width : (k + 1) * width, :] += part
    for h, base, p, lane in blocks():
        here = pl.ds(pl.multiple_of(base + own, 8), rows)
        there = pl.ds(pl.multiple_of(base + far, 8), rows)
        keep_ref[p, h * rows : (h + 1) * rows, :] = acc_ref[here, lane : lane + lanes]
        give_ref[p, h * rows : (h + 1) * rows, :] = acc_ref[there, lane : lane + lanes]


def layer(core, mine, other, near, mid, up):
    planes, line_rows, lanes = mine.shape
    width = up.shape[-1]
    total = 2 * planes * line_rows * lanes // width
    half = jax.ShapeDtypeStruct(mine.shape, jnp.float32)
    spec = pl.BlockSpec(memory_space=pltpu.VMEM)
    return pl.pallas_call(
        layer_kernel,
        in_specs=[pl.BlockSpec(memory_space=pltpu.SMEM)] + [spec] * 5,
        out_specs=[spec] * 4,
        out_shape=[
            jax.ShapeDtypeStruct(up.shape, jnp.bfloat16),
            jax.ShapeDtypeStruct((total, width), jnp.bfloat16),
            half,
            half,
        ],
        scratch_shapes=[pltpu.VMEM((total, width), jnp.float32)],
        compiler_params=pltpu.CompilerParams(vmem_limit_bytes=40 * 1024 * 1024),
        name="layer",
    )(core, mine, other, near, mid, up)


def reduce_grad(keep, give, rows):
    z_hi, z_lo, y = lax.axis_size("z_hi"), lax.axis_size("z_lo"), lax.axis_size("y")
    lanes = keep.shape[-1]
    chunks = (keep + swapped(give)).astype(jnp.bfloat16)
    plane = jnp.sum(lax.all_to_all(chunks, PLANE, 0, 0).astype(jnp.float32), 0)
    line = plane.reshape(z_hi * z_lo, rows // z_lo, lanes)
    piece = jnp.sum(lax.all_to_all(line, LINE, 0, 0), 0)
    pieces = gathered(piece, TM).reshape(z_lo, y, rows // z_lo, lanes)
    return pieces.transpose(0, 2, 1, 3).reshape(rows, y * lanes), plane


def adamw(weight, grad, moment_one, second_moment_state):
    first = 0.9 * moment_one + 0.1 * grad
    second = 0.999 * second_moment_state + 0.001 * grad * grad
    unbiased_one = first / (1.0 - 0.9**10)
    unbiased_two = second / (1.0 - 0.999**10)
    updated = weight - 0.01 * (unbiased_one / (jnp.sqrt(unbiased_two) + 1e-08) + 0.1 * weight)
    return (updated, first, second)


def body(inputs, cotangent, taps, weight, moment_one, second_moment_state):
    series_n, time_n, width = inputs.shape
    span = 2 * DILATION_GAP
    mine, other = gather_weight(weight.astype(jnp.bfloat16))
    earlier = passed_along(inputs[:, time_n - span :, :], 1)
    later = passed_along(jnp.stack([inputs[:, :span, :], cotangent[:, :span, :]]), -1)
    near = jnp.concatenate([earlier, inputs, later[0]], 1)
    up = jnp.concatenate([cotangent, later[1]], 1)
    mid = lax.dynamic_slice_in_dim(near, span - taps[1], time_n + span, 1)
    core = lax.axis_index("core").astype(jnp.int32).reshape(1)
    dpre, wide, keep, give = layer(core, mine, other, near, mid, up)
    grad_shard, plane = reduce_grad(keep, give, weight.shape[0])
    dpre, plane = lax.optimization_barrier((dpre, plane))
    result = cotangent.reshape(-1, width).astype(jnp.float32)
    for k, moved in enumerate(
        (dpre[:, :time_n], lax.dynamic_slice_in_dim(dpre, taps[1], time_n, 1), dpre[:, span:])
    ):
        result = result + lax.dot_general(
            moved.reshape(-1, width),
            wide[k * width : (k + 1) * width],
            (((1,), (1,)), ((), ())),
            preferred_element_type=jnp.float32,
        )
    grad_input = result.astype(jnp.bfloat16).reshape(series_n, time_n, width)
    new_weight, new_moment_one, new_moment_two = adamw(
        weight, grad_shard, moment_one, second_moment_state
    )
    return (grad_input, new_weight, new_moment_one, new_moment_two)


def solution(mesh):
    torus = Mesh(mesh.devices.reshape(4, 4, 4, 4, 2), TM + SERIES)
    tokens = P(SERIES, TM, None)
    rows = P(SERIES, None)
    return jax.shard_map(
        body,
        mesh=torus,
        in_specs=(tokens, tokens, P(), rows, rows, rows),
        out_specs=(tokens, rows, rows, rows),
        check_vma=False,
    )
```

time: 146 us -> 137 us (0.938)
  blocking collectives: 27.7 us -> 0 us
  starting transfers between devices: 35.7 us -> 55.5 us
  waiting for transfers between devices: 32.3 us -> 49.5 us
  other arithmetic: 10.1 us -> 2.98 us
  between operations: 10.7 us -> 4.11 us
  matrix products: 13.5 us -> 8.45 us
  local copies, waits for them, and re-layouts: 15.4 us -> 10.6 us
  Pallas kernels: 0 us -> 4.35 us
    all_to_all x1 -> x0, blocking collectives: 27.7 us -> none  [gathered(): lax.all_to_all(jnp.broadcast_to(piece[None], (size,) + piece.shape), axes...]
    all_to_all x2 -> x3, starting transfers between devices: 13.4 us -> 26.8 us  [gathered(): lax.all_to_all(jnp.broadcast_to(piece[None], (size,) + piece.shape), axes...]
    all_to_all x1, starting transfers between devices: 5.7 us -> 17.6 us  [reduce_grad(): plane = jnp.sum(lax.all_to_all(chunks, PLANE, 0, 0).astype(jnp.float32), 0)]
    all_to_all x1, waiting for transfers between devices: 0.01 us -> 10.7 us  [reduce_grad(): plane = jnp.sum(lax.all_to_all(chunks, PLANE, 0, 0).astype(jnp.float32), 0)]
    all_to_all x2 -> x3, waiting for transfers between devices: 12.7 us -> 23.1 us  [gathered(): lax.all_to_all(jnp.broadcast_to(piece[None], (size,) + piece.shape), axes...]
    dot_general x5 -> x3, matrix products: 13.5 us -> 8.45 us  [body(): lax.dot_general(moved.reshape(-1, width), wide[k * width:(k + 1) * width]...]
    concatenate x2, other arithmetic: 5 us -> 0.19 us  [the longest x1 0.1 us: body(): near = jnp.concatenate([earlier, inputs, later[0]], 1)]
    pallas_call x0 -> x1, Pallas kernels: none -> 4.35 us  [layer(): pl.pallas_call(layer_kernel, in_specs=[pl.BlockSpec(memory_space=pltpu.SM...]
  transfers between devices with their start and end apart: 8 -> 9, of which waited for: 5 -> 8; matrix products, arithmetic and copies ran while one was open for 14% -> 11% of each run, Pallas kernels for 0% -> 0%
where the time goes in v2:
time: 137 us; the launch traced here: 136 us
  starting transfers between devices  55.5 us (41%)
  waiting for transfers between devices  49.5 us (36%)
  local copies, waits for them, and re-layouts  10.6 us (8%)
  matrix products  8.45 us (6%)
  Pallas kernels  4.35 us (3%)
  between operations  4.11 us (3%)
  other arithmetic  2.98 us (2%)
    all_to_all x3, starting transfers between devices, gathered(): lax.all_to_all(jnp.broadcast_to(piece[None], (size,) + piece.shape), axes...  26.8 us
    all_to_all x3, waiting for transfers between devices, gathered(): lax.all_to_all(jnp.broadcast_to(piece[None], (size,) + piece.shape), axes...  23.1 us
    all_to_all x1, starting transfers between devices, reduce_grad(): plane = jnp.sum(lax.all_to_all(chunks, PLANE, 0, 0).astype(jnp.float32), 0)  17.6 us
    all_to_all x1, waiting for transfers between devices, reduce_grad(): plane = jnp.sum(lax.all_to_all(chunks, PLANE, 0, 0).astype(jnp.float32), 0)  10.7 us
    dot_general x3, matrix products, body(): lax.dot_general(moved.reshape(-1, width), wide[k * width:(k + 1) * width]...  8.45 us
    all_to_all x1, waiting for transfers between devices, reduce_grad(): piece = jnp.sum(lax.all_to_all(line, LINE, 0, 0), 0)  7.93 us
    ppermute x2, waiting for transfers between devices, passed_along(): return lax.ppermute(array, TM, pairs)  4.46 us
    pallas_call x1, Pallas kernels, layer(): pl.pallas_call(layer_kernel, in_specs=[pl.BlockSpec(memory_space=pltpu.SM...  4.35 us
  transfers between devices with their start and end apart: 9, of which 8 were waited for; matrix products, arithmetic and copies ran while one was open for 11% of the time, Pallas kernels for 0%

profile of v2, /device:TPU:6, one launch (start us, length us, event | category | flops | bytes accessed | tf_op | source)
XLA Modules:
  0.0 135.6 jit_solution(10414910051785755307)
XLA Ops:
  0.6 0.8 dynamic_slice.16
  1.4 0.6 broadcast_in_dim.8
  2.1 15.2 %all-to-all-start = ((bf16[16,12,128]{2,1,0:T(8,128)(2,1)}), bf16[16,12,128]{2,1,0:T(8,128)(2,1)S(1)}, u32[]{:S(2)}, u32[]{:S(2)}) async-start(bf16[16,12,128]{2,1,0:T(8,128)(2,1)} %broadcast_in_dim.8), calls=%async_computation | async-start | bytes 131072 | tf_op jit(solution)/shard_map/all_to_all | solution.py:25
  17.3 1.0 slice_bitcast_fusion.2
  18.3 11.7 %all-to-all-done = bf16[16,12,128]{2,1,0:T(8,128)(2,1)S(1)} async-done(((bf16[16,12,128]{2,1,0:T(8,128)(2,1)}), bf16[16,12,128]{2,1,0:T(8,128)(2,1)S(1)}, u32[]{:S(2)}, u32[]{:S(2)}) %all-to-all-start) | async-done | bytes 49184 | tf_op jit(solution)/shard_map/all_to_all | solution.py:25
  30.0 1.0 broadcast_in_dim.10
  31.1 0.0 copy-start.8
  31.1 7.5 %all-to-all-start.1 = ((bf16[16,192,128]{2,1,0:T(8,128)(2,1)}), bf16[16,192,128]{2,1,0:T(8,128)(2,1)S(1)}, u32[]{:S(2)}, u32[]{:S(2)}) async-start(bf16[16,192,128]{2,1,0:T(8,128)(2,1)} %broadcast_in_dim.10), calls=%async_computation.1 | async-start | bytes 1572864 | tf_op jit(solution)/shard_map/all_to_all | solution.py:25
  38.6 0.0 copy-start.2
  38.6 1.9 %fusion.16 = (bf16[2,128,512]{2,1,0:T(8,128)(2,1)}, bf16[1,2,128,512]{3,2,1,0:T(8,128)(2,1)S(1)}) fusion(bf16[2,512,512]{2,1,0:T(8,128)(2,1)} %param.6), kind=kLoop, calls=%fused_computation.28 | loop fusion | bytes 1048576 | tf_op jit(solution)/shard_map/slice | solution.py:160
  40.5 0.9 pad_maximum_fusion.2
  41.3 1.3 collective-permute-start.2
  42.6 6.8 %all-to-all-done.1.mine_ref = bf16[16,192,128]{2,1,0:T(8,128)(2,1)S(1)} async-done(((bf16[16,192,128]{2,1,0:T(8,128)(2,1)}), bf16[16,192,128]{2,1,0:T(8,128)(2,1)S(1)}, u32[]{:S(2)}, u32[]{:S(2)}) %all-to-all-start.1) | async-done | bytes 786464 | tf_op jit(solution)/shard_map/all_to_all | solution.py:25
  49.4 1.9 %collective-permute-start = (bf16[16,192,128]{2,1,0:T(8,128)(2,1)S(1)}, bf16[16,192,128]{2,1,0:T(8,128)(2,1)S(1)}, u32[]{:S(2)}, u32[]{:S(2)}) collective-permute-start(bf16[16,192,128]{2,1,0:T(8,128)(2,1)S(1)} %all-to-all-done.1.mine_ref), channel_id=1, source_target_pairs={{0,1},{1,0},{2,3},{3,2},{4,5},{5,4},{6,7},{7,6},{8,9},{9,8},{10,11... | collective-permute-start | bytes 2359304 | tf_op jit(solution)/shard_map/ppermute | solution.py:29
  51.3 2.6 %collective-permute-start.1 = (bf16[2,128,512]{2,1,0:T(8,128)(2,1)}, bf16[2,128,512]{2,1,0:T(8,128)(2,1)S(1)}, u32[]{:S(2)}, u32[]{:S(2)}) collective-permute-start(bf16[2,128,512]{2,1,0:T(8,128)(2,1)} %get-tuple-element.20), channel_id=1, source_target_pairs={{0,32},{32,64},{64,96},{96,128},{128,160},{160,192},{192,224},{224... | collective-permute-start | bytes 786440 | tf_op jit(solution)/shard_map/ppermute | solution.py:20
  53.9 0.0 copy-done.8
  53.9 0.6 slice.38
  55.8 2.8 %collective-permute-done.2 = bf16[2,2,128,512]{3,2,1,0:T(8,128)(2,1)S(1)} collective-permute-done((bf16[2,2,128,512]{3,2,1,0:T(8,128)(2,1)}, bf16[2,2,128,512]{3,2,1,0:T(8,128)(2,1)S(1)}, u32[]{:S(2)}, u32[]{:S(2)}) %collective-permute-start.2) | collective-permute-done | bytes 524320 | tf_op jit(solution)/shard_map/ppermute | solution.py:20
  58.7 0.0 copy-start.4
  58.7 0.0 copy-done.2
  58.7 0.1 pad_maximum_fusion.1.up_ref
  58.8 1.6 %collective-permute-done.1 = bf16[2,128,512]{2,1,0:T(8,128)(2,1)S(1)} collective-permute-done((bf16[2,128,512]{2,1,0:T(8,128)(2,1)}, bf16[2,128,512]{2,1,0:T(8,128)(2,1)S(1)}, u32[]{:S(2)}, u32[]{:S(2)}) %collective-permute-start.1) | collective-permute-done | bytes 262176 | tf_op jit(solution)/shard_map/ppermute | solution.py:20
  60.4 0.0 copy-done.4
  60.4 0.1 pad_maximum_fusion.near_ref
  60.6 0.3 constant_dynamic-slice_fusion.1.mid_ref
  60.9 0.0 collective-permute-done.other_ref
  60.9 4.3 %layer.1 = (bf16[2,640,512]{2,1,0:T(8,128)(2,1)S(1)}, bf16[1536,512]{1,0:T(8,128)(2,1)S(1)}, f32[16,192,128]{2,1,0:T(8,128)S(1)}, f32[16,192,128]{2,1,0:T(8,128)S(1)}) custom-call(s32[1]{0:T(128)} %bitcast.1.core_ref, bf16[16,192,128]{2,1,0:T(8,128)(2,1)S(1)} %all-to-all-done.1.mine_ref, bf16[16,192,128]{2,1,0:T(8,128)(2,1)S(1)} %collective-permute-done.other_ref, ...), custom_call_target="tpu_custom_call" | custom-call | tf_op jit(solution)/shard_map/layer/pallas_call | solution.py:120
  65.2 0.0 copy-start
  65.2 1.2 copy-done
  66.4 1.9 %collective-permute-start.3 = (f32[16,192,128]{2,1,0:T(8,128)S(1)}, f32[16,192,128]{2,1,0:T(8,128)S(1)}, u32[]{:S(2)}, u32[]{:S(2)}) collective-permute-start(f32[16,192,128]{2,1,0:T(8,128)S(1)} %get-tuple-element.11), channel_id=1, source_target_pairs={{0,1},{1,0},{2,3},{3,2},{4,5},{5,4},{6,7},{7,6},{8,9},{9,8},{10,11... | collective-permute-start | bytes 4718600 | tf_op jit(solution)/shard_map/ppermute | solution.py:29
  68.3 3.4 %collective-permute-done.3 = f32[16,192,128]{2,1,0:T(8,128)S(1)} collective-permute-done((f32[16,192,128]{2,1,0:T(8,128)S(1)}, f32[16,192,128]{2,1,0:T(8,128)S(1)}, u32[]{:S(2)}, u32[]{:S(2)}) %collective-permute-start.3) | collective-permute-done | bytes 1572896 | tf_op jit(solution)/shard_map/ppermute | solution.py:29
  71.7 1.1 add_convert_fusion
  72.8 17.6 %all-to-all-start.2 = ((bf16[16,192,128]{2,1,0:T(8,128)(2,1)}), bf16[16,192,128]{2,1,0:T(8,128)(2,1)S(1)}, u32[]{:S(2)}, u32[]{:S(2)}) async-start(bf16[16,192,128]{2,1,0:T(8,128)(2,1)} %add_convert_fusion), calls=%async_computation.2 | async-start | bytes 1572864 | tf_op jit(solution)/shard_map/all_to_all | solution.py:140
  92.3 10.7 %all-to-all-done.2 = bf16[16,192,128]{2,1,0:T(8,128)(2,1)S(1)} async-done(((bf16[16,192,128]{2,1,0:T(8,128)(2,1)}), bf16[16,192,128]{2,1,0:T(8,128)(2,1)S(1)}, u32[]{:S(2)}, u32[]{:S(2)}) %all-to-all-start.2) | async-done | bytes 786464 | tf_op jit(solution)/shard_map/all_to_all | solution.py:140
  102.9 0.1 convert_reduce_fusion
  103.0 0.7 reshape.43
  103.7 3.5 %all-to-all-start.3 = ((f32[16,12,128]{2,1,0:T(8,128)}), f32[16,12,128]{2,1,0:T(8,128)S(1)}, u32[]{:S(2)}, u32[]{:S(2)}) async-start(f32[16,12,128]{2,1,0:T(8,128)} %reshape.43), calls=%async_computation.3 | async-start | bytes 262144 | tf_op jit(solution)/shard_map/all_to_all | solution.py:142
  107.2 0.0 copy-start.1
  107.2 1.3 fusion.15
  108.5 0.5 copy-done.1
  109.0 2.1 %fusion.7 = f32[1024,512]{1,0:T(8,128)} fusion(bf16[1024,512]{1,0:T(8,128)(2,1)S(1)} %bitcast.34, bf16[1536,512]{1,0:T(8,128)(2,1)S(1)} %copy-done.1), kind=kOutput, calls=%fused_computation.11 | convolution fusion | flops 536870912 | bytes 3670016 | tf_op jit(solution)/shard_map/dot_general | solution.py:173
  111.1 0.0 copy-start.3
  111.1 2.1 %fusion.9 = f32[1024,512]{1,0:T(8,128)} fusion(bf16[1024,512]{1,0:T(8,128)(2,1)S(1)} %bitcast.33, bf16[1536,512]{1,0:T(8,128)(2,1)S(1)} %copy-done.1), kind=kOutput, calls=%fused_computation.13 | convolution fusion | flops 536870912 | bytes 3670016 | tf_op jit(solution)/shard_map/dot_general | solution.py:173
  113.1 7.9 %all-to-all-done.3 = f32[16,12,128]{2,1,0:T(8,128)S(1)} async-done(((f32[16,12,128]{2,1,0:T(8,128)}), f32[16,12,128]{2,1,0:T(8,128)S(1)}, u32[]{:S(2)}, u32[]{:S(2)}) %all-to-all-start.3) | async-done | bytes 98336 | tf_op jit(solution)/shard_map/all_to_all | solution.py:142
  121.1 0.7 broadcast_in_dim.22
  121.8 4.0 %all-to-all-start.4 = ((f32[16,12,128]{2,1,0:T(8,128)}), f32[16,12,128]{2,1,0:T(8,128)S(1)}, u32[]{:S(2)}, u32[]{:S(2)}) async-start(f32[16,12,128]{2,1,0:T(8,128)} %broadcast_in_dim.22), calls=%async_computation.4 | async-start | bytes 262144 | tf_op jit(solution)/shard_map/all_to_all | solution.py:25
  125.8 0.0 copy-done.3
  125.8 0.0 copy-start.5
  125.9 0.0 copy-start.6
  125.9 0.0 copy-start.7
  125.9 4.3 %fusion.2 = bf16[1024,512]{1,0:T(8,128)(2,1)} fusion(f32[1024,512]{1,0:T(8,128)} %fusion.7, f32[1024,512]{1,0:T(8,128)} %fusion.9, bf16[2,512,512]{2,1,0:T(8,128)(2,1)S(1)} %copy-done.3, bf16[1024,512]{1,0:T(8,128)(2,1)} %bitcast.32, bf16[1536,512]{1,0:T(8,128)(2,1)S(1)} %copy-done.1), kind=kOutput, calls=%fused_computation.3 | convolution fusion | flops 539492352 | bytes 7864320 | tf_op jit(solution)/shard_map/dot_general | solution.py:173
  130.2 4.6 %all-to-all-done.4 = f32[16,12,128]{2,1,0:T(8,128)S(1)} async-done(((f32[16,12,128]{2,1,0:T(8,128)}), f32[16,12,128]{2,1,0:T(8,128)S(1)}, u32[]{:S(2)}, u32[]{:S(2)}) %all-to-all-start.4) | async-done | bytes 98336 | tf_op jit(solution)/shard_map/all_to_all | solution.py:25
  134.8 0.0 copy-done.5
  134.8 0.0 copy-done.6
  134.8 0.0 copy-done.7
  134.9 0.7 multiply_subtract_fusion
  (5 shorter events, 0.1 us)
Async XLA Ops:
  2.1 27.9 %all-to-all-start = ((bf16[16,12,128]{2,1,0:T(8,128)(2,1)}), bf16[16,12,128]{2,1,0:T(8,128)(2,1)S(1)}, u32[]{:S(2)}, u32[]{:S(2)}) async-start(bf16[16,12,128]{2,1,0:T(8,128)(2,1)} %broadcast_in_dim.8), calls=%async_computation | async-start | bytes 131072 | tf_op jit(solution)/shard_map/all_to_all | solution.py:25
  31.1 22.9 %copy-start.8 = (s32[3]{0:T(128)S(1)}, s32[3]{0:T(128)}, u32[]{:S(2)}) copy-start(s32[3]{0:T(128)} %param.8) | copy-start | bytes 40
  31.1 18.4 %all-to-all-start.1 = ((bf16[16,192,128]{2,1,0:T(8,128)(2,1)}), bf16[16,192,128]{2,1,0:T(8,128)(2,1)S(1)}, u32[]{:S(2)}, u32[]{:S(2)}) async-start(bf16[16,192,128]{2,1,0:T(8,128)(2,1)} %broadcast_in_dim.10), calls=%async_computation.1 | async-start | bytes 1572864 | tf_op jit(solution)/shard_map/all_to_all | solution.py:25
  38.6 20.1 %copy-start.2 = (bf16[2,512,512]{2,1,0:T(8,128)(2,1)S(1)}, bf16[2,512,512]{2,1,0:T(8,128)(2,1)}, u32[]{:S(2)}) copy-start(bf16[2,512,512]{2,1,0:T(8,128)(2,1)} %param.7) | copy-start | bytes 3145732
  41.3 17.3 %collective-permute-start.2 = (bf16[2,2,128,512]{3,2,1,0:T(8,128)(2,1)}, bf16[2,2,128,512]{3,2,1,0:T(8,128)(2,1)S(1)}, u32[]{:S(2)}, u32[]{:S(2)}) collective-permute-start(bf16[2,2,128,512]{3,2,1,0:T(8,128)(2,1)} %pad_maximum_fusion.2), channel_id=1, source_target_pairs={{32,0},{64,32},{96,64},{128,96},{160,128},{192,160},{224,192},{256... | collective-permute-start | bytes 1572872 | tf_op jit(solution)/shard_map/ppermute | solution.py:20
  49.4 11.5 %collective-permute-start = (bf16[16,192,128]{2,1,0:T(8,128)(2,1)S(1)}, bf16[16,192,128]{2,1,0:T(8,128)(2,1)S(1)}, u32[]{:S(2)}, u32[]{:S(2)}) collective-permute-start(bf16[16,192,128]{2,1,0:T(8,128)(2,1)S(1)} %all-to-all-done.1.mine_ref), channel_id=1, source_target_pairs={{0,1},{1,0},{2,3},{3,2},{4,5},{5,4},{6,7},{7,6},{8,9},{9,8},{10,11... | collective-permute-start | bytes 2359304 | tf_op jit(solution)/shard_map/ppermute | solution.py:29
  51.3 9.1 %collective-permute-start.1 = (bf16[2,128,512]{2,1,0:T(8,128)(2,1)}, bf16[2,128,512]{2,1,0:T(8,128)(2,1)S(1)}, u32[]{:S(2)}, u32[]{:S(2)}) collective-permute-start(bf16[2,128,512]{2,1,0:T(8,128)(2,1)} %get-tuple-element.20), channel_id=1, source_target_pairs={{0,32},{32,64},{64,96},{96,128},{128,160},{160,192},{192,224},{224... | collective-permute-start | bytes 786440 | tf_op jit(solution)/shard_map/ppermute | solution.py:20
  58.7 1.8 %copy-start.4 = (bf16[2,512,512]{2,1,0:T(8,128)(2,1)S(1)}, bf16[2,512,512]{2,1,0:T(8,128)(2,1)}, u32[]{:S(2)}) copy-start(bf16[2,512,512]{2,1,0:T(8,128)(2,1)} %param.6) | copy-start | bytes 3145732
  65.2 1.2 copy-start
  66.4 5.3 %collective-permute-start.3 = (f32[16,192,128]{2,1,0:T(8,128)S(1)}, f32[16,192,128]{2,1,0:T(8,128)S(1)}, u32[]{:S(2)}, u32[]{:S(2)}) collective-permute-start(f32[16,192,128]{2,1,0:T(8,128)S(1)} %get-tuple-element.11), channel_id=1, source_target_pairs={{0,1},{1,0},{2,3},{3,2},{4,5},{5,4},{6,7},{7,6},{8,9},{9,8},{10,11... | collective-permute-start | bytes 4718600 | tf_op jit(solution)/shard_map/ppermute | solution.py:29
  72.8 30.2 %all-to-all-start.2 = ((bf16[16,192,128]{2,1,0:T(8,128)(2,1)}), bf16[16,192,128]{2,1,0:T(8,128)(2,1)S(1)}, u32[]{:S(2)}, u32[]{:S(2)}) async-start(bf16[16,192,128]{2,1,0:T(8,128)(2,1)} %add_convert_fusion), calls=%async_computation.2 | async-start | bytes 1572864 | tf_op jit(solution)/shard_map/all_to_all | solution.py:140
  103.7 17.4 %all-to-all-start.3 = ((f32[16,12,128]{2,1,0:T(8,128)}), f32[16,12,128]{2,1,0:T(8,128)S(1)}, u32[]{:S(2)}, u32[]{:S(2)}) async-start(f32[16,12,128]{2,1,0:T(8,128)} %reshape.43), calls=%async_computation.3 | async-start | bytes 262144 | tf_op jit(solution)/shard_map/all_to_all | solution.py:142
  107.2 1.8 %copy-start.1 = (bf16[1536,512]{1,0:T(8,128)(2,1)S(1)}, bf16[1536,512]{1,0:T(8,128)(2,1)}, u32[]{:S(2)}) copy-start(bf16[1536,512]{1,0:T(8,128)(2,1)} %copy-done) | copy-start | bytes 4718596
  111.1 14.7 %copy-start.3 = (bf16[2,512,512]{2,1,0:T(8,128)(2,1)S(1)}, bf16[2,512,512]{2,1,0:T(8,128)(2,1)}, u32[]{:S(2)}) copy-start(bf16[2,512,512]{2,1,0:T(8,128)(2,1)} %param.7) | copy-start | bytes 3145732
  121.8 13.0 %all-to-all-start.4 = ((f32[16,12,128]{2,1,0:T(8,128)}), f32[16,12,128]{2,1,0:T(8,128)S(1)}, u32[]{:S(2)}, u32[]{:S(2)}) async-start(f32[16,12,128]{2,1,0:T(8,128)} %broadcast_in_dim.22), calls=%async_computation.4 | async-start | bytes 262144 | tf_op jit(solution)/shard_map/all_to_all | solution.py:25
  125.8 9.0 %copy-start.5 = (f32[48,512]{1,0:T(8,128)S(1)}, f32[48,512]{1,0:T(8,128)}, u32[]{:S(2)}) copy-start(f32[48,512]{1,0:T(8,128)} %param.9) | copy-start | bytes 294916
  125.9 9.0 %copy-start.6 = (f32[48,512]{1,0:T(8,128)S(1)}, f32[48,512]{1,0:T(8,128)}, u32[]{:S(2)}) copy-start(f32[48,512]{1,0:T(8,128)} %param.10) | copy-start | bytes 294916
  125.9 9.0 %copy-start.7 = (f32[48,512]{1,0:T(8,128)S(1)}, f32[48,512]{1,0:T(8,128)}, u32[]{:S(2)}) copy-start(f32[48,512]{1,0:T(8,128)} %param.11) | copy-start | bytes 294916

commit v3 on v2

--- a/solution.py
+++ b/solution.py
@@ -29,24 +29,105 @@
     return lax.ppermute(array, "core", [(0, 1), (1, 0)])
 
 
-def gather_weight(shard):
-    rows, width = shard.shape
-    z_hi, z_lo = lax.axis_size("z_hi"), lax.axis_size("z_lo")
-    part, lanes = rows // z_lo, width // lax.axis_size("y")
-    piece = lax.dynamic_slice(
-        shard, (lax.axis_index("z_lo") * part, lax.axis_index("y") * lanes), (part, lanes)
-    )
-    line = gathered(piece, LINE).reshape(z_hi * rows, lanes)
-    mine = gathered(line, PLANE)
-    return mine, swapped(mine)
+def away(array):
+    return pltpu.with_memory_space_constraint(array, pltpu.HBM)
+
+
+NEAR = pl.BlockSpec(memory_space=pltpu.VMEM)
+AWAY = pl.BlockSpec(memory_space=pltpu.HBM)
+SCALAR = pl.BlockSpec(memory_space=pltpu.SMEM)
+
+
+def limit(mebibytes):
+    return pltpu.CompilerParams(vmem_limit_bytes=mebibytes * 1024 * 1024)
+
+
+def first_kernel(place_ref, in_hbm, weight_hbm, last_ref, piece_ref, weight_ref, sems):
+    copies, part, lanes = piece_ref.shape
+    span = last_ref.shape[1]
+    y = in_hbm.shape[2] // lanes
+    z_lo = weight_ref.shape[0] // part
+    place = place_ref[0]
+    lane = pl.multiple_of((place % y) * lanes, lanes)
+    fetch_weight = pltpu.make_async_copy(
+        weight_hbm.at[:, pl.ds(lane, lanes)], weight_ref, sems.at[0]
+    )
+    fetch_last = pltpu.make_async_copy(
+        in_hbm.at[:, in_hbm.shape[1] - span :, :], last_ref, sems.at[1]
+    )
+    fetch_weight.start()
+    fetch_last.start()
+    fetch_weight.wait()
+    for i in range(z_lo):
+
+        @pl.when(place // y == i)
+        def _():
+            piece = weight_ref[i * part : (i + 1) * part, :].astype(jnp.bfloat16)
+            for n in range(copies):
+                piece_ref[n] = piece
+
+    fetch_last.wait()
+
+
+def first(inputs, weight, span):
+    rows, width = weight.shape
+    z_hi, z_lo, y = lax.axis_size("z_hi"), lax.axis_size("z_lo"), lax.axis_size("y")
+    place = lax.axis_index(TM).astype(jnp.int32).reshape(1)
+    return pl.pallas_call(
+        first_kernel,
+        in_specs=[SCALAR, AWAY, AWAY],
+        out_specs=[NEAR, NEAR],
+        out_shape=[
+            jax.ShapeDtypeStruct((inputs.shape[0], span, width), inputs.dtype),
+            jax.ShapeDtypeStruct((z_hi * z_lo, rows // z_lo, width // y), jnp.bfloat16),
+        ],
+        scratch_shapes=[
+            pltpu.VMEM((rows, width // y), jnp.float32),
+            pltpu.SemaphoreType.DMA((2,)),
+        ],
+        compiler_params=limit(4),
+        name="first",
+    )(place, away(inputs), away(weight))
+
+
+def ready_kernel(in_hbm, early_hbm, mid_hbm, up_hbm, near_ref, mid_ref, up_ref, sems):
+    span = early_hbm.shape[1]
+    copies = [
+        pltpu.make_async_copy(early_hbm, near_ref.at[:, :span, :], sems.at[0]),
+        pltpu.make_async_copy(in_hbm, near_ref.at[:, span:, :], sems.at[1]),
+        pltpu.make_async_copy(mid_hbm, mid_ref, sems.at[2]),
+        pltpu.make_async_copy(up_hbm, up_ref, sems.at[3]),
+    ]
+    for c in copies:
+        c.start()
+    for c in copies:
+        c.wait()
+
+
+def ready(inputs, early, mid, up):
+    series_n, time_n, width = inputs.shape
+    long = (series_n, early.shape[1] + time_n, width)
+    return pl.pallas_call(
+        ready_kernel,
+        in_specs=[AWAY] * 4,
+        out_specs=[NEAR] * 3,
+        out_shape=[
+            jax.ShapeDtypeStruct(long, inputs.dtype),
+            jax.ShapeDtypeStruct(mid.shape, mid.dtype),
+            jax.ShapeDtypeStruct(up.shape, up.dtype),
+        ],
+        scratch_shapes=[pltpu.SemaphoreType.DMA((4,))],
+        compiler_params=limit(4),
+        name="ready",
+    )(away(inputs), away(early), away(mid), away(up))
 
 
 def layer_kernel(
-    core_ref, mine_ref, other_ref, near_ref, mid_ref, up_ref, dpre_ref, wide_ref, keep_ref, give_ref, acc_ref
+    core_ref, mine_ref, other_ref, near_ref, mid_ref, up_ref,
+    dpre_hbm, wide_hbm, keep_ref, give_ref, dpre_ref, wide_ref, acc_ref, sems,
 ):
-    series_n, time_n, width = up_ref.shape
+    series_n, time_n, width = mid_ref.shape
     span = near_ref.shape[1] - time_n
-    own_n = time_n - span
     planes, line_rows, lanes = mine_ref.shape
     y = width // lanes
     x = planes // y
@@ -66,6 +147,8 @@
         there = pl.ds(pl.multiple_of(base + far, 16), rows)
         wide_ref[here, lane : lane + lanes] = mine_ref[p, h * rows : (h + 1) * rows, :]
         wide_ref[there, lane : lane + lanes] = other_ref[p, h * rows : (h + 1) * rows, :]
+    keep_wide = pltpu.make_async_copy(wide_ref, wide_hbm, sems.at[0])
+    keep_wide.start()
     chunk = 128
     for s in range(series_n):
         for m in range(0, time_n, chunk):
@@ -87,16 +170,14 @@
             dpre_ref[s, m : m + chunk, :] = (up * (sig * (1.0 + pre * (1.0 - sig)))).astype(
                 jnp.bfloat16
             )
+    keep_dpre = pltpu.make_async_copy(dpre_ref, dpre_hbm, sems.at[1])
+    keep_dpre.start()
     for k in range(3):
         for s in range(series_n):
-            taken = (
-                near_ref[s, span : span + own_n, :],
-                mid_ref[s, :own_n, :],
-                near_ref[s, :own_n, :],
-            )[k]
+            taken = (near_ref[s, span:, :], mid_ref[s], near_ref[s, :time_n, :])[k]
             part = lax.dot_general(
                 taken,
-                dpre_ref[s, :own_n, :],
+                dpre_ref[s],
                 (((0,), (0,)), ((), ())),
                 preferred_element_type=jnp.float32,
             )
@@ -109,6 +190,8 @@
         there = pl.ds(pl.multiple_of(base + far, 8), rows)
         keep_ref[p, h * rows : (h + 1) * rows, :] = acc_ref[here, lane : lane + lanes]
         give_ref[p, h * rows : (h + 1) * rows, :] = acc_ref[there, lane : lane + lanes]
+    keep_wide.wait()
+    keep_dpre.wait()
 
 
 def layer(core, mine, other, near, mid, up):
@@ -116,21 +199,86 @@
     width = up.shape[-1]
     total = 2 * planes * line_rows * lanes // width
     half = jax.ShapeDtypeStruct(mine.shape, jnp.float32)
-    spec = pl.BlockSpec(memory_space=pltpu.VMEM)
     return pl.pallas_call(
         layer_kernel,
-        in_specs=[pl.BlockSpec(memory_space=pltpu.SMEM)] + [spec] * 5,
-        out_specs=[spec] * 4,
+        in_specs=[SCALAR] + [NEAR] * 5,
+        out_specs=[AWAY, AWAY, NEAR, NEAR],
         out_shape=[
-            jax.ShapeDtypeStruct(up.shape, jnp.bfloat16),
-            jax.ShapeDtypeStruct((total, width), jnp.bfloat16),
+            pltpu.HBM(up.shape, jnp.bfloat16),
+            pltpu.HBM((total, width), jnp.bfloat16),
             half,
             half,
         ],
-        scratch_shapes=[pltpu.VMEM((total, width), jnp.float32)],
-        compiler_params=pltpu.CompilerParams(vmem_limit_bytes=40 * 1024 * 1024),
+        scratch_shapes=[
+            pltpu.VMEM(up.shape, jnp.bfloat16),
+            pltpu.VMEM((total, width), jnp.bfloat16),
+            pltpu.VMEM((total, width), jnp.float32),
+            pltpu.SemaphoreType.DMA((2,)),
+        ],
+        compiler_params=limit(16),
         name="layer",
     )(core, mine, other, near, mid, up)
+
+
+def spread(first, second, third, wide_ref, up):
+    width = up.shape[-1]
+    result = up.astype(jnp.float32)
+    for k, t in enumerate((first, second, third)):
+        result = result + lax.dot_general(
+            t,
+            wide_ref[k * width : (k + 1) * width, :],
+            (((1,), (1,)), ((), ())),
+            preferred_element_type=jnp.float32,
+        )
+    return result.astype(jnp.bfloat16)
+
+
+def main_kernel(dpre_ref, mid_ref, wide_ref, up_ref, out_hbm, out_ref, sem):
+    series_n, time_n, _ = dpre_ref.shape
+    rows = mid_ref.shape[1]
+    for s in range(series_n):
+        out_ref[s] = spread(
+            dpre_ref[s, :rows, :],
+            mid_ref[s],
+            dpre_ref[s, time_n - rows :, :],
+            wide_ref,
+            up_ref[s, :rows, :],
+        )
+    out = pltpu.make_async_copy(out_ref, out_hbm.at[:, :rows, :], sem)
+    out.start()
+    out.wait()
+
+
+def tail_kernel(dpre_ref, mid_ref, ahead_ref, wide_ref, up_ref, part_hbm, out_hbm, out_ref, sem):
+    series_n, time_n, _ = dpre_ref.shape
+    rows = mid_ref.shape[1]
+    for s in range(series_n):
+        out_ref[s] = spread(
+            dpre_ref[s, time_n - rows :, :],
+            mid_ref[s],
+            ahead_ref[s],
+            wide_ref,
+            up_ref[s, time_n - rows :, :],
+        )
+    out = pltpu.make_async_copy(out_ref, out_hbm.at[:, time_n - rows :, :], sem)
+    out.start()
+    out.wait()
+
+
+def input_grad(kernel, operands, mid, aliases, name):
+    specs = [NEAR] * len(operands)
+    if aliases:
+        specs[-1] = AWAY
+    return pl.pallas_call(
+        kernel,
+        in_specs=specs,
+        out_specs=AWAY,
+        out_shape=jax.ShapeDtypeStruct(operands[0].shape, jnp.bfloat16),
+        scratch_shapes=[pltpu.VMEM(mid.shape, jnp.bfloat16), pltpu.SemaphoreType.DMA],
+        input_output_aliases=aliases,
+        compiler_params=limit(8),
+        name=name,
+    )(*operands)
 
 
 def reduce_grad(keep, give, rows):
@@ -154,29 +302,33 @@
 
 
 def body(inputs, cotangent, taps, weight, moment_one, second_moment_state):
-    series_n, time_n, width = inputs.shape
+    time_n = inputs.shape[1]
     span = 2 * DILATION_GAP
-    mine, other = gather_weight(weight.astype(jnp.bfloat16))
-    earlier = passed_along(inputs[:, time_n - span :, :], 1)
-    later = passed_along(jnp.stack([inputs[:, :span, :], cotangent[:, :span, :]]), -1)
-    near = jnp.concatenate([earlier, inputs, later[0]], 1)
-    up = jnp.concatenate([cotangent, later[1]], 1)
-    mid = lax.dynamic_slice_in_dim(near, span - taps[1], time_n + span, 1)
+    kept = time_n - span
     core = lax.axis_index("core").astype(jnp.int32).reshape(1)
+    last, piece = first(inputs, weight, span)
+    early = passed_along(last, 1)
+    line, early = lax.optimization_barrier((lax.all_to_all(piece, LINE, 0, 0), early))
+    mid = lax.dynamic_slice_in_dim(
+        jnp.concatenate([early, inputs], 1), span - taps[1], time_n, 1
+    )
+    mine = gathered(line.reshape(-1, line.shape[-1]), PLANE)
+    mine, early, mid, core = lax.optimization_barrier((mine, early, mid, core))
+    other = swapped(mine)
+    near, mid, up = ready(inputs, early, mid, cotangent)
     dpre, wide, keep, give = layer(core, mine, other, near, mid, up)
     grad_shard, plane = reduce_grad(keep, give, weight.shape[0])
     dpre, plane = lax.optimization_barrier((dpre, plane))
-    result = cotangent.reshape(-1, width).astype(jnp.float32)
-    for k, moved in enumerate(
-        (dpre[:, :time_n], lax.dynamic_slice_in_dim(dpre, taps[1], time_n, 1), dpre[:, span:])
-    ):
-        result = result + lax.dot_general(
-            moved.reshape(-1, width),
-            wide[k * width : (k + 1) * width],
-            (((1,), (1,)), ((), ())),
-            preferred_element_type=jnp.float32,
-        )
-    grad_input = result.astype(jnp.bfloat16).reshape(series_n, time_n, width)
+    mid = lax.dynamic_slice_in_dim(dpre, taps[1], kept, 1)
+    part = input_grad(main_kernel, (dpre, mid, wide, cotangent), mid, {}, "main")
+    head, part = lax.optimization_barrier((dpre[:, :span, :], part))
+    ahead = passed_along(head, -1)
+    mid = lax.dynamic_slice_in_dim(
+        jnp.concatenate([dpre[:, kept:, :], ahead], 1), taps[1], span, 1
+    )
+    grad_input = input_grad(
+        tail_kernel, (dpre, mid, ahead, wide, cotangent, part), mid, {5: 0}, "tail"
+    )
     new_weight, new_moment_one, new_moment_two = adamw(
         weight, grad_shard, moment_one, second_moment_state
     )

time: 137 us -> 121 us (0.88)
  blocking collectives: 0 us -> 27.7 us
  starting transfers between devices: 55.5 us -> 29.6 us
  waiting for transfers between devices: 49.5 us -> 34.6 us
  matrix products: 8.45 us -> 0 us
  Pallas kernels: 4.35 us -> 12.5 us
  local copies, waits for them, and re-layouts: 10.6 us -> 5.86 us
  between operations: 4.11 us -> 5.49 us
    all_to_all x0 -> x1, blocking collectives: none -> 27.7 us  [body(): lax.all_to_all(piece, LINE, 0, 0)]
    all_to_all x3 -> x2, starting transfers between devices: 26.8 us -> 11.3 us  [gathered(): lax.all_to_all(jnp.broadcast_to(piece[None], (size,) + piece.shape), axes...]
    all_to_all x1, starting transfers between devices: 17.6 us -> 5.77 us  [reduce_grad(): plane = jnp.sum(lax.all_to_all(chunks, PLANE, 0, 0).astype(jnp.float32), 0)]
    all_to_all x3 -> x2, waiting for transfers between devices: 23.1 us -> 11.3 us  [gathered(): lax.all_to_all(jnp.broadcast_to(piece[None], (size,) + piece.shape), axes...]
    dot_general x3 -> x0, matrix products: 8.45 us -> none  [body(): lax.dot_general(moved.reshape(-1, width), wide[k * width:(k + 1) * width]...]
    pallas_call x1 -> x5, Pallas kernels: 4.35 us -> 12.5 us  [the longest x1 5.33 us: layer(): pl.pallas_call(layer_kernel, in_specs=[SCALAR] + [NEAR] * 5, out_specs=[A...]
    ppermute x2, waiting for transfers between devices: 4.46 us -> 0.01 us  [passed_along(): return lax.ppermute(array, TM, pairs)]
    slice x3 -> x2, local copies, waits for them, and re-layouts: 3.72 us -> 0.62 us  [the longest x1 0.58 us: body(): taps[1]]
  transfers between devices with their start and end apart: 9 -> 8, of which waited for: 8 -> 6; matrix products, arithmetic and copies ran while one was open for 11% -> 3% of each run, Pallas kernels for 0% -> 5%
where the time goes in v3:
time: 121 us; the launch traced here: 119 us
  waiting for transfers between devices  34.6 us (29%)
  starting transfers between devices  29.6 us (24%)
  blocking collectives  27.7 us (23%)
  Pallas kernels  12.5 us (10%)
  local copies, waits for them, and re-layouts  5.86 us (5%)
  between operations  5.49 us (5%)
  other arithmetic  3.59 us (3%)
    all_to_all x1, blocking collectives, body(): lax.all_to_all(piece, LINE, 0, 0)  27.7 us
    all_to_all x2, waiting for transfers between devices, gathered(): lax.all_to_all(jnp.broadcast_to(piece[None], (size,) + piece.shape), axes...  11.3 us
    all_to_all x2, starting transfers between devices, gathered(): lax.all_to_all(jnp.broadcast_to(piece[None], (size,) + piece.shape), axes...  11.3 us
    all_to_all x1, waiting for transfers between devices, reduce_grad(): plane = jnp.sum(lax.all_to_all(chunks, PLANE, 0, 0).astype(jnp.float32), 0)  11 us
    all_to_all x1, waiting for transfers between devices, reduce_grad(): piece = jnp.sum(lax.all_to_all(line, LINE, 0, 0), 0)  8.83 us
    all_to_all x1, starting transfers between devices, reduce_grad(): plane = jnp.sum(lax.all_to_all(chunks, PLANE, 0, 0).astype(jnp.float32), 0)  5.77 us
    pallas_call x1, Pallas kernels, layer(): pl.pallas_call(layer_kernel, in_specs=[SCALAR] + [NEAR] * 5, out_specs=[A...  5.33 us
    ppermute x2, starting transfers between devices, passed_along(): return lax.ppermute(array, TM, pairs)  4.92 us
  transfers between devices with their start and end apart: 8, of which 6 were waited for; matrix products, arithmetic and copies ran while one was open for 3% of the time, Pallas kernels for 5%

profile of v3, /device:TPU:6, one launch (start us, length us, event | category | flops | bytes accessed | tf_op | source)
XLA Modules:
  0.0 119.3 jit_solution(6505526548512728226)
XLA Ops:
  0.6 1.0 first.1
  1.6 0.0 copy-start.9
  1.6 0.0 copy-start.4
  1.7 3.6 %collective-permute-start = (bf16[2,128,512]{2,1,0:T(8,128)(2,1)S(1)}, bf16[2,128,512]{2,1,0:T(8,128)(2,1)S(1)}, u32[]{:S(2)}, u32[]{:S(2)}) collective-permute-start(bf16[2,128,512]{2,1,0:T(8,128)(2,1)S(1)} %get-tuple-element.23), channel_id=1, source_target_pairs={{0,32},{32,64},{64,96},{96,128},{128,160},{160,192},{192,224},{224... | collective-permute-start | bytes 786440 | tf_op jit(solution)/shard_map/ppermute | solution.py:20
  5.3 27.7 %all_to_all.25 = bf16[16,12,128]{2,1,0:T(8,128)(2,1)S(1)} all-to-all(bf16[16,12,128]{2,1,0:T(8,128)(2,1)S(1)} %get-tuple-element.22), channel_id=1, replica_groups=mesh['z_lo'=4,'y'=4,'z_hi'=4,'x'=4,'core'=2] {'z_hi','z_lo'}, dimensions={0} | all-to-all | bytes 98304 | tf_op jit(solution)/shard_map/all_to_all | solution.py:311
  33.0 0.0 collective-permute-done.early_hbm
  33.0 0.0 copy-start.5
  33.1 1.0 broadcast_in_dim.14
  34.1 7.1 %all-to-all-start.1 = ((bf16[16,192,128]{2,1,0:T(8,128)(2,1)}), bf16[16,192,128]{2,1,0:T(8,128)(2,1)S(1)}, u32[]{:S(2)}, u32[]{:S(2)}) async-start(bf16[16,192,128]{2,1,0:T(8,128)(2,1)} %broadcast_in_dim.14), calls=%async_computation.1 | async-start | bytes 1572864 | tf_op jit(solution)/shard_map/all_to_all | solution.py:25
  41.2 0.0 copy-done.9
  41.2 0.6 slice.11
  43.1 0.0 copy-done.4
  43.1 1.4 %fusion.mid_hbm = bf16[2,512,512]{2,1,0:T(8,128)(2,1)} fusion(s32[]{:T(128)S(6)} %select_n.9, bf16[2,128,512]{2,1,0:T(8,128)(2,1)S(1)} %collective-permute-done.early_hbm, bf16[2,512,512]{2,1,0:T(8,128)(2,1)S(1)} %copy-done.4), kind=kLoop, calls=%fused_computation.4 | loop fusion | flops 2097152 | bytes 2359300 | tf_op jit(solution)/shard_map/concatenate | solution.py:313
  44.5 0.0 copy-done.5
  44.5 7.2 %all-to-all-done.1.mine_ref = bf16[16,192,128]{2,1,0:T(8,128)(2,1)S(1)} async-done(((bf16[16,192,128]{2,1,0:T(8,128)(2,1)}), bf16[16,192,128]{2,1,0:T(8,128)(2,1)S(1)}, u32[]{:S(2)}, u32[]{:S(2)}) %all-to-all-start.1) | async-done | bytes 786464 | tf_op jit(solution)/shard_map/all_to_all | solution.py:25
  51.7 1.9 %collective-permute-start.1 = (bf16[16,192,128]{2,1,0:T(8,128)(2,1)S(1)}, bf16[16,192,128]{2,1,0:T(8,128)(2,1)S(1)}, u32[]{:S(2)}, u32[]{:S(2)}) collective-permute-start(bf16[16,192,128]{2,1,0:T(8,128)(2,1)S(1)} %all-to-all-done.1.mine_ref), channel_id=1, source_target_pairs={{0,1},{1,0},{2,3},{3,2},{4,5},{5,4},{6,7},{7,6},{8,9},{9,8},{10,11... | collective-permute-start | bytes 2359304 | tf_op jit(solution)/shard_map/ppermute | solution.py:29
  53.7 2.0 %ready.1 = (bf16[2,640,512]{2,1,0:T(8,128)(2,1)S(1)}, bf16[2,512,512]{2,1,0:T(8,128)(2,1)S(1)}, bf16[2,512,512]{2,1,0:T(8,128)(2,1)S(1)}) custom-call(bf16[2,512,512]{2,1,0:T(8,128)(2,1)} %in_hbm.3, bf16[2,128,512]{2,1,0:T(8,128)(2,1)} %copy-done.5, bf16[2,512,512]{2,1,0:T(8,128)(2,1)} %fusion.mid_hbm, bf16[2,512,512]{2,1,0:T(8,128)(2,1)} %up_ref.3), custom_call_target="tpu_custom_call" | custom-call | tf_op jit(solution)/shard_map/ready/pallas_call | solution.py:110
  55.7 0.3 collective-permute-done.1.other_ref
  55.9 5.3 %layer.1 = (bf16[2,512,512]{2,1,0:T(8,128)(2,1)}, bf16[1536,512]{1,0:T(8,128)(2,1)}, f32[16,192,128]{2,1,0:T(8,128)S(1)}, f32[16,192,128]{2,1,0:T(8,128)S(1)}) custom-call(s32[1]{0:T(128)} %bitcast.2.core_ref, bf16[16,192,128]{2,1,0:T(8,128)(2,1)S(1)} %all-to-all-done.1.mine_ref, bf16[16,192,128]{2,1,0:T(8,128)(2,1)S(1)} %collective-permute-done.1.other_ref, ...), custom_call_target="tpu_custom_call" | custom-call | tf_op jit(solution)/shard_map/layer/pallas_call | solution.py:202
  61.2 2.2 %collective-permute-start.2 = (f32[16,192,128]{2,1,0:T(8,128)S(1)}, f32[16,192,128]{2,1,0:T(8,128)S(1)}, u32[]{:S(2)}, u32[]{:S(2)}) collective-permute-start(f32[16,192,128]{2,1,0:T(8,128)S(1)} %get-tuple-element.35), channel_id=1, source_target_pairs={{0,1},{1,0},{2,3},{3,2},{4,5},{5,4},{6,7},{7,6},{8,9},{9,8},{10,11... | collective-permute-start | bytes 4718600 | tf_op jit(solution)/shard_map/ppermute | solution.py:29
  63.4 3.1 %collective-permute-done.2 = f32[16,192,128]{2,1,0:T(8,128)S(1)} collective-permute-done((f32[16,192,128]{2,1,0:T(8,128)S(1)}, f32[16,192,128]{2,1,0:T(8,128)S(1)}, u32[]{:S(2)}, u32[]{:S(2)}) %collective-permute-start.2) | collective-permute-done | bytes 1572896 | tf_op jit(solution)/shard_map/ppermute | solution.py:29
  66.6 1.1 add_convert_fusion
  67.6 0.0 copy-start
  67.6 5.8 %all-to-all-start.2 = ((bf16[16,192,128]{2,1,0:T(8,128)(2,1)}), bf16[16,192,128]{2,1,0:T(8,128)(2,1)S(1)}, u32[]{:S(2)}, u32[]{:S(2)}) async-start(bf16[16,192,128]{2,1,0:T(8,128)(2,1)} %add_convert_fusion), calls=%async_computation.2 | async-start | bytes 1572864 | tf_op jit(solution)/shard_map/all_to_all | solution.py:288
  73.4 0.0 copy-start.1
  75.4 11.0 %all-to-all-done.2 = bf16[16,192,128]{2,1,0:T(8,128)(2,1)S(1)} async-done(((bf16[16,192,128]{2,1,0:T(8,128)(2,1)}), bf16[16,192,128]{2,1,0:T(8,128)(2,1)S(1)}, u32[]{:S(2)}, u32[]{:S(2)}) %all-to-all-start.2) | async-done | bytes 786464 | tf_op jit(solution)/shard_map/all_to_all | solution.py:288
  86.5 0.1 convert_reduce_fusion
  86.6 0.7 reshape.27
  87.2 3.5 %all-to-all-start.3 = ((f32[16,12,128]{2,1,0:T(8,128)}), f32[16,12,128]{2,1,0:T(8,128)S(1)}, u32[]{:S(2)}, u32[]{:S(2)}) async-start(f32[16,12,128]{2,1,0:T(8,128)} %reshape.27), calls=%async_computation.3 | async-start | bytes 262144 | tf_op jit(solution)/shard_map/all_to_all | solution.py:290
  90.8 0.0 copy-done
  90.8 0.0 copy-start.2
  90.8 0.2 constant_dynamic-slice_fusion.mid_ref
  91.0 0.0 copy-done.1
  91.0 1.2 copy-done.2
  92.2 2.3 %main.1.part_hbm = bf16[2,512,512]{2,1,0:T(8,128)(2,1)} custom-call(bf16[2,512,512]{2,1,0:T(8,128)(2,1)S(1)} %copy-done, bf16[2,384,512]{2,1,0:T(8,128)(2,1)S(1)} %constant_dynamic-slice_fusion.mid_ref, bf16[1536,512]{1,0:T(8,128)(2,1)S(1)} %copy-done.2, bf16[2,512,512]{2,1,0:T(8,128)(2,1)S(1)} %copy-done.1), custom_call_target="tpu_custom_call" | custom-call | tf_op jit(solution)/shard_map/main/pallas_call | solution.py:272
  94.5 1.3 %collective-permute-start.3 = (bf16[2,128,512]{2,1,0:T(8,128)(2,1)S(1)}, bf16[2,128,512]{2,1,0:T(8,128)(2,1)S(1)}, u32[]{:S(2)}, u32[]{:S(2)}) collective-permute-start(bf16[2,128,512]{2,1,0:T(8,128)(2,1)S(1)} %get-tuple-element.38), channel_id=1, source_target_pairs={{32,0},{64,32},{96,64},{128,96},{160,128},{192,160},{224,192},{256... | collective-permute-start | bytes 786440 | tf_op jit(solution)/shard_map/ppermute | solution.py:20
  95.8 8.8 %all-to-all-done.3 = f32[16,12,128]{2,1,0:T(8,128)S(1)} async-done(((f32[16,12,128]{2,1,0:T(8,128)}), f32[16,12,128]{2,1,0:T(8,128)S(1)}, u32[]{:S(2)}, u32[]{:S(2)}) %all-to-all-start.3) | async-done | bytes 98336 | tf_op jit(solution)/shard_map/all_to_all | solution.py:290
  104.7 0.7 broadcast_in_dim.15
  105.4 4.2 %all-to-all-start.4 = ((f32[16,12,128]{2,1,0:T(8,128)}), f32[16,12,128]{2,1,0:T(8,128)S(1)}, u32[]{:S(2)}, u32[]{:S(2)}) async-start(f32[16,12,128]{2,1,0:T(8,128)} %broadcast_in_dim.15), calls=%async_computation.4 | async-start | bytes 262144 | tf_op jit(solution)/shard_map/all_to_all | solution.py:25
  110.8 0.0 collective-permute-done.3.ahead_ref
  110.8 0.2 fusion.1.mid_ref
  111.1 0.0 copy-start.3
  111.1 1.4 %copy-done.3 = bf16[1536,512]{1,0:T(8,128)(2,1)S(1)} copy-done((bf16[1536,512]{1,0:T(8,128)(2,1)S(1)}, bf16[1536,512]{1,0:T(8,128)(2,1)}, u32[]{:S(2)}) %copy-start.3) | copy-done | bytes 1572888
  112.5 0.0 copy-start.6
  112.5 0.0 copy-start.7
  112.5 0.0 copy-start.8
  112.5 1.9 %tail.1 = bf16[2,512,512]{2,1,0:T(8,128)(2,1)} custom-call(bf16[2,512,512]{2,1,0:T(8,128)(2,1)S(1)} %copy-done, bf16[2,128,512]{2,1,0:T(8,128)(2,1)S(1)} %fusion.1.mid_ref, bf16[2,128,512]{2,1,0:T(8,128)(2,1)S(1)} %collective-permute-done.3.ahead_ref, bf16[1536,512]{1,0:T(8,128)(2,1)S(1)} %copy-done.3, ...), custom_call_target="tpu_custom_call", output_to_operand_aliasing={{}: (5, {})} | custom-call | tf_op jit(solution)/shard_map/tail/pallas_call | solution.py:272
  114.4 4.1 %all-to-all-done.4 = f32[16,12,128]{2,1,0:T(8,128)S(1)} async-done(((f32[16,12,128]{2,1,0:T(8,128)}), f32[16,12,128]{2,1,0:T(8,128)S(1)}, u32[]{:S(2)}, u32[]{:S(2)}) %all-to-all-start.4) | async-done | bytes 98336 | tf_op jit(solution)/shard_map/all_to_all | solution.py:25
  118.5 0.0 copy-done.6
  118.5 0.0 copy-done.7
  118.5 0.0 copy-done.8
  118.6 0.7 multiply_subtract_fusion
  (5 shorter events, 0.1 us)
Async XLA Ops:
  1.6 39.6 %copy-start.9 = (s32[3]{0:T(128)S(1)}, s32[3]{0:T(128)}, u32[]{:S(2)}) copy-start(s32[3]{0:T(128)} %param.8) | copy-start | bytes 40
  1.6 41.4 %copy-start.4 = (bf16[2,512,512]{2,1,0:T(8,128)(2,1)S(1)}, bf16[2,512,512]{2,1,0:T(8,128)(2,1)}, u32[]{:S(2)}) copy-start(bf16[2,512,512]{2,1,0:T(8,128)(2,1)} %in_hbm.3) | copy-start | bytes 3145732
  1.7 31.4 %collective-permute-start = (bf16[2,128,512]{2,1,0:T(8,128)(2,1)S(1)}, bf16[2,128,512]{2,1,0:T(8,128)(2,1)S(1)}, u32[]{:S(2)}, u32[]{:S(2)}) collective-permute-start(bf16[2,128,512]{2,1,0:T(8,128)(2,1)S(1)} %get-tuple-element.23), channel_id=1, source_target_pairs={{0,32},{32,64},{64,96},{96,128},{128,160},{160,192},{192,224},{224... | collective-permute-start | bytes 786440 | tf_op jit(solution)/shard_map/ppermute | solution.py:20
  33.0 11.5 %copy-start.5 = (bf16[2,128,512]{2,1,0:T(8,128)(2,1)}, bf16[2,128,512]{2,1,0:T(8,128)(2,1)S(1)}, u32[]{:S(2)}) copy-start(bf16[2,128,512]{2,1,0:T(8,128)(2,1)S(1)} %collective-permute-done.early_hbm) | copy-start | bytes 786436
  34.1 17.7 %all-to-all-start.1 = ((bf16[16,192,128]{2,1,0:T(8,128)(2,1)}), bf16[16,192,128]{2,1,0:T(8,128)(2,1)S(1)}, u32[]{:S(2)}, u32[]{:S(2)}) async-start(bf16[16,192,128]{2,1,0:T(8,128)(2,1)} %broadcast_in_dim.14), calls=%async_computation.1 | async-start | bytes 1572864 | tf_op jit(solution)/shard_map/all_to_all | solution.py:25
  51.7 4.2 %collective-permute-start.1 = (bf16[16,192,128]{2,1,0:T(8,128)(2,1)S(1)}, bf16[16,192,128]{2,1,0:T(8,128)(2,1)S(1)}, u32[]{:S(2)}, u32[]{:S(2)}) collective-permute-start(bf16[16,192,128]{2,1,0:T(8,128)(2,1)S(1)} %all-to-all-done.1.mine_ref), channel_id=1, source_target_pairs={{0,1},{1,0},{2,3},{3,2},{4,5},{5,4},{6,7},{7,6},{8,9},{9,8},{10,11... | collective-permute-start | bytes 2359304 | tf_op jit(solution)/shard_map/ppermute | solution.py:29
  61.2 5.3 %collective-permute-start.2 = (f32[16,192,128]{2,1,0:T(8,128)S(1)}, f32[16,192,128]{2,1,0:T(8,128)S(1)}, u32[]{:S(2)}, u32[]{:S(2)}) collective-permute-start(f32[16,192,128]{2,1,0:T(8,128)S(1)} %get-tuple-element.35), channel_id=1, source_target_pairs={{0,1},{1,0},{2,3},{3,2},{4,5},{5,4},{6,7},{7,6},{8,9},{9,8},{10,11... | collective-permute-start | bytes 4718600 | tf_op jit(solution)/shard_map/ppermute | solution.py:29
  67.6 23.1 %copy-start = (bf16[2,512,512]{2,1,0:T(8,128)(2,1)S(1)}, bf16[2,512,512]{2,1,0:T(8,128)(2,1)}, u32[]{:S(2)}) copy-start(bf16[2,512,512]{2,1,0:T(8,128)(2,1)} %get-tuple-element.36.dpre_ref) | copy-start | bytes 3145732
  67.6 18.8 %all-to-all-start.2 = ((bf16[16,192,128]{2,1,0:T(8,128)(2,1)}), bf16[16,192,128]{2,1,0:T(8,128)(2,1)S(1)}, u32[]{:S(2)}, u32[]{:S(2)}) async-start(bf16[16,192,128]{2,1,0:T(8,128)(2,1)} %add_convert_fusion), calls=%async_computation.2 | async-start | bytes 1572864 | tf_op jit(solution)/shard_map/all_to_all | solution.py:288
  73.4 17.6 %copy-start.1 = (bf16[2,512,512]{2,1,0:T(8,128)(2,1)S(1)}, bf16[2,512,512]{2,1,0:T(8,128)(2,1)}, u32[]{:S(2)}) copy-start(bf16[2,512,512]{2,1,0:T(8,128)(2,1)} %up_ref.3) | copy-start | bytes 3145732
  87.2 17.4 %all-to-all-start.3 = ((f32[16,12,128]{2,1,0:T(8,128)}), f32[16,12,128]{2,1,0:T(8,128)S(1)}, u32[]{:S(2)}, u32[]{:S(2)}) async-start(f32[16,12,128]{2,1,0:T(8,128)} %reshape.27), calls=%async_computation.3 | async-start | bytes 262144 | tf_op jit(solution)/shard_map/all_to_all | solution.py:290
  90.8 1.4 %copy-start.2 = (bf16[1536,512]{1,0:T(8,128)(2,1)S(1)}, bf16[1536,512]{1,0:T(8,128)(2,1)}, u32[]{:S(2)}) copy-start(bf16[1536,512]{1,0:T(8,128)(2,1)} %get-tuple-element.37.wide_ref) | copy-start | bytes 4718596
  94.5 16.3 %collective-permute-start.3 = (bf16[2,128,512]{2,1,0:T(8,128)(2,1)S(1)}, bf16[2,128,512]{2,1,0:T(8,128)(2,1)S(1)}, u32[]{:S(2)}, u32[]{:S(2)}) collective-permute-start(bf16[2,128,512]{2,1,0:T(8,128)(2,1)S(1)} %get-tuple-element.38), channel_id=1, source_target_pairs={{32,0},{64,32},{96,64},{128,96},{160,128},{192,160},{224,192},{256... | collective-permute-start | bytes 786440 | tf_op jit(solution)/shard_map/ppermute | solution.py:20
  105.4 13.1 %all-to-all-start.4 = ((f32[16,12,128]{2,1,0:T(8,128)}), f32[16,12,128]{2,1,0:T(8,128)S(1)}, u32[]{:S(2)}, u32[]{:S(2)}) async-start(f32[16,12,128]{2,1,0:T(8,128)} %broadcast_in_dim.15), calls=%async_computation.4 | async-start | bytes 262144 | tf_op jit(solution)/shard_map/all_to_all | solution.py:25
  111.1 1.4 %copy-start.3 = (bf16[1536,512]{1,0:T(8,128)(2,1)S(1)}, bf16[1536,512]{1,0:T(8,128)(2,1)}, u32[]{:S(2)}) copy-start(bf16[1536,512]{1,0:T(8,128)(2,1)} %get-tuple-element.37.wide_ref) | copy-start | bytes 4718596
  112.5 6.0 %copy-start.6 = (f32[48,512]{1,0:T(8,128)S(1)}, f32[48,512]{1,0:T(8,128)}, u32[]{:S(2)}) copy-start(f32[48,512]{1,0:T(8,128)} %weight_hbm.1) | copy-start | bytes 294916
  112.5 6.0 %copy-start.7 = (f32[48,512]{1,0:T(8,128)S(1)}, f32[48,512]{1,0:T(8,128)}, u32[]{:S(2)}) copy-start(f32[48,512]{1,0:T(8,128)} %param.10) | copy-start | bytes 294916
  112.5 6.1 %copy-start.8 = (f32[48,512]{1,0:T(8,128)S(1)}, f32[48,512]{1,0:T(8,128)}, u32[]{:S(2)}) copy-start(f32[48,512]{1,0:T(8,128)} %param.11) | copy-start | bytes 294916

commit v4 on v3

v4 whole, which is shorter than its diff:
```python
import jax
import jax.numpy as jnp
from jax import lax
from jax.experimental import pallas as pl
from jax.experimental.pallas import tpu as pltpu
from jax.sharding import Mesh
from jax.sharding import PartitionSpec as P

DILATION_GAP = 64
TM = ("z_lo", "y")
SERIES = ("z_hi", "x", "core")
PLANE = ("x", "y")
LINE = ("z_hi", "z_lo")
BLOCK_ROWS = 48


def passed_along(array, by):
    size = lax.axis_size(TM)
    pairs = [(i, i + by) for i in range(size) if 0 <= i + by < size]
    return lax.ppermute(array, TM, pairs)


def gathered(piece, axes):
    size = lax.axis_size(axes)
    return lax.all_to_all(jnp.broadcast_to(piece[None], (size,) + piece.shape), axes, 0, 0)


def swapped(array):
    return lax.ppermute(array, "core", [(0, 1), (1, 0)])


def away(array):
    return pltpu.with_memory_space_constraint(array, pltpu.HBM)


COVER = pl.CostEstimate(flops=1 << 36, bytes_accessed=1 << 30, transcendentals=0)
NEAR = pl.BlockSpec(memory_space=pltpu.VMEM)
AWAY = pl.BlockSpec(memory_space=pltpu.HBM)
SCALAR = pl.BlockSpec(memory_space=pltpu.SMEM)


def limit(mebibytes):
    return pltpu.CompilerParams(vmem_limit_bytes=mebibytes * 1024 * 1024)


def first_kernel(place_ref, in_hbm, weight_hbm, last_ref, piece_ref, weight_ref, sems):
    copies, part, lanes = piece_ref.shape
    span = last_ref.shape[1]
    y = in_hbm.shape[2] // lanes
    z_lo = weight_ref.shape[0] // part
    place = place_ref[0]
    lane = pl.multiple_of((place % y) * lanes, lanes)
    fetch_weight = pltpu.make_async_copy(
        weight_hbm.at[:, pl.ds(lane, lanes)], weight_ref, sems.at[0]
    )
    fetch_last = pltpu.make_async_copy(
        in_hbm.at[:, in_hbm.shape[1] - span :, :], last_ref, sems.at[1]
    )
    fetch_weight.start()
    fetch_last.start()
    fetch_weight.wait()
    for i in range(z_lo):

        @pl.when(place // y == i)
        def _():
            piece = weight_ref[i * part : (i + 1) * part, :].astype(jnp.bfloat16)
            for n in range(copies):
                piece_ref[n] = piece

    fetch_last.wait()


def first(inputs, weight, span):
    rows, width = weight.shape
    z_hi, z_lo, y = lax.axis_size("z_hi"), lax.axis_size("z_lo"), lax.axis_size("y")
    place = lax.axis_index(TM).astype(jnp.int32).reshape(1)
    return pl.pallas_call(
        first_kernel,
        in_specs=[SCALAR, AWAY, AWAY],
        out_specs=[NEAR, NEAR],
        out_shape=[
            jax.ShapeDtypeStruct((inputs.shape[0], span, width), inputs.dtype),
            jax.ShapeDtypeStruct((z_hi * z_lo, rows // z_lo, width // y), jnp.bfloat16),
        ],
        scratch_shapes=[
            pltpu.VMEM((rows, width // y), jnp.float32),
            pltpu.SemaphoreType.DMA((2,)),
        ],
        compiler_params=limit(4),
        name="first",
    )(place, away(inputs), away(weight))


def spread_kernel(line_ref, out_ref, plane_ref):
    devices, part, _ = line_ref.shape
    for n in range(devices):
        plane_ref[n * part : (n + 1) * part, :] = line_ref[n]
    for n in range(out_ref.shape[0]):
        out_ref[n] = plane_ref[...]


def spread(line, copies):
    devices, part, lanes = line.shape
    return pl.pallas_call(
        spread_kernel,
        in_specs=[NEAR],
        out_specs=NEAR,
        out_shape=jax.ShapeDtypeStruct((copies, devices * part, lanes), line.dtype),
        scratch_shapes=[pltpu.VMEM((devices * part, lanes), line.dtype)],
        compiler_params=limit(4),
        name="spread",
    )(line)


def selector(shift, rows):
    at = lax.broadcasted_iota(jnp.int32, (rows, 2 * rows), 1)
    row = lax.broadcasted_iota(jnp.int32, (rows, 2 * rows), 0)
    return jnp.where(at == row + shift, 1.0, 0.0).astype(jnp.bfloat16)


def picked(choose, block):
    return jnp.dot(choose, block, preferred_element_type=jnp.float32).astype(jnp.bfloat16)


def ready_kernel(taps_ref, in_hbm, early_hbm, up_hbm, near_ref, mid_ref, up_ref, sems):
    series_n, time_n, _ = in_hbm.shape
    span = early_hbm.shape[1]
    copies = [
        pltpu.make_async_copy(early_hbm, near_ref.at[:, :span, :], sems.at[0]),
        pltpu.make_async_copy(in_hbm, near_ref.at[:, span:, :], sems.at[1]),
        pltpu.make_async_copy(up_hbm, up_ref, sems.at[2]),
    ]
    for c in copies:
        c.start()
    choose = selector(span - taps_ref[1], span)
    for c in copies[:2]:
        c.wait()
    for s in range(series_n):
        for m in range(0, time_n, span):
            mid_ref[s, m : m + span, :] = picked(choose, near_ref[s, m : m + 2 * span, :])
    copies[2].wait()


def ready(taps, inputs, early, up):
    series_n, time_n, width = inputs.shape
    long = (series_n, early.shape[1] + time_n, width)
    return pl.pallas_call(
        ready_kernel,
        in_specs=[SCALAR] + [AWAY] * 3,
        out_specs=[NEAR] * 3,
        out_shape=[
            jax.ShapeDtypeStruct(long, inputs.dtype),
            jax.ShapeDtypeStruct(inputs.shape, inputs.dtype),
            jax.ShapeDtypeStruct(up.shape, up.dtype),
        ],
        scratch_shapes=[pltpu.SemaphoreType.DMA((3,))],
        compiler_params=limit(8),
        name="ready",
    )(taps, away(inputs), away(early), away(up))


def layer_kernel(
    core_ref, mine_ref, other_ref, near_ref, mid_ref, up_ref,
    dpre_hbm, head_ref, wide_ref, keep_ref, give_ref, dpre_ref, acc_ref, sems,
):
    series_n, time_n, width = mid_ref.shape
    span = near_ref.shape[1] - time_n
    planes, line_rows, lanes = mine_ref.shape
    y = width // lanes
    x = planes // y
    rows = BLOCK_ROWS
    z_hi = line_rows // rows
    core = core_ref[0]

    def blocks():
        for h in range(z_hi):
            for i in range(x):
                for j in range(y):
                    yield h, (h * x + i) * 2 * rows, i * y + j, j * lanes

    own, far = core * rows, (1 - core) * rows
    for h, base, p, lane in blocks():
        here = pl.ds(pl.multiple_of(base + own, 16), rows)
        there = pl.ds(pl.multiple_of(base + far, 16), rows)
        wide_ref[here, lane : lane + lanes] = mine_ref[p, h * rows : (h + 1) * rows, :]
        wide_ref[there, lane : lane + lanes] = other_ref[p, h * rows : (h + 1) * rows, :]
    chunk = 128
    saves = []
    for s in range(series_n):
        for m in range(0, time_n, chunk):
            taken = (
                near_ref[s, span + m : span + m + chunk, :],
                mid_ref[s, m : m + chunk, :],
                near_ref[s, m : m + chunk, :],
            )
            pre = sum(
                jnp.dot(
                    t,
                    wide_ref[k * width : (k + 1) * width, :],
                    preferred_element_type=jnp.float32,
                )
                for k, t in enumerate(taken)
            )
            sig = jax.nn.sigmoid(pre)
            up = up_ref[s, m : m + chunk, :].astype(jnp.float32)
            dpre_ref[s, m : m + chunk, :] = (up * (sig * (1.0 + pre * (1.0 - sig)))).astype(
                jnp.bfloat16
            )
        head_ref[s] = dpre_ref[s, :span, :]
        saves.append(pltpu.make_async_copy(dpre_ref.at[s], dpre_hbm.at[s], sems.at[s]))
        saves[-1].start()
    for k in range(3):
        for s in range(series_n):
            taken = (near_ref[s, span:, :], mid_ref[s], near_ref[s, :time_n, :])[k]
            part = lax.dot_general(
                taken,
                dpre_ref[s],
                (((0,), (0,)), ((), ())),
                preferred_element_type=jnp.float32,
            )
            if s == 0:
                acc_ref[k * width : (k + 1) * width, :] = part
            else:
                acc_ref[k * width : (k + 1) * width, :] += part
    for h, base, p, lane in blocks():
        here = pl.ds(pl.multiple_of(base + own, 8), rows)
        there = pl.ds(pl.multiple_of(base + far, 8), rows)
        keep_ref[p, h * rows : (h + 1) * rows, :] = acc_ref[here, lane : lane + lanes]
        give_ref[p, h * rows : (h + 1) * rows, :] = acc_ref[there, lane : lane + lanes].astype(
            jnp.bfloat16
        )

    for c in saves:
        c.wait()

def layer(core, mine, other, near, mid, up):
    planes, line_rows, lanes = mine.shape
    width = up.shape[-1]
    total = 2 * planes * line_rows * lanes // width
    return pl.pallas_call(
        layer_kernel,
        in_specs=[SCALAR] + [NEAR] * 5,
        out_specs=[AWAY] + [NEAR] * 4,
        out_shape=[
            pltpu.HBM(up.shape, jnp.bfloat16),
            jax.ShapeDtypeStruct((up.shape[0], near.shape[1] - up.shape[1], width), jnp.bfloat16),
            jax.ShapeDtypeStruct((total, width), jnp.bfloat16),
            jax.ShapeDtypeStruct(mine.shape, jnp.float32),
            jax.ShapeDtypeStruct(mine.shape, jnp.bfloat16),
        ],
        scratch_shapes=[
            pltpu.VMEM(up.shape, jnp.bfloat16),
            pltpu.VMEM((total, width), jnp.float32),
            pltpu.SemaphoreType.DMA((up.shape[0],)),
        ],
        compiler_params=limit(16),
        name="layer",
    )(core, mine, other, near, mid, up)


def back_kernel(taps_ref, dpre_ref, ahead_ref, wide_ref, up_ref, out_hbm, out_ref, sems):
    series_n, time_n, width = dpre_ref.shape
    span = ahead_ref.shape[1]
    choose = selector(taps_ref[1], span)
    outs = []
    for s in range(series_n):
        later = jnp.concatenate([dpre_ref[s, span:, :], ahead_ref[s]], 0)
        mid = [
            picked(choose, dpre_ref[s, m : m + 2 * span, :]) for m in range(0, time_n - span, span)
        ]
        mid.append(picked(choose, later[time_n - 2 * span :, :]))
        result = up_ref[s].astype(jnp.float32)
        for k, rows in enumerate((dpre_ref[s], jnp.concatenate(mid, 0), later)):
            result = result + lax.dot_general(
                rows,
                wide_ref[k * width : (k + 1) * width, :],
                (((1,), (1,)), ((), ())),
                preferred_element_type=jnp.float32,
            )
        out_ref[s] = result.astype(jnp.bfloat16)
        outs.append(pltpu.make_async_copy(out_ref.at[s], out_hbm.at[s], sems.at[s]))
        outs[-1].start()
    for c in outs:
        c.wait()


def back(taps, dpre, ahead, wide, up):
    return pl.pallas_call(
        back_kernel,
        in_specs=[SCALAR] + [NEAR] * 4,
        out_specs=AWAY,
        out_shape=pltpu.HBM(dpre.shape, jnp.bfloat16),
        scratch_shapes=[
            pltpu.VMEM(dpre.shape, jnp.bfloat16),
            pltpu.SemaphoreType.DMA((dpre.shape[0],)),
        ],
        compiler_params=limit(8),
        cost_estimate=COVER,
        name="back",
    )(taps, dpre, ahead, wide, up)


def plane_sum(keep, given, rows):
    z_hi, z_lo = lax.axis_size("z_hi"), lax.axis_size("z_lo")
    chunks = (keep + given.astype(jnp.float32)).astype(jnp.bfloat16)
    plane = jnp.sum(lax.all_to_all(chunks, PLANE, 0, 0).astype(jnp.float32), 0)
    return plane.reshape(z_hi * z_lo, rows // z_lo, keep.shape[-1])


def rows_of(piece):
    z_lo, y = lax.axis_size("z_lo"), lax.axis_size("y")
    part, lanes = piece.shape
    pieces = gathered(piece, TM).reshape(z_lo, y, part, lanes)
    return pieces.transpose(0, 2, 1, 3).reshape(z_lo * part, y * lanes)


def adamw(weight, grad, moment_one, second_moment_state):
    first = 0.9 * moment_one + 0.1 * grad
    second = 0.999 * second_moment_state + 0.001 * grad * grad
    unbiased_one = first / (1.0 - 0.9**10)
    unbiased_two = second / (1.0 - 0.999**10)
    updated = weight - 0.01 * (unbiased_one / (jnp.sqrt(unbiased_two) + 1e-08) + 0.1 * weight)
    return (updated, first, second)


def body(inputs, cotangent, taps, weight, moment_one, second_moment_state):
    span = 2 * DILATION_GAP
    core = lax.axis_index("core").astype(jnp.int32).reshape(1)
    last, piece = first(inputs, weight, span)
    early = passed_along(last, 1)
    line, early, core = lax.optimization_barrier((lax.all_to_all(piece, LINE, 0, 0), early, core))
    copies = spread(line, lax.axis_size(PLANE))
    mine = lax.all_to_all(copies, PLANE, 0, 0)
    other = swapped(mine)
    mine, early = lax.optimization_barrier((mine, early))
    near, mid, up = ready(taps, inputs, early, cotangent)
    dpre, head, wide, keep, give = layer(core, mine, other, near, mid, up)
    given = swapped(give)
    ahead = passed_along(head, -1)
    grad_input = back(taps, dpre, ahead, wide, cotangent)
    line = plane_sum(keep, given, weight.shape[0])
    line, grad_input = lax.optimization_barrier((line, grad_input))
    piece = jnp.sum(lax.all_to_all(line, LINE, 0, 0), 0)
    grad_shard = rows_of(piece)
    new_weight, new_moment_one, new_moment_two = adamw(
        weight, grad_shard, moment_one, second_moment_state
    )
    return (grad_input, new_weight, new_moment_one, new_moment_two)


def solution(mesh):
    torus = Mesh(mesh.devices.reshape(4, 4, 4, 4, 2), TM + SERIES)
    tokens = P(SERIES, TM, None)
    rows = P(SERIES, None)
    return jax.shard_map(
        body,
        mesh=torus,
        in_specs=(tokens, tokens, P(), rows, rows, rows),
        out_specs=(tokens, rows, rows, rows),
        check_vma=False,
    )
```

time: 121 us -> 119 us (0.983)
  blocking collectives: 27.7 us -> 47.7 us
  waiting for transfers between devices: 34.6 us -> 21.3 us
  between operations: 5.49 us -> 0.83 us
  local copies, waits for them, and re-layouts: 5.86 us -> 1.33 us
  starting transfers between devices: 29.6 us -> 31.2 us
    all_to_all x1 -> x3, blocking collectives: 27.7 us -> 47.7 us  [the longest x1 18 us: body(): piece = jnp.sum(lax.all_to_all(line, LINE, 0, 0), 0)]
    all_to_all x4 -> x2, waiting for transfers between devices: 31.2 us -> 20.5 us  [the longest x1 12.7 us: body(): lax.all_to_all(piece, LINE, 0, 0)]
    ppermute x2, waiting for transfers between devices: 3.4 us -> 0.59 us  [swapped(): return lax.ppermute(array, 'core', [(0, 1), (1, 0)])]
    broadcast_in_dim x3 -> x1, local copies, waits for them, and re-layouts: 1.71 us -> 0.01 us  [gathered(): jnp.broadcast_to(piece[None], (size,) + piece.shape)]
    concatenate x2 -> x0, other arithmetic: 1.64 us -> none  [the longest x1 1.4 us: body(): jnp.concatenate([early, inputs], 1)]
    all_to_all x4 -> x2, starting transfers between devices: 20.6 us -> 22.1 us  [the longest x1 15.2 us: body(): lax.all_to_all(piece, LINE, 0, 0)]
    unnamed x20 -> x14, local copies, waits for them, and re-layouts: 2.63 us -> 1.26 us
  transfers between devices with their start and end apart: 8 -> 6, of which waited for: 6 -> 4; matrix products, arithmetic and copies ran while one was open for 3% -> 1% of each run, Pallas kernels for 5% -> 5%
where the time goes in v4:
time: 119 us; the launch traced here: 118 us
  blocking collectives  47.7 us (40%)
  starting transfers between devices  31.2 us (26%)
  waiting for transfers between devices  21.3 us (18%)
  Pallas kernels  12.3 us (10%)
  other arithmetic  3.13 us (3%)
  local copies, waits for them, and re-layouts  1.33 us (1%)
    all_to_all x1, blocking collectives, body(): piece = jnp.sum(lax.all_to_all(line, LINE, 0, 0), 0)  18 us
    all_to_all x1, blocking collectives, body(): mine = lax.all_to_all(copies, PLANE, 0, 0)  17.2 us
    all_to_all x1, starting transfers between devices, body(): lax.all_to_all(piece, LINE, 0, 0)  15.2 us
    all_to_all x1, waiting for transfers between devices, body(): lax.all_to_all(piece, LINE, 0, 0)  12.7 us
    all_to_all x1, blocking collectives, gathered(): lax.all_to_all(jnp.broadcast_to(piece[None], (size,) + piece.shape), axes...  12.5 us
    all_to_all x1, waiting for transfers between devices, plane_sum(): plane = jnp.sum(lax.all_to_all(chunks, PLANE, 0, 0).astype(jnp.float32), 0)  7.74 us
    all_to_all x1, starting transfers between devices, plane_sum(): plane = jnp.sum(lax.all_to_all(chunks, PLANE, 0, 0).astype(jnp.float32), 0)  6.85 us
    ppermute x2, starting transfers between devices, passed_along(): return lax.ppermute(array, TM, pairs)  4.79 us
  transfers between devices with their start and end apart: 6, of which 4 were waited for; matrix products, arithmetic and copies ran while one was open for 1% of the time, Pallas kernels for 5%

profile of v4, /device:TPU:6, one launch (start us, length us, event | category | flops | bytes accessed | tf_op | source)
XLA Modules:
  0.0 117.8 jit_solution(12443613062236064233)
XLA Ops:
  0.6 0.0 copy-start.1
  0.6 1.6 %first.1 = (bf16[2,128,512]{2,1,0:T(8,128)(2,1)S(1)}, bf16[16,12,128]{2,1,0:T(8,128)(2,1)}) custom-call(s32[1]{0:T(128)} %bitcast.place_ref, bf16[2,512,512]{2,1,0:T(8,128)(2,1)} %in_hbm.3, f32[48,512]{1,0:T(8,128)} %weight_hbm.1), custom_call_target="tpu_custom_call" | custom-call | tf_op jit(solution)/shard_map/first/pallas_call | solution.py:77
  2.3 3.5 %collective-permute-start = (bf16[2,128,512]{2,1,0:T(8,128)(2,1)S(1)}, bf16[2,128,512]{2,1,0:T(8,128)(2,1)S(1)}, u32[]{:S(2)}, u32[]{:S(2)}) collective-permute-start(bf16[2,128,512]{2,1,0:T(8,128)(2,1)S(1)} %get-tuple-element.22), channel_id=1, source_target_pairs={{0,32},{32,64},{64,96},{96,128},{128,160},{160,192},{192,224},{224... | collective-permute-start | bytes 786440 | tf_op jit(solution)/shard_map/ppermute | solution.py:20
  5.8 15.2 %all-to-all-start = ((bf16[16,12,128]{2,1,0:T(8,128)(2,1)}), bf16[16,12,128]{2,1,0:T(8,128)(2,1)S(1)}, u32[]{:S(2)}, u32[]{:S(2)}) async-start(bf16[16,12,128]{2,1,0:T(8,128)(2,1)} %get-tuple-element.21), calls=%async_computation | async-start | bytes 131072 | tf_op jit(solution)/shard_map/all_to_all | solution.py:331
  21.0 12.7 %all-to-all-done.line_ref = bf16[16,12,128]{2,1,0:T(8,128)(2,1)S(1)} async-done(((bf16[16,12,128]{2,1,0:T(8,128)(2,1)}), bf16[16,12,128]{2,1,0:T(8,128)(2,1)S(1)}, u32[]{:S(2)}, u32[]{:S(2)}) %all-to-all-start) | async-done | bytes 49184 | tf_op jit(solution)/shard_map/all_to_all | solution.py:331
  33.7 0.0 collective-permute-done.early_hbm
  33.7 0.0 copy-start.4
  33.7 0.1 spread.1
  33.9 17.2 %all_to_all.25.mine_ref = bf16[16,192,128]{2,1,0:T(8,128)(2,1)S(1)} all-to-all(bf16[16,192,128]{2,1,0:T(8,128)(2,1)S(1)} %spread.1), channel_id=1, replica_groups=mesh['z_lo'=4,'y'=4,'z_hi'=4,'x'=4,'core'=2] {'x','y'}, dimensions={0} | all-to-all | bytes 1572864 | tf_op jit(solution)/shard_map/all_to_all | solution.py:333
  51.1 1.9 %collective-permute-start.1 = (bf16[16,192,128]{2,1,0:T(8,128)(2,1)S(1)}, bf16[16,192,128]{2,1,0:T(8,128)(2,1)S(1)}, u32[]{:S(2)}, u32[]{:S(2)}) collective-permute-start(bf16[16,192,128]{2,1,0:T(8,128)(2,1)S(1)} %all_to_all.25.mine_ref), channel_id=1, source_target_pairs={{0,1},{1,0},{2,3},{3,2},{4,5},{5,4},{6,7},{7,6},{8,9},{9,8},{10,11... | collective-permute-start | bytes 2359304 | tf_op jit(solution)/shard_map/ppermute | solution.py:29
  53.0 0.0 copy-done.4
  53.0 0.0 copy-done.1
  53.0 2.3 %ready.1 = (bf16[2,640,512]{2,1,0:T(8,128)(2,1)S(1)}, bf16[2,512,512]{2,1,0:T(8,128)(2,1)S(1)}, bf16[2,512,512]{2,1,0:T(8,128)(2,1)S(1)}) custom-call(s32[3]{0:T(128)S(1)} %copy-done.1, bf16[2,512,512]{2,1,0:T(8,128)(2,1)} %in_hbm.3, bf16[2,128,512]{2,1,0:T(8,128)(2,1)} %copy-done.4, bf16[2,512,512]{2,1,0:T(8,128)(2,1)} %up_ref.1), custom_call_target="tpu_custom_call" | custom-call | tf_op jit(solution)/shard_map/ready/pallas_call | solution.py:147
  55.4 0.0 collective-permute-done.1.other_ref
  55.4 4.7 %layer.1 = (bf16[2,512,512]{2,1,0:T(8,128)(2,1)}, bf16[2,128,512]{2,1,0:T(8,128)(2,1)S(1)}, bf16[1536,512]{1,0:T(8,128)(2,1)S(1)}, f32[16,192,128]{2,1,0:T(8,128)S(1)}, bf16[16,192,128]{2,1,0:T(8,128)(2,1)S(1)}) custom-call(s32[1]{0:T(128)} %bitcast.1.core_ref, bf16[16,192,128]{2,1,0:T(8,128)(2,1)S(1)} %all_to_all.25.mine_ref, ...), custom_call_target="tpu_custom_call" | custom-call | tf_op jit(solution)/shard_map/layer/pallas_call | solution.py:240
  60.1 2.4 %collective-permute-start.2 = (bf16[16,192,128]{2,1,0:T(8,128)(2,1)S(1)}, bf16[16,192,128]{2,1,0:T(8,128)(2,1)S(1)}, u32[]{:S(2)}, u32[]{:S(2)}) collective-permute-start(bf16[16,192,128]{2,1,0:T(8,128)(2,1)S(1)} %get-tuple-element.32), channel_id=1, source_target_pairs={{0,1},{1,0},{2,3},{3,2},{4,5},{5,4},{6,7},{7,6},{8,9},{9,8},{10,11... | collective-permute-start | bytes 2359304 | tf_op jit(solution)/shard_map/ppermute | solution.py:29
  62.5 1.3 %collective-permute-start.3 = (bf16[2,128,512]{2,1,0:T(8,128)(2,1)S(1)}, bf16[2,128,512]{2,1,0:T(8,128)(2,1)S(1)}, u32[]{:S(2)}, u32[]{:S(2)}) collective-permute-start(bf16[2,128,512]{2,1,0:T(8,128)(2,1)S(1)} %get-tuple-element.34), channel_id=1, source_target_pairs={{32,0},{64,32},{96,64},{128,96},{160,128},{192,160},{224,192},{256... | collective-permute-start | bytes 786440 | tf_op jit(solution)/shard_map/ppermute | solution.py:20
  63.8 0.6 collective-permute-done.2
  64.4 1.1 add_convert_fusion
  65.5 0.0 copy-start
  65.5 6.9 %all-to-all-start.2 = ((bf16[16,192,128]{2,1,0:T(8,128)(2,1)}), bf16[16,192,128]{2,1,0:T(8,128)(2,1)}, u32[]{:S(2)}, u32[]{:S(2)}) async-start(bf16[16,192,128]{2,1,0:T(8,128)(2,1)} %add_convert_fusion), calls=%async_computation.2 | async-start | bytes 1572864 | tf_op jit(solution)/shard_map/all_to_all | solution.py:306
  72.4 0.3 collective-permute-done.3.ahead_ref
  72.6 0.0 copy-done
  72.6 0.0 copy-start.2
  72.6 1.2 %copy-done.2 = bf16[2,512,512]{2,1,0:T(8,128)(2,1)S(1)} copy-done((bf16[2,512,512]{2,1,0:T(8,128)(2,1)S(1)}, bf16[2,512,512]{2,1,0:T(8,128)(2,1)}, u32[]{:S(2)}) %copy-start.2) | copy-done | bytes 1048600
  73.9 3.5 %back.1 = bf16[2,512,512]{2,1,0:T(8,128)(2,1)} custom-call(s32[3]{0:T(128)S(1)} %copy-done.1, bf16[2,512,512]{2,1,0:T(8,128)(2,1)S(1)} %copy-done.2, bf16[2,128,512]{2,1,0:T(8,128)(2,1)S(1)} %collective-permute-done.3.ahead_ref, bf16[1536,512]{1,0:T(8,128)(2,1)S(1)} %get-tuple-element.35.wide_ref, bf16[2,512,512]{2,1,0:T(8,128)(2,1)S(1)} %copy-done), custom_call_target="tpu_custom_call" | custom-call | flops 68719476736 | bytes 1073741824 | tf_op jit(solution)/shard_map/back/pallas_call | solution.py:288
  77.4 0.0 copy-start.3
  77.4 0.0 copy-start.5
  77.4 0.0 copy-start.6
  77.4 7.7 %all-to-all-done.2 = bf16[16,192,128]{2,1,0:T(8,128)(2,1)} async-done(((bf16[16,192,128]{2,1,0:T(8,128)(2,1)}), bf16[16,192,128]{2,1,0:T(8,128)(2,1)}, u32[]{:S(2)}, u32[]{:S(2)}) %all-to-all-start.2) | async-done | bytes 786464 | tf_op jit(solution)/shard_map/all_to_all | solution.py:306
  85.2 1.2 %convert_reduce_fusion = f32[192,128]{1,0:T(8,128)S(1)} fusion(bf16[16,192,128]{2,1,0:T(8,128)(2,1)} %all-to-all-done.2), kind=kLoop, calls=%fused_computation | loop fusion | flops 761856 | bytes 884736 | tf_op jit(solution)/shard_map/reduce_sum | solution.py:306
  86.5 18.0 %all_to_all.26 = f32[16,12,128]{2,1,0:T(8,128)S(1)} all-to-all(f32[16,12,128]{2,1,0:T(8,128)S(1)} %reshape.26), channel_id=1, replica_groups=mesh['z_lo'=4,'y'=4,'z_hi'=4,'x'=4,'core'=2] {'z_hi','z_lo'}, dimensions={0} | all-to-all | bytes 196608 | tf_op jit(solution)/shard_map/all_to_all | solution.py:343
  104.5 12.5 %all_to_all.27 = f32[16,12,128]{2,1,0:T(8,128)S(1)} all-to-all(f32[16,12,128]{2,1,0:T(8,128)S(1)} %broadcast_in_dim.2), channel_id=1, replica_groups=mesh['z_lo'=4,'y'=4,'z_hi'=4,'x'=4,'core'=2] {'z_lo','y'}, dimensions={0} | all-to-all | bytes 196608 | tf_op jit(solution)/shard_map/all_to_all | solution.py:25
  117.1 0.0 copy-done.3
  117.1 0.0 copy-done.5
  117.1 0.0 copy-done.6
  117.1 0.7 multiply_subtract_fusion
  (5 shorter events, 0.1 us)
Async XLA Ops:
  0.6 52.4 %copy-start.1 = (s32[3]{0:T(128)S(1)}, s32[3]{0:T(128)}, u32[]{:S(2)}) copy-start(s32[3]{0:T(128)} %taps_ref.3) | copy-start | bytes 40
  2.3 31.5 %collective-permute-start = (bf16[2,128,512]{2,1,0:T(8,128)(2,1)S(1)}, bf16[2,128,512]{2,1,0:T(8,128)(2,1)S(1)}, u32[]{:S(2)}, u32[]{:S(2)}) collective-permute-start(bf16[2,128,512]{2,1,0:T(8,128)(2,1)S(1)} %get-tuple-element.22), channel_id=1, source_target_pairs={{0,32},{32,64},{64,96},{96,128},{128,160},{160,192},{192,224},{224... | collective-permute-start | bytes 786440 | tf_op jit(solution)/shard_map/ppermute | solution.py:20
  5.8 27.9 %all-to-all-start = ((bf16[16,12,128]{2,1,0:T(8,128)(2,1)}), bf16[16,12,128]{2,1,0:T(8,128)(2,1)S(1)}, u32[]{:S(2)}, u32[]{:S(2)}) async-start(bf16[16,12,128]{2,1,0:T(8,128)(2,1)} %get-tuple-element.21), calls=%async_computation | async-start | bytes 131072 | tf_op jit(solution)/shard_map/all_to_all | solution.py:331
  33.7 19.3 %copy-start.4 = (bf16[2,128,512]{2,1,0:T(8,128)(2,1)}, bf16[2,128,512]{2,1,0:T(8,128)(2,1)S(1)}, u32[]{:S(2)}) copy-start(bf16[2,128,512]{2,1,0:T(8,128)(2,1)S(1)} %collective-permute-done.early_hbm) | copy-start | bytes 786436
  51.1 4.3 %collective-permute-start.1 = (bf16[16,192,128]{2,1,0:T(8,128)(2,1)S(1)}, bf16[16,192,128]{2,1,0:T(8,128)(2,1)S(1)}, u32[]{:S(2)}, u32[]{:S(2)}) collective-permute-start(bf16[16,192,128]{2,1,0:T(8,128)(2,1)S(1)} %all_to_all.25.mine_ref), channel_id=1, source_target_pairs={{0,1},{1,0},{2,3},{3,2},{4,5},{5,4},{6,7},{7,6},{8,9},{9,8},{10,11... | collective-permute-start | bytes 2359304 | tf_op jit(solution)/shard_map/ppermute | solution.py:29
  60.1 4.3 %collective-permute-start.2 = (bf16[16,192,128]{2,1,0:T(8,128)(2,1)S(1)}, bf16[16,192,128]{2,1,0:T(8,128)(2,1)S(1)}, u32[]{:S(2)}, u32[]{:S(2)}) collective-permute-start(bf16[16,192,128]{2,1,0:T(8,128)(2,1)S(1)} %get-tuple-element.32), channel_id=1, source_target_pairs={{0,1},{1,0},{2,3},{3,2},{4,5},{5,4},{6,7},{7,6},{8,9},{9,8},{10,11... | collective-permute-start | bytes 2359304 | tf_op jit(solution)/shard_map/ppermute | solution.py:29
  62.5 10.1 %collective-permute-start.3 = (bf16[2,128,512]{2,1,0:T(8,128)(2,1)S(1)}, bf16[2,128,512]{2,1,0:T(8,128)(2,1)S(1)}, u32[]{:S(2)}, u32[]{:S(2)}) collective-permute-start(bf16[2,128,512]{2,1,0:T(8,128)(2,1)S(1)} %get-tuple-element.34), channel_id=1, source_target_pairs={{32,0},{64,32},{96,64},{128,96},{160,128},{192,160},{224,192},{256... | collective-permute-start | bytes 786440 | tf_op jit(solution)/shard_map/ppermute | solution.py:20
  65.5 7.1 %copy-start = (bf16[2,512,512]{2,1,0:T(8,128)(2,1)S(1)}, bf16[2,512,512]{2,1,0:T(8,128)(2,1)}, u32[]{:S(2)}) copy-start(bf16[2,512,512]{2,1,0:T(8,128)(2,1)} %up_ref.1) | copy-start | bytes 3145732
  65.5 19.7 %all-to-all-start.2 = ((bf16[16,192,128]{2,1,0:T(8,128)(2,1)}), bf16[16,192,128]{2,1,0:T(8,128)(2,1)}, u32[]{:S(2)}, u32[]{:S(2)}) async-start(bf16[16,192,128]{2,1,0:T(8,128)(2,1)} %add_convert_fusion), calls=%async_computation.2 | async-start | bytes 1572864 | tf_op jit(solution)/shard_map/all_to_all | solution.py:306
  72.6 1.2 %copy-start.2 = (bf16[2,512,512]{2,1,0:T(8,128)(2,1)S(1)}, bf16[2,512,512]{2,1,0:T(8,128)(2,1)}, u32[]{:S(2)}) copy-start(bf16[2,512,512]{2,1,0:T(8,128)(2,1)} %get-tuple-element.33.dpre_ref) | copy-start | bytes 3145732
  77.4 39.7 %copy-start.3 = (f32[48,512]{1,0:T(8,128)S(1)}, f32[48,512]{1,0:T(8,128)}, u32[]{:S(2)}) copy-start(f32[48,512]{1,0:T(8,128)} %weight_hbm.1) | copy-start | bytes 294916
  77.4 39.7 %copy-start.5 = (f32[48,512]{1,0:T(8,128)S(1)}, f32[48,512]{1,0:T(8,128)}, u32[]{:S(2)}) copy-start(f32[48,512]{1,0:T(8,128)} %param.10) | copy-start | bytes 294916
  77.4 39.7 %copy-start.6 = (f32[48,512]{1,0:T(8,128)S(1)}, f32[48,512]{1,0:T(8,128)}, u32[]{:S(2)}) copy-start(f32[48,512]{1,0:T(8,128)} %param.11) | copy-start | bytes 294916

commit v5 on v4

--- a/solution.py
+++ b/solution.py
@@ -108,6 +108,7 @@
         out_shape=jax.ShapeDtypeStruct((copies, devices * part, lanes), line.dtype),
         scratch_shapes=[pltpu.VMEM((devices * part, lanes), line.dtype)],
         compiler_params=limit(4),
+        cost_estimate=COVER,
         name="spread",
     )(line)
 
@@ -122,41 +123,71 @@
     return jnp.dot(choose, block, preferred_element_type=jnp.float32).astype(jnp.bfloat16)
 
 
-def ready_kernel(taps_ref, in_hbm, early_hbm, up_hbm, near_ref, mid_ref, up_ref, sems):
+def middle_kernel(taps_ref, in_hbm, early_ref, mid_hbm, near_ref, mid_ref, sems):
     series_n, time_n, _ = in_hbm.shape
+    span = early_ref.shape[1]
+    fetch = pltpu.make_async_copy(in_hbm, near_ref.at[:, span:, :], sems.at[0])
+    fetch.start()
+    near_ref[:, :span, :] = early_ref[...]
+    choose = selector(span - taps_ref[1], span)
+    fetch.wait()
+    for s in range(series_n):
+        for m in range(0, time_n, span):
+            mid_ref[s, m : m + span, :] = picked(choose, near_ref[s, m : m + 2 * span, :])
+    out = pltpu.make_async_copy(mid_ref, mid_hbm, sems.at[1])
+    out.start()
+    out.wait()
+
+
+def middle(taps, inputs, early):
+    series_n, time_n, width = inputs.shape
+    long = (series_n, early.shape[1] + time_n, width)
+    return pl.pallas_call(
+        middle_kernel,
+        in_specs=[SCALAR, AWAY, NEAR],
+        out_specs=AWAY,
+        out_shape=pltpu.HBM(inputs.shape, inputs.dtype),
+        scratch_shapes=[
+            pltpu.VMEM(long, inputs.dtype),
+            pltpu.VMEM(inputs.shape, inputs.dtype),
+            pltpu.SemaphoreType.DMA((2,)),
+        ],
+        compiler_params=limit(8),
+        cost_estimate=COVER,
+        name="middle",
+    )(taps, away(inputs), early)
+
+
+def ready_kernel(in_hbm, early_hbm, mid_hbm, up_hbm, near_ref, mid_ref, up_ref, sems):
     span = early_hbm.shape[1]
     copies = [
         pltpu.make_async_copy(early_hbm, near_ref.at[:, :span, :], sems.at[0]),
         pltpu.make_async_copy(in_hbm, near_ref.at[:, span:, :], sems.at[1]),
-        pltpu.make_async_copy(up_hbm, up_ref, sems.at[2]),
+        pltpu.make_async_copy(mid_hbm, mid_ref, sems.at[2]),
+        pltpu.make_async_copy(up_hbm, up_ref, sems.at[3]),
     ]
     for c in copies:
         c.start()
-    choose = selector(span - taps_ref[1], span)
-    for c in copies[:2]:
+    for c in copies:
         c.wait()
-    for s in range(series_n):
-        for m in range(0, time_n, span):
-            mid_ref[s, m : m + span, :] = picked(choose, near_ref[s, m : m + 2 * span, :])
-    copies[2].wait()
-
-
-def ready(taps, inputs, early, up):
+
+
+def ready(inputs, early, mid, up):
     series_n, time_n, width = inputs.shape
     long = (series_n, early.shape[1] + time_n, width)
     return pl.pallas_call(
         ready_kernel,
-        in_specs=[SCALAR] + [AWAY] * 3,
+        in_specs=[AWAY] * 4,
         out_specs=[NEAR] * 3,
         out_shape=[
             jax.ShapeDtypeStruct(long, inputs.dtype),
             jax.ShapeDtypeStruct(inputs.shape, inputs.dtype),
             jax.ShapeDtypeStruct(up.shape, up.dtype),
         ],
-        scratch_shapes=[pltpu.SemaphoreType.DMA((3,))],
+        scratch_shapes=[pltpu.SemaphoreType.DMA((4,))],
         compiler_params=limit(8),
         name="ready",
-    )(taps, away(inputs), away(early), away(up))
+    )(away(inputs), away(early), away(mid), away(up))
 
 
 def layer_kernel(
@@ -300,11 +331,32 @@
     )(taps, dpre, ahead, wide, up)
 
 
-def plane_sum(keep, given, rows):
-    z_hi, z_lo = lax.axis_size("z_hi"), lax.axis_size("z_lo")
+def fold_kernel(chunks_ref, line_ref, sum_ref):
+    devices, part, _ = line_ref.shape
+    total = chunks_ref[0].astype(jnp.float32)
+    for n in range(1, chunks_ref.shape[0]):
+        total = total + chunks_ref[n].astype(jnp.float32)
+    sum_ref[...] = total
+    for n in range(devices):
+        line_ref[n] = sum_ref[n * part : (n + 1) * part, :]
+
+
+def fold(chunks, devices):
+    _, rows, lanes = chunks.shape
+    return pl.pallas_call(
+        fold_kernel,
+        in_specs=[NEAR],
+        out_specs=NEAR,
+        out_shape=jax.ShapeDtypeStruct((devices, rows // devices, lanes), jnp.float32),
+        scratch_shapes=[pltpu.VMEM((rows, lanes), jnp.float32)],
+        compiler_params=limit(4),
+        name="fold",
+    )(chunks)
+
+
+def plane_sum(keep, given):
     chunks = (keep + given.astype(jnp.float32)).astype(jnp.bfloat16)
-    plane = jnp.sum(lax.all_to_all(chunks, PLANE, 0, 0).astype(jnp.float32), 0)
-    return plane.reshape(z_hi * z_lo, rows // z_lo, keep.shape[-1])
+    return fold(lax.all_to_all(chunks, PLANE, 0, 0), lax.axis_size(LINE))
 
 
 def rows_of(piece):
@@ -327,18 +379,19 @@
     span = 2 * DILATION_GAP
     core = lax.axis_index("core").astype(jnp.int32).reshape(1)
     last, piece = first(inputs, weight, span)
+    line = lax.all_to_all(piece, LINE, 0, 0)
     early = passed_along(last, 1)
-    line, early, core = lax.optimization_barrier((lax.all_to_all(piece, LINE, 0, 0), early, core))
-    copies = spread(line, lax.axis_size(PLANE))
+    copies, core = lax.optimization_barrier((spread(line, lax.axis_size(PLANE)), core))
     mine = lax.all_to_all(copies, PLANE, 0, 0)
+    mid = middle(taps, inputs, early)
+    mine, early, mid = lax.optimization_barrier((mine, early, mid))
     other = swapped(mine)
-    mine, early = lax.optimization_barrier((mine, early))
-    near, mid, up = ready(taps, inputs, early, cotangent)
+    near, mid, up = ready(inputs, early, mid, cotangent)
     dpre, head, wide, keep, give = layer(core, mine, other, near, mid, up)
     given = swapped(give)
     ahead = passed_along(head, -1)
     grad_input = back(taps, dpre, ahead, wide, cotangent)
-    line = plane_sum(keep, given, weight.shape[0])
+    line = plane_sum(keep, given)
     line, grad_input = lax.optimization_barrier((line, grad_input))
     piece = jnp.sum(lax.all_to_all(line, LINE, 0, 0), 0)
     grad_shard = rows_of(piece)

time: 119 us -> 116 us (0.975)
  blocking collectives: 47.7 us -> 30.5 us
  starting transfers between devices: 31.2 us -> 38.3 us
  Pallas kernels: 12.3 us -> 17.3 us
  waiting for transfers between devices: 21.3 us -> 24.8 us
  other arithmetic: 3.13 us -> 1.86 us
    all_to_all x1 -> x0, blocking collectives: 17.2 us -> none  [body(): mine = lax.all_to_all(copies, PLANE, 0, 0)]
    all_to_all x2 -> x3, starting transfers between devices: 22.1 us -> 29.5 us  [the longest x1 15.2 us: body(): line = lax.all_to_all(piece, LINE, 0, 0)]
    pallas_call x1 -> x3, Pallas kernels: 2.33 us -> 5.3 us  [the longest x1 3.2 us: middle(): pl.pallas_call(middle_kernel, in_specs=[SCALAR, AWAY, NEAR], out_specs=AW...]
    all_to_all x2 -> x3, waiting for transfers between devices: 20.5 us -> 22.9 us  [the longest x1 9.22 us: body(): line = lax.all_to_all(piece, LINE, 0, 0)]
    reduce_sum x1 -> x0, other arithmetic: 1.25 us -> none  [plane_sum(): plane = jnp.sum(lax.all_to_all(chunks, PLANE, 0, 0).astype(jnp.float32), 0)]
  transfers between devices with their start and end apart: 6 -> 7, of which waited for: 4 -> 6; matrix products, arithmetic and copies ran while one was open for 1% -> 1% of each run, Pallas kernels for 5% -> 9%
where the time goes in v5:
time: 116 us; the launch traced here: 115 us
  starting transfers between devices  38.3 us (33%)
  blocking collectives  30.5 us (26%)
  waiting for transfers between devices  24.8 us (21%)
  Pallas kernels  17.3 us (15%)
  other arithmetic  1.86 us (2%)
  local copies, waits for them, and re-layouts  1.32 us (1%)
    all_to_all x1, blocking collectives, body(): piece = jnp.sum(lax.all_to_all(line, LINE, 0, 0), 0)  18.2 us
    all_to_all x1, starting transfers between devices, body(): line = lax.all_to_all(piece, LINE, 0, 0)  15.2 us
    all_to_all x1, blocking collectives, gathered(): lax.all_to_all(jnp.broadcast_to(piece[None], (size,) + piece.shape), axes...  12.3 us
    all_to_all x1, waiting for transfers between devices, body(): line = lax.all_to_all(piece, LINE, 0, 0)  9.22 us
    all_to_all x1, starting transfers between devices, body(): mine = lax.all_to_all(copies, PLANE, 0, 0)  7.63 us
    all_to_all x1, waiting for transfers between devices, body(): mine = lax.all_to_all(copies, PLANE, 0, 0)  7.49 us
    all_to_all x1, starting transfers between devices, plane_sum(): return fold(lax.all_to_all(chunks, PLANE, 0, 0), lax.axis_size(LINE))  6.64 us
    all_to_all x1, waiting for transfers between devices, plane_sum(): return fold(lax.all_to_all(chunks, PLANE, 0, 0), lax.axis_size(LINE))  6.21 us
  transfers between devices with their start and end apart: 7, of which 6 were waited for; matrix products, arithmetic and copies ran while one was open for 1% of the time, Pallas kernels for 9%

profile of v5, /device:TPU:6, one launch (start us, length us, event | category | flops | bytes accessed | tf_op | source)
XLA Modules:
  0.0 114.9 jit_solution(5162682592007864038)
XLA Ops:
  0.6 1.6 %first.1 = (bf16[2,128,512]{2,1,0:T(8,128)(2,1)S(1)}, bf16[16,12,128]{2,1,0:T(8,128)(2,1)}) custom-call(s32[1]{0:T(128)} %bitcast.place_ref, bf16[2,512,512]{2,1,0:T(8,128)(2,1)} %in_hbm.5, f32[48,512]{1,0:T(8,128)} %weight_hbm.1), custom_call_target="tpu_custom_call" | custom-call | tf_op jit(solution)/shard_map/first/pallas_call | solution.py:77
  2.3 15.2 %all-to-all-start = ((bf16[16,12,128]{2,1,0:T(8,128)(2,1)}), bf16[16,12,128]{2,1,0:T(8,128)(2,1)S(1)}, u32[]{:S(2)}, u32[]{:S(2)}) async-start(bf16[16,12,128]{2,1,0:T(8,128)(2,1)} %get-tuple-element.21), calls=%async_computation | async-start | bytes 131072 | tf_op jit(solution)/shard_map/all_to_all | solution.py:382
  17.5 3.5 %collective-permute-start = (bf16[2,128,512]{2,1,0:T(8,128)(2,1)S(1)}, bf16[2,128,512]{2,1,0:T(8,128)(2,1)S(1)}, u32[]{:S(2)}, u32[]{:S(2)}) collective-permute-start(bf16[2,128,512]{2,1,0:T(8,128)(2,1)S(1)} %get-tuple-element.24), channel_id=1, source_target_pairs={{0,32},{32,64},{64,96},{96,128},{128,160},{160,192},{192,224},{224... | collective-permute-start | bytes 786440 | tf_op jit(solution)/shard_map/ppermute | solution.py:20
  21.0 9.2 %all-to-all-done.line_ref = bf16[16,12,128]{2,1,0:T(8,128)(2,1)S(1)} async-done(((bf16[16,12,128]{2,1,0:T(8,128)(2,1)}), bf16[16,12,128]{2,1,0:T(8,128)(2,1)S(1)}, u32[]{:S(2)}, u32[]{:S(2)}) %all-to-all-start) | async-done | bytes 49184 | tf_op jit(solution)/shard_map/all_to_all | solution.py:382
  30.2 1.0 spread.1
  31.2 0.0 copy-start.3
  31.2 7.6 %all-to-all-start.1 = ((bf16[16,192,128]{2,1,0:T(8,128)(2,1)}), bf16[16,192,128]{2,1,0:T(8,128)(2,1)S(1)}, u32[]{:S(2)}, u32[]{:S(2)}) async-start(bf16[16,192,128]{2,1,0:T(8,128)(2,1)} %spread.1), calls=%async_computation.1 | async-start | bytes 1572864 | tf_op jit(solution)/shard_map/all_to_all | solution.py:385
  38.9 0.0 collective-permute-done.early_ref.early_hbm
  38.9 0.0 copy-done.3
  38.9 0.0 copy-start.1
  38.9 3.2 %middle.1.mid_hbm = bf16[2,512,512]{2,1,0:T(8,128)(2,1)} custom-call(s32[3]{0:T(128)S(1)} %copy-done.3, bf16[2,512,512]{2,1,0:T(8,128)(2,1)} %in_hbm.5, bf16[2,128,512]{2,1,0:T(8,128)(2,1)S(1)} %collective-permute-done.early_ref.early_hbm), custom_call_target="tpu_custom_call" | custom-call | flops 68719476736 | bytes 1073741824 | tf_op jit(solution)/shard_map/middle/pallas_call | solution.py:145
  42.1 0.0 copy-done.1
  42.1 7.5 %all-to-all-done.1.mine_ref = bf16[16,192,128]{2,1,0:T(8,128)(2,1)S(1)} async-done(((bf16[16,192,128]{2,1,0:T(8,128)(2,1)}), bf16[16,192,128]{2,1,0:T(8,128)(2,1)S(1)}, u32[]{:S(2)}, u32[]{:S(2)}) %all-to-all-start.1) | async-done | bytes 786464 | tf_op jit(solution)/shard_map/all_to_all | solution.py:385
  49.6 1.9 %collective-permute-start.1 = (bf16[16,192,128]{2,1,0:T(8,128)(2,1)S(1)}, bf16[16,192,128]{2,1,0:T(8,128)(2,1)S(1)}, u32[]{:S(2)}, u32[]{:S(2)}) collective-permute-start(bf16[16,192,128]{2,1,0:T(8,128)(2,1)S(1)} %all-to-all-done.1.mine_ref), channel_id=1, source_target_pairs={{0,1},{1,0},{2,3},{3,2},{4,5},{5,4},{6,7},{7,6},{8,9},{9,8},{10,11... | collective-permute-start | bytes 2359304 | tf_op jit(solution)/shard_map/ppermute | solution.py:29
  51.5 2.0 %ready.1 = (bf16[2,640,512]{2,1,0:T(8,128)(2,1)S(1)}, bf16[2,512,512]{2,1,0:T(8,128)(2,1)S(1)}, bf16[2,512,512]{2,1,0:T(8,128)(2,1)S(1)}) custom-call(bf16[2,512,512]{2,1,0:T(8,128)(2,1)} %in_hbm.5, bf16[2,128,512]{2,1,0:T(8,128)(2,1)} %copy-done.1, bf16[2,512,512]{2,1,0:T(8,128)(2,1)} %middle.1.mid_hbm, bf16[2,512,512]{2,1,0:T(8,128)(2,1)} %up_ref.1), custom_call_target="tpu_custom_call" | custom-call | tf_op jit(solution)/shard_map/ready/pallas_call | solution.py:178
  53.5 0.3 collective-permute-done.1.other_ref
  53.8 5.4 %layer.1 = (bf16[2,512,512]{2,1,0:T(8,128)(2,1)}, bf16[2,128,512]{2,1,0:T(8,128)(2,1)}, bf16[1536,512]{1,0:T(8,128)(2,1)S(1)}, f32[16,192,128]{2,1,0:T(8,128)S(1)}, bf16[16,192,128]{2,1,0:T(8,128)(2,1)S(1)}) custom-call(s32[1]{0:T(128)} %bitcast.1.core_ref, bf16[16,192,128]{2,1,0:T(8,128)(2,1)S(1)} %all-to-all-done.1.mine_ref, ...), custom_call_target="tpu_custom_call" | custom-call | tf_op jit(solution)/shard_map/layer/pallas_call | solution.py:271
  59.1 2.2 %collective-permute-start.2 = (bf16[16,192,128]{2,1,0:T(8,128)(2,1)S(1)}, bf16[16,192,128]{2,1,0:T(8,128)(2,1)S(1)}, u32[]{:S(2)}, u32[]{:S(2)}) collective-permute-start(bf16[16,192,128]{2,1,0:T(8,128)(2,1)S(1)} %get-tuple-element.32), channel_id=1, source_target_pairs={{0,1},{1,0},{2,3},{3,2},{4,5},{5,4},{6,7},{7,6},{8,9},{9,8},{10,11... | collective-permute-start | bytes 2359304 | tf_op jit(solution)/shard_map/ppermute | solution.py:29
  61.3 1.3 %collective-permute-start.3 = (bf16[2,128,512]{2,1,0:T(8,128)(2,1)}, bf16[2,128,512]{2,1,0:T(8,128)(2,1)}, u32[]{:S(2)}, u32[]{:S(2)}) collective-permute-start(bf16[2,128,512]{2,1,0:T(8,128)(2,1)} %get-tuple-element.34), channel_id=1, source_target_pairs={{32,0},{64,32},{96,64},{128,96},{160,128},{192,160},{224,192},{256... | collective-permute-start | bytes 786440 | tf_op jit(solution)/shard_map/ppermute | solution.py:20
  62.6 0.7 collective-permute-done.2
  63.3 1.1 add_convert_fusion
  64.4 0.0 copy-start
  64.4 6.6 %all-to-all-start.2 = ((bf16[16,192,128]{2,1,0:T(8,128)(2,1)}), bf16[16,192,128]{2,1,0:T(8,128)(2,1)S(1)}, u32[]{:S(2)}, u32[]{:S(2)}) async-start(bf16[16,192,128]{2,1,0:T(8,128)(2,1)} %add_convert_fusion), calls=%async_computation.2 | async-start | bytes 1572864 | tf_op jit(solution)/shard_map/all_to_all | solution.py:359
  71.0 0.9 collective-permute-done.3.ahead_ref
  72.0 0.0 copy-done
  72.0 0.0 copy-start.2
  72.0 1.2 %copy-done.2 = bf16[2,512,512]{2,1,0:T(8,128)(2,1)S(1)} copy-done((bf16[2,512,512]{2,1,0:T(8,128)(2,1)S(1)}, bf16[2,512,512]{2,1,0:T(8,128)(2,1)}, u32[]{:S(2)}) %copy-start.2) | copy-done | bytes 1048600
  73.2 4.0 %back.1 = bf16[2,512,512]{2,1,0:T(8,128)(2,1)} custom-call(s32[3]{0:T(128)S(1)} %copy-done.3, bf16[2,512,512]{2,1,0:T(8,128)(2,1)S(1)} %copy-done.2, bf16[2,128,512]{2,1,0:T(8,128)(2,1)} %collective-permute-done.3.ahead_ref, bf16[1536,512]{1,0:T(8,128)(2,1)S(1)} %get-tuple-element.35.wide_ref, bf16[2,512,512]{2,1,0:T(8,128)(2,1)S(1)} %copy-done), custom_call_target="tpu_custom_call" | custom-call | flops 68719476736 | bytes 1073741824 | tf_op jit(solution)/shard_map/back/pallas_call | solution.py:319
  77.2 0.0 copy-start.4
  77.2 0.0 copy-start.5
  77.2 0.0 copy-start.6
  77.2 6.2 %all-to-all-done.2.chunks_ref = bf16[16,192,128]{2,1,0:T(8,128)(2,1)S(1)} async-done(((bf16[16,192,128]{2,1,0:T(8,128)(2,1)}), bf16[16,192,128]{2,1,0:T(8,128)(2,1)S(1)}, u32[]{:S(2)}, u32[]{:S(2)}) %all-to-all-start.2) | async-done | bytes 786464 | tf_op jit(solution)/shard_map/all_to_all | solution.py:359
  83.4 0.1 fold.1
  83.6 18.2 %all_to_all.25 = f32[16,12,128]{2,1,0:T(8,128)S(1)} all-to-all(f32[16,12,128]{2,1,0:T(8,128)S(1)} %fold.1), channel_id=1, replica_groups=mesh['z_lo'=4,'y'=4,'z_hi'=4,'x'=4,'core'=2] {'z_hi','z_lo'}, dimensions={0} | all-to-all | bytes 196608 | tf_op jit(solution)/shard_map/all_to_all | solution.py:396
  101.8 12.3 %all_to_all.26 = f32[16,12,128]{2,1,0:T(8,128)S(1)} all-to-all(f32[16,12,128]{2,1,0:T(8,128)S(1)} %broadcast_in_dim.2), channel_id=1, replica_groups=mesh['z_lo'=4,'y'=4,'z_hi'=4,'x'=4,'core'=2] {'z_lo','y'}, dimensions={0} | all-to-all | bytes 196608 | tf_op jit(solution)/shard_map/all_to_all | solution.py:25
  114.2 0.0 copy-done.4
  114.2 0.0 copy-done.5
  114.2 0.0 copy-done.6
  114.2 0.7 multiply_subtract_fusion
  (4 shorter events, 0.1 us)
Async XLA Ops:
  2.3 27.9 %all-to-all-start = ((bf16[16,12,128]{2,1,0:T(8,128)(2,1)}), bf16[16,12,128]{2,1,0:T(8,128)(2,1)S(1)}, u32[]{:S(2)}, u32[]{:S(2)}) async-start(bf16[16,12,128]{2,1,0:T(8,128)(2,1)} %get-tuple-element.21), calls=%async_computation | async-start | bytes 131072 | tf_op jit(solution)/shard_map/all_to_all | solution.py:382
  17.5 21.4 %collective-permute-start = (bf16[2,128,512]{2,1,0:T(8,128)(2,1)S(1)}, bf16[2,128,512]{2,1,0:T(8,128)(2,1)S(1)}, u32[]{:S(2)}, u32[]{:S(2)}) collective-permute-start(bf16[2,128,512]{2,1,0:T(8,128)(2,1)S(1)} %get-tuple-element.24), channel_id=1, source_target_pairs={{0,32},{32,64},{64,96},{96,128},{128,160},{160,192},{192,224},{224... | collective-permute-start | bytes 786440 | tf_op jit(solution)/shard_map/ppermute | solution.py:20
  31.2 7.6 %copy-start.3 = (s32[3]{0:T(128)S(1)}, s32[3]{0:T(128)}, u32[]{:S(2)}) copy-start(s32[3]{0:T(128)} %taps_ref.3) | copy-start | bytes 40
  31.2 18.4 %all-to-all-start.1 = ((bf16[16,192,128]{2,1,0:T(8,128)(2,1)}), bf16[16,192,128]{2,1,0:T(8,128)(2,1)S(1)}, u32[]{:S(2)}, u32[]{:S(2)}) async-start(bf16[16,192,128]{2,1,0:T(8,128)(2,1)} %spread.1), calls=%async_computation.1 | async-start | bytes 1572864 | tf_op jit(solution)/shard_map/all_to_all | solution.py:385
  38.9 3.2 %copy-start.1 = (bf16[2,128,512]{2,1,0:T(8,128)(2,1)}, bf16[2,128,512]{2,1,0:T(8,128)(2,1)S(1)}, u32[]{:S(2)}) copy-start(bf16[2,128,512]{2,1,0:T(8,128)(2,1)S(1)} %collective-permute-done.early_ref.early_hbm) | copy-start | bytes 786436
  49.6 4.2 %collective-permute-start.1 = (bf16[16,192,128]{2,1,0:T(8,128)(2,1)S(1)}, bf16[16,192,128]{2,1,0:T(8,128)(2,1)S(1)}, u32[]{:S(2)}, u32[]{:S(2)}) collective-permute-start(bf16[16,192,128]{2,1,0:T(8,128)(2,1)S(1)} %all-to-all-done.1.mine_ref), channel_id=1, source_target_pairs={{0,1},{1,0},{2,3},{3,2},{4,5},{5,4},{6,7},{7,6},{8,9},{9,8},{10,11... | collective-permute-start | bytes 2359304 | tf_op jit(solution)/shard_map/ppermute | solution.py:29
  59.1 4.2 %collective-permute-start.2 = (bf16[16,192,128]{2,1,0:T(8,128)(2,1)S(1)}, bf16[16,192,128]{2,1,0:T(8,128)(2,1)S(1)}, u32[]{:S(2)}, u32[]{:S(2)}) collective-permute-start(bf16[16,192,128]{2,1,0:T(8,128)(2,1)S(1)} %get-tuple-element.32), channel_id=1, source_target_pairs={{0,1},{1,0},{2,3},{3,2},{4,5},{5,4},{6,7},{7,6},{8,9},{9,8},{10,11... | collective-permute-start | bytes 2359304 | tf_op jit(solution)/shard_map/ppermute | solution.py:29
  61.3 10.7 %collective-permute-start.3 = (bf16[2,128,512]{2,1,0:T(8,128)(2,1)}, bf16[2,128,512]{2,1,0:T(8,128)(2,1)}, u32[]{:S(2)}, u32[]{:S(2)}) collective-permute-start(bf16[2,128,512]{2,1,0:T(8,128)(2,1)} %get-tuple-element.34), channel_id=1, source_target_pairs={{32,0},{64,32},{96,64},{128,96},{160,128},{192,160},{224,192},{256... | collective-permute-start | bytes 786440 | tf_op jit(solution)/shard_map/ppermute | solution.py:20
  64.4 7.6 %copy-start = (bf16[2,512,512]{2,1,0:T(8,128)(2,1)S(1)}, bf16[2,512,512]{2,1,0:T(8,128)(2,1)}, u32[]{:S(2)}) copy-start(bf16[2,512,512]{2,1,0:T(8,128)(2,1)} %up_ref.1) | copy-start | bytes 3145732
  64.4 19.0 %all-to-all-start.2 = ((bf16[16,192,128]{2,1,0:T(8,128)(2,1)}), bf16[16,192,128]{2,1,0:T(8,128)(2,1)S(1)}, u32[]{:S(2)}, u32[]{:S(2)}) async-start(bf16[16,192,128]{2,1,0:T(8,128)(2,1)} %add_convert_fusion), calls=%async_computation.2 | async-start | bytes 1572864 | tf_op jit(solution)/shard_map/all_to_all | solution.py:359
  72.0 1.2 %copy-start.2 = (bf16[2,512,512]{2,1,0:T(8,128)(2,1)S(1)}, bf16[2,512,512]{2,1,0:T(8,128)(2,1)}, u32[]{:S(2)}) copy-start(bf16[2,512,512]{2,1,0:T(8,128)(2,1)} %get-tuple-element.33.dpre_ref) | copy-start | bytes 3145732
  77.2 37.0 %copy-start.4 = (f32[48,512]{1,0:T(8,128)S(1)}, f32[48,512]{1,0:T(8,128)}, u32[]{:S(2)}) copy-start(f32[48,512]{1,0:T(8,128)} %weight_hbm.1) | copy-start | bytes 294916
  77.2 37.0 %copy-start.5 = (f32[48,512]{1,0:T(8,128)S(1)}, f32[48,512]{1,0:T(8,128)}, u32[]{:S(2)}) copy-start(f32[48,512]{1,0:T(8,128)} %param.10) | copy-start | bytes 294916
  77.2 37.0 %copy-start.6 = (f32[48,512]{1,0:T(8,128)S(1)}, f32[48,512]{1,0:T(8,128)}, u32[]{:S(2)}) copy-start(f32[48,512]{1,0:T(8,128)} %param.11) | copy-start | bytes 294916

commit v6 on v5

--- a/solution.py
+++ b/solution.py
@@ -192,7 +192,7 @@
 
 def layer_kernel(
     core_ref, mine_ref, other_ref, near_ref, mid_ref, up_ref,
-    dpre_hbm, head_ref, wide_ref, keep_ref, give_ref, dpre_ref, acc_ref, sems,
+    dpre_hbm, head_hbm, wide_ref, keep_ref, give_ref, dpre_ref, acc_ref, sems,
 ):
     series_n, time_n, width = mid_ref.shape
     span = near_ref.shape[1] - time_n
@@ -237,9 +237,12 @@
             dpre_ref[s, m : m + chunk, :] = (up * (sig * (1.0 + pre * (1.0 - sig)))).astype(
                 jnp.bfloat16
             )
-        head_ref[s] = dpre_ref[s, :span, :]
-        saves.append(pltpu.make_async_copy(dpre_ref.at[s], dpre_hbm.at[s], sems.at[s]))
-        saves[-1].start()
+        for c in (
+            pltpu.make_async_copy(dpre_ref.at[s], dpre_hbm.at[s], sems.at[2 * s]),
+            pltpu.make_async_copy(dpre_ref.at[s, :span, :], head_hbm.at[s], sems.at[2 * s + 1]),
+        ):
+            c.start()
+            saves.append(c)
     for k in range(3):
         for s in range(series_n):
             taken = (near_ref[s, span:, :], mid_ref[s], near_ref[s, :time_n, :])[k]
@@ -271,10 +274,10 @@
     return pl.pallas_call(
         layer_kernel,
         in_specs=[SCALAR] + [NEAR] * 5,
-        out_specs=[AWAY] + [NEAR] * 4,
+        out_specs=[AWAY] * 2 + [NEAR] * 3,
         out_shape=[
             pltpu.HBM(up.shape, jnp.bfloat16),
-            jax.ShapeDtypeStruct((up.shape[0], near.shape[1] - up.shape[1], width), jnp.bfloat16),
+            pltpu.HBM((up.shape[0], near.shape[1] - up.shape[1], width), jnp.bfloat16),
             jax.ShapeDtypeStruct((total, width), jnp.bfloat16),
             jax.ShapeDtypeStruct(mine.shape, jnp.float32),
             jax.ShapeDtypeStruct(mine.shape, jnp.bfloat16),
@@ -282,7 +285,7 @@
         scratch_shapes=[
             pltpu.VMEM(up.shape, jnp.bfloat16),
             pltpu.VMEM((total, width), jnp.float32),
-            pltpu.SemaphoreType.DMA((up.shape[0],)),
+            pltpu.SemaphoreType.DMA((2 * up.shape[0],)),
         ],
         compiler_params=limit(16),
         name="layer",

time: 116 us -> 116 us (level)
  no operation moved by 1% of the time
where the time goes in v6:
time: 116 us; the launch traced here: 114 us
  starting transfers between devices  38.3 us (33%)
  blocking collectives  30.5 us (26%)
  waiting for transfers between devices  24.8 us (21%)
  Pallas kernels  16.6 us (14%)
  other arithmetic  1.86 us (2%)
  local copies, waits for them, and re-layouts  1.32 us (1%)
    all_to_all x1, blocking collectives, body(): piece = jnp.sum(lax.all_to_all(line, LINE, 0, 0), 0)  18.3 us
    all_to_all x1, starting transfers between devices, body(): line = lax.all_to_all(piece, LINE, 0, 0)  15.2 us
    all_to_all x1, blocking collectives, gathered(): lax.all_to_all(jnp.broadcast_to(piece[None], (size,) + piece.shape), axes...  12.3 us
    all_to_all x1, waiting for transfers between devices, body(): line = lax.all_to_all(piece, LINE, 0, 0)  9.22 us
    all_to_all x1, starting transfers between devices, body(): mine = lax.all_to_all(copies, PLANE, 0, 0)  7.63 us
    all_to_all x1, waiting for transfers between devices, body(): mine = lax.all_to_all(copies, PLANE, 0, 0)  7.49 us
    all_to_all x1, starting transfers between devices, plane_sum(): return fold(lax.all_to_all(chunks, PLANE, 0, 0), lax.axis_size(LINE))  6.65 us
    all_to_all x1, waiting for transfers between devices, plane_sum(): return fold(lax.all_to_all(chunks, PLANE, 0, 0), lax.axis_size(LINE))  6.2 us
  transfers between devices with their start and end apart: 7, of which 6 were waited for; matrix products, arithmetic and copies ran while one was open for 1% of the time, Pallas kernels for 9%

profile of v6, /device:TPU:6, one launch (start us, length us, event | category | flops | bytes accessed | tf_op | source)
XLA Modules:
  0.0 114.3 jit_solution(8050328922125525889)
XLA Ops:
  0.6 1.6 %first.1 = (bf16[2,128,512]{2,1,0:T(8,128)(2,1)S(1)}, bf16[16,12,128]{2,1,0:T(8,128)(2,1)}) custom-call(s32[1]{0:T(128)} %bitcast.place_ref, bf16[2,512,512]{2,1,0:T(8,128)(2,1)} %in_hbm.5, f32[48,512]{1,0:T(8,128)} %weight_hbm.1), custom_call_target="tpu_custom_call" | custom-call | tf_op jit(solution)/shard_map/first/pallas_call | solution.py:77
  2.3 15.2 %all-to-all-start = ((bf16[16,12,128]{2,1,0:T(8,128)(2,1)}), bf16[16,12,128]{2,1,0:T(8,128)(2,1)S(1)}, u32[]{:S(2)}, u32[]{:S(2)}) async-start(bf16[16,12,128]{2,1,0:T(8,128)(2,1)} %get-tuple-element.21), calls=%async_computation | async-start | bytes 131072 | tf_op jit(solution)/shard_map/all_to_all | solution.py:385
  17.5 3.5 %collective-permute-start = (bf16[2,128,512]{2,1,0:T(8,128)(2,1)S(1)}, bf16[2,128,512]{2,1,0:T(8,128)(2,1)S(1)}, u32[]{:S(2)}, u32[]{:S(2)}) collective-permute-start(bf16[2,128,512]{2,1,0:T(8,128)(2,1)S(1)} %get-tuple-element.24), channel_id=1, source_target_pairs={{0,32},{32,64},{64,96},{96,128},{128,160},{160,192},{192,224},{224... | collective-permute-start | bytes 786440 | tf_op jit(solution)/shard_map/ppermute | solution.py:20
  21.0 9.2 %all-to-all-done.line_ref = bf16[16,12,128]{2,1,0:T(8,128)(2,1)S(1)} async-done(((bf16[16,12,128]{2,1,0:T(8,128)(2,1)}), bf16[16,12,128]{2,1,0:T(8,128)(2,1)S(1)}, u32[]{:S(2)}, u32[]{:S(2)}) %all-to-all-start) | async-done | bytes 49184 | tf_op jit(solution)/shard_map/all_to_all | solution.py:385
  30.2 1.0 spread.1
  31.2 0.0 copy-start.3
  31.2 7.6 %all-to-all-start.1 = ((bf16[16,192,128]{2,1,0:T(8,128)(2,1)}), bf16[16,192,128]{2,1,0:T(8,128)(2,1)S(1)}, u32[]{:S(2)}, u32[]{:S(2)}) async-start(bf16[16,192,128]{2,1,0:T(8,128)(2,1)} %spread.1), calls=%async_computation.1 | async-start | bytes 1572864 | tf_op jit(solution)/shard_map/all_to_all | solution.py:388
  38.9 0.0 collective-permute-done.early_ref.early_hbm
  38.9 0.0 copy-done.3
  38.9 0.0 copy-start.1
  38.9 3.2 %middle.1.mid_hbm = bf16[2,512,512]{2,1,0:T(8,128)(2,1)} custom-call(s32[3]{0:T(128)S(1)} %copy-done.3, bf16[2,512,512]{2,1,0:T(8,128)(2,1)} %in_hbm.5, bf16[2,128,512]{2,1,0:T(8,128)(2,1)S(1)} %collective-permute-done.early_ref.early_hbm), custom_call_target="tpu_custom_call" | custom-call | flops 68719476736 | bytes 1073741824 | tf_op jit(solution)/shard_map/middle/pallas_call | solution.py:145
  42.1 0.0 copy-done.1
  42.1 7.5 %all-to-all-done.1.mine_ref = bf16[16,192,128]{2,1,0:T(8,128)(2,1)S(1)} async-done(((bf16[16,192,128]{2,1,0:T(8,128)(2,1)}), bf16[16,192,128]{2,1,0:T(8,128)(2,1)S(1)}, u32[]{:S(2)}, u32[]{:S(2)}) %all-to-all-start.1) | async-done | bytes 786464 | tf_op jit(solution)/shard_map/all_to_all | solution.py:388
  49.6 1.9 %collective-permute-start.1 = (bf16[16,192,128]{2,1,0:T(8,128)(2,1)S(1)}, bf16[16,192,128]{2,1,0:T(8,128)(2,1)S(1)}, u32[]{:S(2)}, u32[]{:S(2)}) collective-permute-start(bf16[16,192,128]{2,1,0:T(8,128)(2,1)S(1)} %all-to-all-done.1.mine_ref), channel_id=1, source_target_pairs={{0,1},{1,0},{2,3},{3,2},{4,5},{5,4},{6,7},{7,6},{8,9},{9,8},{10,11... | collective-permute-start | bytes 2359304 | tf_op jit(solution)/shard_map/ppermute | solution.py:29
  51.5 2.0 %ready.1 = (bf16[2,640,512]{2,1,0:T(8,128)(2,1)S(1)}, bf16[2,512,512]{2,1,0:T(8,128)(2,1)S(1)}, bf16[2,512,512]{2,1,0:T(8,128)(2,1)S(1)}) custom-call(bf16[2,512,512]{2,1,0:T(8,128)(2,1)} %in_hbm.5, bf16[2,128,512]{2,1,0:T(8,128)(2,1)} %copy-done.1, bf16[2,512,512]{2,1,0:T(8,128)(2,1)} %middle.1.mid_hbm, bf16[2,512,512]{2,1,0:T(8,128)(2,1)} %up_ref.1), custom_call_target="tpu_custom_call" | custom-call | tf_op jit(solution)/shard_map/ready/pallas_call | solution.py:178
  53.5 0.3 collective-permute-done.1.other_ref
  53.8 4.7 %layer.1 = (bf16[2,512,512]{2,1,0:T(8,128)(2,1)}, bf16[2,128,512]{2,1,0:T(8,128)(2,1)}, bf16[1536,512]{1,0:T(8,128)(2,1)S(1)}, f32[16,192,128]{2,1,0:T(8,128)S(1)}, bf16[16,192,128]{2,1,0:T(8,128)(2,1)S(1)}) custom-call(s32[1]{0:T(128)} %bitcast.1.core_ref, bf16[16,192,128]{2,1,0:T(8,128)(2,1)S(1)} %all-to-all-done.1.mine_ref, ...), custom_call_target="tpu_custom_call" | custom-call | tf_op jit(solution)/shard_map/layer/pallas_call | solution.py:274
  58.5 2.2 %collective-permute-start.2 = (bf16[16,192,128]{2,1,0:T(8,128)(2,1)S(1)}, bf16[16,192,128]{2,1,0:T(8,128)(2,1)S(1)}, u32[]{:S(2)}, u32[]{:S(2)}) collective-permute-start(bf16[16,192,128]{2,1,0:T(8,128)(2,1)S(1)} %get-tuple-element.32), channel_id=1, source_target_pairs={{0,1},{1,0},{2,3},{3,2},{4,5},{5,4},{6,7},{7,6},{8,9},{9,8},{10,11... | collective-permute-start | bytes 2359304 | tf_op jit(solution)/shard_map/ppermute | solution.py:29
  60.6 1.3 %collective-permute-start.3 = (bf16[2,128,512]{2,1,0:T(8,128)(2,1)}, bf16[2,128,512]{2,1,0:T(8,128)(2,1)}, u32[]{:S(2)}, u32[]{:S(2)}) collective-permute-start(bf16[2,128,512]{2,1,0:T(8,128)(2,1)} %get-tuple-element.34), channel_id=1, source_target_pairs={{32,0},{64,32},{96,64},{128,96},{160,128},{192,160},{224,192},{256... | collective-permute-start | bytes 786440 | tf_op jit(solution)/shard_map/ppermute | solution.py:20
  61.9 0.7 collective-permute-done.2
  62.6 1.1 add_convert_fusion
  63.7 0.0 copy-start
  63.7 6.6 %all-to-all-start.2 = ((bf16[16,192,128]{2,1,0:T(8,128)(2,1)}), bf16[16,192,128]{2,1,0:T(8,128)(2,1)S(1)}, u32[]{:S(2)}, u32[]{:S(2)}) async-start(bf16[16,192,128]{2,1,0:T(8,128)(2,1)} %add_convert_fusion), calls=%async_computation.2 | async-start | bytes 1572864 | tf_op jit(solution)/shard_map/all_to_all | solution.py:362
  70.4 0.9 collective-permute-done.3.ahead_ref
  71.3 0.0 copy-done
  71.3 0.0 copy-start.2
  71.3 1.2 %copy-done.2 = bf16[2,512,512]{2,1,0:T(8,128)(2,1)S(1)} copy-done((bf16[2,512,512]{2,1,0:T(8,128)(2,1)S(1)}, bf16[2,512,512]{2,1,0:T(8,128)(2,1)}, u32[]{:S(2)}) %copy-start.2) | copy-done | bytes 1048600
  72.5 4.0 %back.1 = bf16[2,512,512]{2,1,0:T(8,128)(2,1)} custom-call(s32[3]{0:T(128)S(1)} %copy-done.3, bf16[2,512,512]{2,1,0:T(8,128)(2,1)S(1)} %copy-done.2, bf16[2,128,512]{2,1,0:T(8,128)(2,1)} %collective-permute-done.3.ahead_ref, bf16[1536,512]{1,0:T(8,128)(2,1)S(1)} %get-tuple-element.35.wide_ref, bf16[2,512,512]{2,1,0:T(8,128)(2,1)S(1)} %copy-done), custom_call_target="tpu_custom_call" | custom-call | flops 68719476736 | bytes 1073741824 | tf_op jit(solution)/shard_map/back/pallas_call | solution.py:322
  76.5 0.0 copy-start.4
  76.5 0.0 copy-start.5
  76.5 0.0 copy-start.6
  76.6 6.2 %all-to-all-done.2.chunks_ref = bf16[16,192,128]{2,1,0:T(8,128)(2,1)S(1)} async-done(((bf16[16,192,128]{2,1,0:T(8,128)(2,1)}), bf16[16,192,128]{2,1,0:T(8,128)(2,1)S(1)}, u32[]{:S(2)}, u32[]{:S(2)}) %all-to-all-start.2) | async-done | bytes 786464 | tf_op jit(solution)/shard_map/all_to_all | solution.py:362
  82.8 0.1 fold.1
  82.9 18.3 %all_to_all.25 = f32[16,12,128]{2,1,0:T(8,128)S(1)} all-to-all(f32[16,12,128]{2,1,0:T(8,128)S(1)} %fold.1), channel_id=1, replica_groups=mesh['z_lo'=4,'y'=4,'z_hi'=4,'x'=4,'core'=2] {'z_hi','z_lo'}, dimensions={0} | all-to-all | bytes 196608 | tf_op jit(solution)/shard_map/all_to_all | solution.py:399
  101.2 12.3 %all_to_all.26 = f32[16,12,128]{2,1,0:T(8,128)S(1)} all-to-all(f32[16,12,128]{2,1,0:T(8,128)S(1)} %broadcast_in_dim.2), channel_id=1, replica_groups=mesh['z_lo'=4,'y'=4,'z_hi'=4,'x'=4,'core'=2] {'z_lo','y'}, dimensions={0} | all-to-all | bytes 196608 | tf_op jit(solution)/shard_map/all_to_all | solution.py:25
  113.5 0.0 copy-done.4
  113.5 0.0 copy-done.5
  113.5 0.0 copy-done.6
  113.5 0.7 multiply_subtract_fusion
  (4 shorter events, 0.1 us)
Async XLA Ops:
  2.3 27.9 %all-to-all-start = ((bf16[16,12,128]{2,1,0:T(8,128)(2,1)}), bf16[16,12,128]{2,1,0:T(8,128)(2,1)S(1)}, u32[]{:S(2)}, u32[]{:S(2)}) async-start(bf16[16,12,128]{2,1,0:T(8,128)(2,1)} %get-tuple-element.21), calls=%async_computation | async-start | bytes 131072 | tf_op jit(solution)/shard_map/all_to_all | solution.py:385
  17.5 21.4 %collective-permute-start = (bf16[2,128,512]{2,1,0:T(8,128)(2,1)S(1)}, bf16[2,128,512]{2,1,0:T(8,128)(2,1)S(1)}, u32[]{:S(2)}, u32[]{:S(2)}) collective-permute-start(bf16[2,128,512]{2,1,0:T(8,128)(2,1)S(1)} %get-tuple-element.24), channel_id=1, source_target_pairs={{0,32},{32,64},{64,96},{96,128},{128,160},{160,192},{192,224},{224... | collective-permute-start | bytes 786440 | tf_op jit(solution)/shard_map/ppermute | solution.py:20
  31.2 7.6 %copy-start.3 = (s32[3]{0:T(128)S(1)}, s32[3]{0:T(128)}, u32[]{:S(2)}) copy-start(s32[3]{0:T(128)} %taps_ref.3) | copy-start | bytes 40
  31.2 18.4 %all-to-all-start.1 = ((bf16[16,192,128]{2,1,0:T(8,128)(2,1)}), bf16[16,192,128]{2,1,0:T(8,128)(2,1)S(1)}, u32[]{:S(2)}, u32[]{:S(2)}) async-start(bf16[16,192,128]{2,1,0:T(8,128)(2,1)} %spread.1), calls=%async_computation.1 | async-start | bytes 1572864 | tf_op jit(solution)/shard_map/all_to_all | solution.py:388
  38.9 3.2 %copy-start.1 = (bf16[2,128,512]{2,1,0:T(8,128)(2,1)}, bf16[2,128,512]{2,1,0:T(8,128)(2,1)S(1)}, u32[]{:S(2)}) copy-start(bf16[2,128,512]{2,1,0:T(8,128)(2,1)S(1)} %collective-permute-done.early_ref.early_hbm) | copy-start | bytes 786436
  49.6 4.2 %collective-permute-start.1 = (bf16[16,192,128]{2,1,0:T(8,128)(2,1)S(1)}, bf16[16,192,128]{2,1,0:T(8,128)(2,1)S(1)}, u32[]{:S(2)}, u32[]{:S(2)}) collective-permute-start(bf16[16,192,128]{2,1,0:T(8,128)(2,1)S(1)} %all-to-all-done.1.mine_ref), channel_id=1, source_target_pairs={{0,1},{1,0},{2,3},{3,2},{4,5},{5,4},{6,7},{7,6},{8,9},{9,8},{10,11... | collective-permute-start | bytes 2359304 | tf_op jit(solution)/shard_map/ppermute | solution.py:29
  58.5 4.2 %collective-permute-start.2 = (bf16[16,192,128]{2,1,0:T(8,128)(2,1)S(1)}, bf16[16,192,128]{2,1,0:T(8,128)(2,1)S(1)}, u32[]{:S(2)}, u32[]{:S(2)}) collective-permute-start(bf16[16,192,128]{2,1,0:T(8,128)(2,1)S(1)} %get-tuple-element.32), channel_id=1, source_target_pairs={{0,1},{1,0},{2,3},{3,2},{4,5},{5,4},{6,7},{7,6},{8,9},{9,8},{10,11... | collective-permute-start | bytes 2359304 | tf_op jit(solution)/shard_map/ppermute | solution.py:29
  60.6 10.7 %collective-permute-start.3 = (bf16[2,128,512]{2,1,0:T(8,128)(2,1)}, bf16[2,128,512]{2,1,0:T(8,128)(2,1)}, u32[]{:S(2)}, u32[]{:S(2)}) collective-permute-start(bf16[2,128,512]{2,1,0:T(8,128)(2,1)} %get-tuple-element.34), channel_id=1, source_target_pairs={{32,0},{64,32},{96,64},{128,96},{160,128},{192,160},{224,192},{256... | collective-permute-start | bytes 786440 | tf_op jit(solution)/shard_map/ppermute | solution.py:20
  63.7 7.6 %copy-start = (bf16[2,512,512]{2,1,0:T(8,128)(2,1)S(1)}, bf16[2,512,512]{2,1,0:T(8,128)(2,1)}, u32[]{:S(2)}) copy-start(bf16[2,512,512]{2,1,0:T(8,128)(2,1)} %up_ref.1) | copy-start | bytes 3145732
  63.7 19.0 %all-to-all-start.2 = ((bf16[16,192,128]{2,1,0:T(8,128)(2,1)}), bf16[16,192,128]{2,1,0:T(8,128)(2,1)S(1)}, u32[]{:S(2)}, u32[]{:S(2)}) async-start(bf16[16,192,128]{2,1,0:T(8,128)(2,1)} %add_convert_fusion), calls=%async_computation.2 | async-start | bytes 1572864 | tf_op jit(solution)/shard_map/all_to_all | solution.py:362
  71.3 1.2 %copy-start.2 = (bf16[2,512,512]{2,1,0:T(8,128)(2,1)S(1)}, bf16[2,512,512]{2,1,0:T(8,128)(2,1)}, u32[]{:S(2)}) copy-start(bf16[2,512,512]{2,1,0:T(8,128)(2,1)} %get-tuple-element.33.dpre_ref) | copy-start | bytes 3145732
  76.5 37.0 %copy-start.4 = (f32[48,512]{1,0:T(8,128)S(1)}, f32[48,512]{1,0:T(8,128)}, u32[]{:S(2)}) copy-start(f32[48,512]{1,0:T(8,128)} %weight_hbm.1) | copy-start | bytes 294916
  76.5 37.0 %copy-start.5 = (f32[48,512]{1,0:T(8,128)S(1)}, f32[48,512]{1,0:T(8,128)}, u32[]{:S(2)}) copy-start(f32[48,512]{1,0:T(8,128)} %param.10) | copy-start | bytes 294916
  76.5 37.0 %copy-start.6 = (f32[48,512]{1,0:T(8,128)S(1)}, f32[48,512]{1,0:T(8,128)}, u32[]{:S(2)}) copy-start(f32[48,512]{1,0:T(8,128)} %param.11) | copy-start | bytes 294916

commit v7 on v6

--- a/solution.py
+++ b/solution.py
@@ -43,22 +43,15 @@
     return pltpu.CompilerParams(vmem_limit_bytes=mebibytes * 1024 * 1024)
 
 
-def first_kernel(place_ref, in_hbm, weight_hbm, last_ref, piece_ref, weight_ref, sems):
+def first_kernel(place_ref, weight_hbm, piece_ref, weight_ref, sem):
     copies, part, lanes = piece_ref.shape
-    span = last_ref.shape[1]
-    y = in_hbm.shape[2] // lanes
     z_lo = weight_ref.shape[0] // part
+    y = weight_hbm.shape[1] // lanes
     place = place_ref[0]
     lane = pl.multiple_of((place % y) * lanes, lanes)
-    fetch_weight = pltpu.make_async_copy(
-        weight_hbm.at[:, pl.ds(lane, lanes)], weight_ref, sems.at[0]
-    )
-    fetch_last = pltpu.make_async_copy(
-        in_hbm.at[:, in_hbm.shape[1] - span :, :], last_ref, sems.at[1]
-    )
-    fetch_weight.start()
-    fetch_last.start()
-    fetch_weight.wait()
+    fetch = pltpu.make_async_copy(weight_hbm.at[:, pl.ds(lane, lanes)], weight_ref, sem)
+    fetch.start()
+    fetch.wait()
     for i in range(z_lo):
 
         @pl.when(place // y == i)
@@ -67,28 +60,20 @@
             for n in range(copies):
                 piece_ref[n] = piece
 
-    fetch_last.wait()
-
-
-def first(inputs, weight, span):
+
+def first(weight):
     rows, width = weight.shape
     z_hi, z_lo, y = lax.axis_size("z_hi"), lax.axis_size("z_lo"), lax.axis_size("y")
     place = lax.axis_index(TM).astype(jnp.int32).reshape(1)
     return pl.pallas_call(
         first_kernel,
-        in_specs=[SCALAR, AWAY, AWAY],
-        out_specs=[NEAR, NEAR],
-        out_shape=[
-            jax.ShapeDtypeStruct((inputs.shape[0], span, width), inputs.dtype),
-            jax.ShapeDtypeStruct((z_hi * z_lo, rows // z_lo, width // y), jnp.bfloat16),
-        ],
-        scratch_shapes=[
-            pltpu.VMEM((rows, width // y), jnp.float32),
-            pltpu.SemaphoreType.DMA((2,)),
-        ],
+        in_specs=[SCALAR, AWAY],
+        out_specs=NEAR,
+        out_shape=jax.ShapeDtypeStruct((z_hi * z_lo, rows // z_lo, width // y), jnp.bfloat16),
+        scratch_shapes=[pltpu.VMEM((rows, width // y), jnp.float32), pltpu.SemaphoreType.DMA],
         compiler_params=limit(4),
         name="first",
-    )(place, away(inputs), away(weight))
+    )(place, away(weight))
 
 
 def spread_kernel(line_ref, out_ref, plane_ref):
@@ -381,9 +366,8 @@
 def body(inputs, cotangent, taps, weight, moment_one, second_moment_state):
     span = 2 * DILATION_GAP
     core = lax.axis_index("core").astype(jnp.int32).reshape(1)
-    last, piece = first(inputs, weight, span)
-    line = lax.all_to_all(piece, LINE, 0, 0)
-    early = passed_along(last, 1)
+    line = lax.all_to_all(first(weight), LINE, 0, 0)
+    early = passed_along(inputs[:, inputs.shape[1] - span :, :], 1)
     copies, core = lax.optimization_barrier((spread(line, lax.axis_size(PLANE)), core))
     mine = lax.all_to_all(copies, PLANE, 0, 0)
     mid = middle(taps, inputs, early)

time: 116 us -> 116 us (level)
  transfers between devices with their start and end apart: 7 -> 7, of which waited for: 6 -> 6; matrix products, arithmetic and copies ran while one was open for 1% -> 2% of each run, Pallas kernels for 9% -> 9%
where the time goes in v7:
time: 116 us; the launch traced here: 114 us
  starting transfers between devices  38.3 us (33%)
  blocking collectives  30.5 us (26%)
  waiting for transfers between devices  23.9 us (21%)
  Pallas kernels  16.4 us (14%)
  local copies, waits for them, and re-layouts  2.3 us (2%)
  other arithmetic  1.86 us (2%)
    all_to_all x1, blocking collectives, body(): piece = jnp.sum(lax.all_to_all(line, LINE, 0, 0), 0)  18.2 us
    all_to_all x1, starting transfers between devices, body(): line = lax.all_to_all(first(weight), LINE, 0, 0)  15.2 us
    all_to_all x1, blocking collectives, gathered(): lax.all_to_all(jnp.broadcast_to(piece[None], (size,) + piece.shape), axes...  12.3 us
    all_to_all x1, waiting for transfers between devices, body(): line = lax.all_to_all(first(weight), LINE, 0, 0)  8.24 us
    all_to_all x1, waiting for transfers between devices, body(): mine = lax.all_to_all(copies, PLANE, 0, 0)  7.56 us
    all_to_all x1, starting transfers between devices, body(): mine = lax.all_to_all(copies, PLANE, 0, 0)  7.56 us
    all_to_all x1, starting transfers between devices, plane_sum(): return fold(lax.all_to_all(chunks, PLANE, 0, 0), lax.axis_size(LINE))  6.65 us
    all_to_all x1, waiting for transfers between devices, plane_sum(): return fold(lax.all_to_all(chunks, PLANE, 0, 0), lax.axis_size(LINE))  6.22 us
  transfers between devices with their start and end apart: 7, of which 6 were waited for; matrix products, arithmetic and copies ran while one was open for 2% of the time, Pallas kernels for 9%

profile of v7, /device:TPU:6, one launch (start us, length us, event | category | flops | bytes accessed | tf_op | source)
XLA Modules:
  0.0 114.1 jit_solution(15712187505346641478)
XLA Ops:
  0.6 1.4 %first.1 = bf16[16,12,128]{2,1,0:T(8,128)(2,1)} custom-call(s32[1]{0:T(128)} %bitcast.place_ref, f32[48,512]{1,0:T(8,128)} %weight_hbm.1), custom_call_target="tpu_custom_call" | custom-call | tf_op jit(solution)/shard_map/first/pallas_call | solution.py:68
  2.0 15.2 %all-to-all-start = ((bf16[16,12,128]{2,1,0:T(8,128)(2,1)}), bf16[16,12,128]{2,1,0:T(8,128)(2,1)S(1)}, u32[]{:S(2)}, u32[]{:S(2)}) async-start(bf16[16,12,128]{2,1,0:T(8,128)(2,1)} %first.1), calls=%async_computation | async-start | bytes 131072 | tf_op jit(solution)/shard_map/all_to_all | solution.py:369
  17.3 1.0 slice.3
  18.2 3.5 %collective-permute-start = (bf16[2,128,512]{2,1,0:T(8,128)(2,1)S(1)}, bf16[2,128,512]{2,1,0:T(8,128)(2,1)S(1)}, u32[]{:S(2)}, u32[]{:S(2)}) collective-permute-start(bf16[2,128,512]{2,1,0:T(8,128)(2,1)S(1)} %slice.3), channel_id=1, source_target_pairs={{0,32},{32,64},{64,96},{96,128},{128,160},{160,192},{192,224},{224... | collective-permute-start | bytes 786440 | tf_op jit(solution)/shard_map/ppermute | solution.py:20
  21.7 8.2 %all-to-all-done.line_ref = bf16[16,12,128]{2,1,0:T(8,128)(2,1)S(1)} async-done(((bf16[16,12,128]{2,1,0:T(8,128)(2,1)}), bf16[16,12,128]{2,1,0:T(8,128)(2,1)S(1)}, u32[]{:S(2)}, u32[]{:S(2)}) %all-to-all-start) | async-done | bytes 49184 | tf_op jit(solution)/shard_map/all_to_all | solution.py:369
  30.0 1.0 spread.1
  31.0 0.0 copy-start.3
  31.0 7.6 %all-to-all-start.1 = ((bf16[16,192,128]{2,1,0:T(8,128)(2,1)}), bf16[16,192,128]{2,1,0:T(8,128)(2,1)S(1)}, u32[]{:S(2)}, u32[]{:S(2)}) async-start(bf16[16,192,128]{2,1,0:T(8,128)(2,1)} %spread.1), calls=%async_computation.1 | async-start | bytes 1572864 | tf_op jit(solution)/shard_map/all_to_all | solution.py:372
  38.6 0.0 collective-permute-done.early_ref.early_hbm
  38.6 0.0 copy-done.3
  38.6 0.0 copy-start.1
  38.6 3.2 %middle.1.mid_hbm = bf16[2,512,512]{2,1,0:T(8,128)(2,1)} custom-call(s32[3]{0:T(128)S(1)} %copy-done.3, bf16[2,512,512]{2,1,0:T(8,128)(2,1)} %in_hbm.3, bf16[2,128,512]{2,1,0:T(8,128)(2,1)S(1)} %collective-permute-done.early_ref.early_hbm), custom_call_target="tpu_custom_call" | custom-call | flops 68719476736 | bytes 1073741824 | tf_op jit(solution)/shard_map/middle/pallas_call | solution.py:130
  41.8 0.0 copy-done.1
  41.8 7.6 %all-to-all-done.1.mine_ref = bf16[16,192,128]{2,1,0:T(8,128)(2,1)S(1)} async-done(((bf16[16,192,128]{2,1,0:T(8,128)(2,1)}), bf16[16,192,128]{2,1,0:T(8,128)(2,1)S(1)}, u32[]{:S(2)}, u32[]{:S(2)}) %all-to-all-start.1) | async-done | bytes 786464 | tf_op jit(solution)/shard_map/all_to_all | solution.py:372
  49.4 1.9 %collective-permute-start.1 = (bf16[16,192,128]{2,1,0:T(8,128)(2,1)S(1)}, bf16[16,192,128]{2,1,0:T(8,128)(2,1)S(1)}, u32[]{:S(2)}, u32[]{:S(2)}) collective-permute-start(bf16[16,192,128]{2,1,0:T(8,128)(2,1)S(1)} %all-to-all-done.1.mine_ref), channel_id=1, source_target_pairs={{0,1},{1,0},{2,3},{3,2},{4,5},{5,4},{6,7},{7,6},{8,9},{9,8},{10,11... | collective-permute-start | bytes 2359304 | tf_op jit(solution)/shard_map/ppermute | solution.py:29
  51.3 2.0 %ready.1 = (bf16[2,640,512]{2,1,0:T(8,128)(2,1)S(1)}, bf16[2,512,512]{2,1,0:T(8,128)(2,1)S(1)}, bf16[2,512,512]{2,1,0:T(8,128)(2,1)S(1)}) custom-call(bf16[2,512,512]{2,1,0:T(8,128)(2,1)} %in_hbm.3, bf16[2,128,512]{2,1,0:T(8,128)(2,1)} %copy-done.1, bf16[2,512,512]{2,1,0:T(8,128)(2,1)} %middle.1.mid_hbm, bf16[2,512,512]{2,1,0:T(8,128)(2,1)} %up_ref.1), custom_call_target="tpu_custom_call" | custom-call | tf_op jit(solution)/shard_map/ready/pallas_call | solution.py:163
  53.3 0.3 collective-permute-done.1.other_ref
  53.5 4.7 %layer.1 = (bf16[2,512,512]{2,1,0:T(8,128)(2,1)}, bf16[2,128,512]{2,1,0:T(8,128)(2,1)}, bf16[1536,512]{1,0:T(8,128)(2,1)S(1)}, f32[16,192,128]{2,1,0:T(8,128)S(1)}, bf16[16,192,128]{2,1,0:T(8,128)(2,1)S(1)}) custom-call(s32[1]{0:T(128)} %bitcast.1.core_ref, bf16[16,192,128]{2,1,0:T(8,128)(2,1)S(1)} %all-to-all-done.1.mine_ref, ...), custom_call_target="tpu_custom_call" | custom-call | tf_op jit(solution)/shard_map/layer/pallas_call | solution.py:259
  58.2 2.2 %collective-permute-start.2 = (bf16[16,192,128]{2,1,0:T(8,128)(2,1)S(1)}, bf16[16,192,128]{2,1,0:T(8,128)(2,1)S(1)}, u32[]{:S(2)}, u32[]{:S(2)}) collective-permute-start(bf16[16,192,128]{2,1,0:T(8,128)(2,1)S(1)} %get-tuple-element.28), channel_id=1, source_target_pairs={{0,1},{1,0},{2,3},{3,2},{4,5},{5,4},{6,7},{7,6},{8,9},{9,8},{10,11... | collective-permute-start | bytes 2359304 | tf_op jit(solution)/shard_map/ppermute | solution.py:29
  60.4 1.3 %collective-permute-start.3 = (bf16[2,128,512]{2,1,0:T(8,128)(2,1)}, bf16[2,128,512]{2,1,0:T(8,128)(2,1)}, u32[]{:S(2)}, u32[]{:S(2)}) collective-permute-start(bf16[2,128,512]{2,1,0:T(8,128)(2,1)} %get-tuple-element.30), channel_id=1, source_target_pairs={{32,0},{64,32},{96,64},{128,96},{160,128},{192,160},{224,192},{256... | collective-permute-start | bytes 786440 | tf_op jit(solution)/shard_map/ppermute | solution.py:20
  61.7 0.7 collective-permute-done.2
  62.4 1.1 add_convert_fusion
  63.5 0.0 copy-start
  63.5 6.7 %all-to-all-start.2 = ((bf16[16,192,128]{2,1,0:T(8,128)(2,1)}), bf16[16,192,128]{2,1,0:T(8,128)(2,1)S(1)}, u32[]{:S(2)}, u32[]{:S(2)}) async-start(bf16[16,192,128]{2,1,0:T(8,128)(2,1)} %add_convert_fusion), calls=%async_computation.2 | async-start | bytes 1572864 | tf_op jit(solution)/shard_map/all_to_all | solution.py:347
  70.2 0.9 collective-permute-done.3.ahead_ref
  71.1 0.0 copy-done
  71.1 0.0 copy-start.2
  71.1 1.2 %copy-done.2 = bf16[2,512,512]{2,1,0:T(8,128)(2,1)S(1)} copy-done((bf16[2,512,512]{2,1,0:T(8,128)(2,1)S(1)}, bf16[2,512,512]{2,1,0:T(8,128)(2,1)}, u32[]{:S(2)}) %copy-start.2) | copy-done | bytes 1048600
  72.3 4.0 %back.1 = bf16[2,512,512]{2,1,0:T(8,128)(2,1)} custom-call(s32[3]{0:T(128)S(1)} %copy-done.3, bf16[2,512,512]{2,1,0:T(8,128)(2,1)S(1)} %copy-done.2, bf16[2,128,512]{2,1,0:T(8,128)(2,1)} %collective-permute-done.3.ahead_ref, bf16[1536,512]{1,0:T(8,128)(2,1)S(1)} %get-tuple-element.31.wide_ref, bf16[2,512,512]{2,1,0:T(8,128)(2,1)S(1)} %copy-done), custom_call_target="tpu_custom_call" | custom-call | flops 68719476736 | bytes 1073741824 | tf_op jit(solution)/shard_map/back/pallas_call | solution.py:307
  76.3 0.0 copy-start.4
  76.3 0.0 copy-start.5
  76.3 0.0 copy-start.6
  76.3 6.2 %all-to-all-done.2.chunks_ref = bf16[16,192,128]{2,1,0:T(8,128)(2,1)S(1)} async-done(((bf16[16,192,128]{2,1,0:T(8,128)(2,1)}), bf16[16,192,128]{2,1,0:T(8,128)(2,1)S(1)}, u32[]{:S(2)}, u32[]{:S(2)}) %all-to-all-start.2) | async-done | bytes 786464 | tf_op jit(solution)/shard_map/all_to_all | solution.py:347
  82.6 0.1 fold.1
  82.7 18.2 %all_to_all.25 = f32[16,12,128]{2,1,0:T(8,128)S(1)} all-to-all(f32[16,12,128]{2,1,0:T(8,128)S(1)} %fold.1), channel_id=1, replica_groups=mesh['z_lo'=4,'y'=4,'z_hi'=4,'x'=4,'core'=2] {'z_hi','z_lo'}, dimensions={0} | all-to-all | bytes 196608 | tf_op jit(solution)/shard_map/all_to_all | solution.py:383
  101.0 12.3 %all_to_all.26 = f32[16,12,128]{2,1,0:T(8,128)S(1)} all-to-all(f32[16,12,128]{2,1,0:T(8,128)S(1)} %broadcast_in_dim.2), channel_id=1, replica_groups=mesh['z_lo'=4,'y'=4,'z_hi'=4,'x'=4,'core'=2] {'z_lo','y'}, dimensions={0} | all-to-all | bytes 196608 | tf_op jit(solution)/shard_map/all_to_all | solution.py:25
  113.3 0.0 copy-done.4
  113.3 0.0 copy-done.5
  113.3 0.0 copy-done.6
  113.3 0.7 multiply_subtract_fusion
  (4 shorter events, 0.1 us)
Async XLA Ops:
  2.0 27.9 %all-to-all-start = ((bf16[16,12,128]{2,1,0:T(8,128)(2,1)}), bf16[16,12,128]{2,1,0:T(8,128)(2,1)S(1)}, u32[]{:S(2)}, u32[]{:S(2)}) async-start(bf16[16,12,128]{2,1,0:T(8,128)(2,1)} %first.1), calls=%async_computation | async-start | bytes 131072 | tf_op jit(solution)/shard_map/all_to_all | solution.py:369
  18.2 20.3 %collective-permute-start = (bf16[2,128,512]{2,1,0:T(8,128)(2,1)S(1)}, bf16[2,128,512]{2,1,0:T(8,128)(2,1)S(1)}, u32[]{:S(2)}, u32[]{:S(2)}) collective-permute-start(bf16[2,128,512]{2,1,0:T(8,128)(2,1)S(1)} %slice.3), channel_id=1, source_target_pairs={{0,32},{32,64},{64,96},{96,128},{128,160},{160,192},{192,224},{224... | collective-permute-start | bytes 786440 | tf_op jit(solution)/shard_map/ppermute | solution.py:20
  31.0 7.6 %copy-start.3 = (s32[3]{0:T(128)S(1)}, s32[3]{0:T(128)}, u32[]{:S(2)}) copy-start(s32[3]{0:T(128)} %taps_ref.3) | copy-start | bytes 40
  31.0 18.4 %all-to-all-start.1 = ((bf16[16,192,128]{2,1,0:T(8,128)(2,1)}), bf16[16,192,128]{2,1,0:T(8,128)(2,1)S(1)}, u32[]{:S(2)}, u32[]{:S(2)}) async-start(bf16[16,192,128]{2,1,0:T(8,128)(2,1)} %spread.1), calls=%async_computation.1 | async-start | bytes 1572864 | tf_op jit(solution)/shard_map/all_to_all | solution.py:372
  38.6 3.2 %copy-start.1 = (bf16[2,128,512]{2,1,0:T(8,128)(2,1)}, bf16[2,128,512]{2,1,0:T(8,128)(2,1)S(1)}, u32[]{:S(2)}) copy-start(bf16[2,128,512]{2,1,0:T(8,128)(2,1)S(1)} %collective-permute-done.early_ref.early_hbm) | copy-start | bytes 786436
  49.4 4.2 %collective-permute-start.1 = (bf16[16,192,128]{2,1,0:T(8,128)(2,1)S(1)}, bf16[16,192,128]{2,1,0:T(8,128)(2,1)S(1)}, u32[]{:S(2)}, u32[]{:S(2)}) collective-permute-start(bf16[16,192,128]{2,1,0:T(8,128)(2,1)S(1)} %all-to-all-done.1.mine_ref), channel_id=1, source_target_pairs={{0,1},{1,0},{2,3},{3,2},{4,5},{5,4},{6,7},{7,6},{8,9},{9,8},{10,11... | collective-permute-start | bytes 2359304 | tf_op jit(solution)/shard_map/ppermute | solution.py:29
  58.2 4.2 %collective-permute-start.2 = (bf16[16,192,128]{2,1,0:T(8,128)(2,1)S(1)}, bf16[16,192,128]{2,1,0:T(8,128)(2,1)S(1)}, u32[]{:S(2)}, u32[]{:S(2)}) collective-permute-start(bf16[16,192,128]{2,1,0:T(8,128)(2,1)S(1)} %get-tuple-element.28), channel_id=1, source_target_pairs={{0,1},{1,0},{2,3},{3,2},{4,5},{5,4},{6,7},{7,6},{8,9},{9,8},{10,11... | collective-permute-start | bytes 2359304 | tf_op jit(solution)/shard_map/ppermute | solution.py:29
  60.4 10.7 %collective-permute-start.3 = (bf16[2,128,512]{2,1,0:T(8,128)(2,1)}, bf16[2,128,512]{2,1,0:T(8,128)(2,1)}, u32[]{:S(2)}, u32[]{:S(2)}) collective-permute-start(bf16[2,128,512]{2,1,0:T(8,128)(2,1)} %get-tuple-element.30), channel_id=1, source_target_pairs={{32,0},{64,32},{96,64},{128,96},{160,128},{192,160},{224,192},{256... | collective-permute-start | bytes 786440 | tf_op jit(solution)/shard_map/ppermute | solution.py:20
  63.5 7.6 %copy-start = (bf16[2,512,512]{2,1,0:T(8,128)(2,1)S(1)}, bf16[2,512,512]{2,1,0:T(8,128)(2,1)}, u32[]{:S(2)}) copy-start(bf16[2,512,512]{2,1,0:T(8,128)(2,1)} %up_ref.1) | copy-start | bytes 3145732
  63.5 19.0 %all-to-all-start.2 = ((bf16[16,192,128]{2,1,0:T(8,128)(2,1)}), bf16[16,192,128]{2,1,0:T(8,128)(2,1)S(1)}, u32[]{:S(2)}, u32[]{:S(2)}) async-start(bf16[16,192,128]{2,1,0:T(8,128)(2,1)} %add_convert_fusion), calls=%async_computation.2 | async-start | bytes 1572864 | tf_op jit(solution)/shard_map/all_to_all | solution.py:347
  71.1 1.2 %copy-start.2 = (bf16[2,512,512]{2,1,0:T(8,128)(2,1)S(1)}, bf16[2,512,512]{2,1,0:T(8,128)(2,1)}, u32[]{:S(2)}) copy-start(bf16[2,512,512]{2,1,0:T(8,128)(2,1)} %get-tuple-element.29.dpre_ref) | copy-start | bytes 3145732
  76.3 37.0 %copy-start.4 = (f32[48,512]{1,0:T(8,128)S(1)}, f32[48,512]{1,0:T(8,128)}, u32[]{:S(2)}) copy-start(f32[48,512]{1,0:T(8,128)} %weight_hbm.1) | copy-start | bytes 294916
  76.3 37.0 %copy-start.5 = (f32[48,512]{1,0:T(8,128)S(1)}, f32[48,512]{1,0:T(8,128)}, u32[]{:S(2)}) copy-start(f32[48,512]{1,0:T(8,128)} %param.10) | copy-start | bytes 294916
  76.3 37.0 %copy-start.6 = (f32[48,512]{1,0:T(8,128)S(1)}, f32[48,512]{1,0:T(8,128)}, u32[]{:S(2)}) copy-start(f32[48,512]{1,0:T(8,128)} %param.11) | copy-start | bytes 294916
